TPU v7x, 32 devices: a whole 2x2x4 slice. The times are simulated.
32 devices in a mesh: tile: 16 (over z, y, x), mode: 2 (over core).
Axes of the slice: x: 2, y: 2, z: 4, core: 2. Of those that a mesh axis runs over, the one named last changes fastest.
Arguments:
- obj: float32 [16, 2, 384, 384], P('tile'), may hold values from -6 to 6
- probe: float32 [4, 2, 256, 256], P('mode'), may hold values from -3 to 3
- mode_weights: float32 [8, 4], P(None, 'mode'), may hold values from 0.25 to 1
- measured: float32 [64, 256, 256], P('tile'), may hold values from 0 to 4
- corner: int32 [64, 2], P('tile'), may hold values from 0 to 383, as said below
- counts: int32 [16], P('tile'), may hold values from 1 to 4, 32 in all
- weight_index: int32 [64], P('tile'), may hold values from 0 to 7
Outputs:
- obj_new: float32 [16, 2, 384, 384], P('tile')
- probe_new: float32 [4, 2, 256, 256], P('mode')
Inputs may be any that keep to these rules, and one draw needn't show every extreme that they name: Tile t has live slots 0 to counts[t] - 1 of its block; the counts sum to 32 and some tile has 4. The first slot of every tile has both corner coordinates between 192 and 320.
All inputs are finite; a program needn't handle non-finite values.
Results may differ from a plain program's by a relative error of at most 0.019.
The roundings to bfloat16 on the way count: a program that leaves them out, or rounds other values in their place, can miss the bound.
Values may be sent and summed in bfloat16 or wider, within the bound.
No kernel may reach another device: no remote copies, remote signals or barrier semaphores. Data moves between devices by JAX's collectives and lax.ppermute only.
A program may use at most 64 MiB of HBM per device.

v0:
```python
import functools
import math

import jax
import jax.numpy as jnp
from jax import lax
from jax.experimental import pallas as pl
from jax.experimental.pallas import tpu as pltpu
from jax.sharding import PartitionSpec as P


GC = 8
POS_DEV = 2
ITERS = 2
STRIP = 32

step_object = 0.1
step_probe = 4.0

f32 = jnp.float32
bf16 = jnp.bfloat16
VM = pl.BlockSpec(memory_space=pltpu.VMEM)
SM = pl.BlockSpec(memory_space=pltpu.SMEM)


def shifted(array, by):
    peers = lax.axis_size("tile")
    return lax.ppermute(array, "tile", [(i, (i + by) % peers) for i in range(peers)])


def flipped(array, mask):
    peers = lax.axis_size("tile")
    return lax.ppermute(array, "tile", [(i, i ^ mask) for i in range(peers)])


def swapped(array):
    return lax.ppermute(array, "mode", [(0, 1), (1, 0)])


def dft_tables(length):
    index = jnp.arange(length, dtype=jnp.int32)
    product = index[:, None] * index[None, :] % length
    angle = product.astype(f32) * (2.0 * math.pi / length)
    factor = 1.0 / math.sqrt(length)
    real = jnp.cos(angle) * factor
    imag = -(jnp.sin(angle) * factor)
    one = jnp.concatenate(
        [jnp.concatenate([real, -imag], 1), jnp.concatenate([imag, real], 1)], 0
    ).astype(bf16)
    two = jnp.concatenate(
        [jnp.concatenate([real, imag], 1), jnp.concatenate([-imag, real], 1)], 0
    ).astype(bf16)
    return one, two


def dot(a, b):
    return jnp.dot(a, b, preferred_element_type=f32)


LANES = 128


def blocks(t, n, refs):
    right, low, diag = refs
    return ((right, 0, t, t, n), (low, t, 0, n, t), (diag, t, t, n, n))


def packed_rows(t, n):
    return (t * n // LANES, n * t // LANES, n * n // LANES)


def patch_kernel(
    live, corner, kind, wm, wo,
    tm, rm, bm, dm, to, ro, bo, do, meas, pm, po, one, two,
    own_keep, own_send, edge_keep, edge_send, pgm, pgo,
    frame, grad, psi, xs, ts, orr, oii, term, acc,
):
    n = pm.shape[-1]
    t = tm.shape[-1]
    half = pm.shape[0]
    modes = 2 * half
    me = lax.axis_index("mode")
    for plane, (a, b, c, d) in ((me, (tm, rm, bm, dm)), (1 - me, (to, ro, bo, do))):
        frame[plane, pl.ds(0, t), pl.ds(0, t)] = a[...].astype(f32)
        for ref, top, left, high, wide in blocks(t, n, (b, c, d)):
            for k in range(wide // LANES):
                part = ref[pl.ds(k * high, high), :].astype(f32)
                frame[plane, pl.ds(top, high), pl.ds(left + k * LANES, LANES)] = part
    grad[...] = jnp.zeros_like(grad)
    acc[...] = jnp.zeros_like(acc)

    def probe_at(m, c, rows):
        ref = pm if m < half else po
        return ref[m % half, c, rows, :]

    def slot_body(g, carry):
        s = me + 2 * g

        @pl.when(s < live[0])
        def _():
            row = corner[0, s]
            col = corner[1, s]
            rb = pl.multiple_of(row // 8 * 8, 8)
            rr = row - rb
            cb = pl.multiple_of(col // 128 * 128, 128)
            cc = col - cb
            high, wide = n + 8, n + 128
            for p, out in ((0, orr), (1, oii)):
                win = frame[p, pl.ds(rb, high), pl.ds(cb, wide)]
                win = pltpu.roll(win, lax.rem(wide - cc, wide), 1)[:, :n]
                win = pltpu.roll(win, lax.rem(high - rr, high), 0)[:n]
                out[...] = win
            strips = [pl.ds(i * STRIP, STRIP) for i in range(n // STRIP)]
            lower = [pl.ds(n + i * STRIP, STRIP) for i in range(n // STRIP)]
            w = [wm[m, kind[s]] if m < half else wo[m - half, kind[s]] for m in range(modes)]
            for m in range(modes):
                for up, lo in zip(strips, lower):
                    a, b = orr[up, :], oii[up, :]
                    pr, pi = probe_at(m, 0, up), probe_at(m, 1, up)
                    xs[m, up, :] = (pr * a - pi * b).astype(bf16)
                    xs[m, lo, :] = (pr * b + pi * a).astype(bf16)
            for m in range(modes):
                y = dot(one[...], xs[m])
                ts[pl.ds(m * n, n), pl.ds(0, n)] = y[:n].astype(bf16)
                ts[pl.ds(m * n, n), pl.ds(n, n)] = y[n:].astype(bf16)
            psi[...] = dot(ts[...], two[...])
            for i, (up, lo) in enumerate(zip(strips, lower)):
                total = jnp.zeros((STRIP, n), f32)
                for m in range(modes):
                    rows = pl.ds(m * n + i * STRIP, STRIP)
                    a, b = psi[rows, pl.ds(0, n)], psi[rows, pl.ds(n, n)]
                    total = total + w[m] * (a * a + b * b)
                resid = total - meas[s, up, :]
                for m in range(modes):
                    rows = pl.ds(m * n + i * STRIP, STRIP)
                    scale = w[m] * resid
                    xs[m, up, :] = (scale * psi[rows, pl.ds(0, n)]).astype(bf16)
                    xs[m, lo, :] = (scale * psi[rows, pl.ds(n, n)]).astype(bf16)
            for m in range(modes):
                y = dot(two[...], xs[m])
                ts[pl.ds(m * n, n), pl.ds(0, n)] = y[:n].astype(bf16)
                ts[pl.ds(m * n, n), pl.ds(n, n)] = y[n:].astype(bf16)
            psi[...] = dot(ts[...], one[...])
            for i, up in enumerate(strips):
                a, b = orr[up, :], oii[up, :]
                tr = jnp.zeros((STRIP, n), f32)
                ti = jnp.zeros((STRIP, n), f32)
                for m in range(modes):
                    rows = pl.ds(m * n + i * STRIP, STRIP)
                    cr, ci = psi[rows, pl.ds(0, n)], psi[rows, pl.ds(n, n)]
                    pr, pi = probe_at(m, 0, up), probe_at(m, 1, up)
                    tr = tr + (pr * cr + pi * ci)
                    ti = ti + (pr * ci - pi * cr)
                    acc[m, 0, up, :] += a * cr + b * ci
                    acc[m, 1, up, :] += a * ci - b * cr
                term[0, up, pl.ds(0, n)] = tr
                term[1, up, pl.ds(0, n)] = ti
            for p in range(2):
                term[p, pl.ds(n, 8), :] = jnp.zeros((8, wide), f32)
                term[p, pl.ds(0, n), pl.ds(n, 128)] = jnp.zeros((n, 128), f32)
                moved = pltpu.roll(pltpu.roll(term[p], rr, 0), cc, 1)
                grad[p, pl.ds(rb, high), pl.ds(cb, wide)] += moved

        return carry

    lax.fori_loop(0, meas.shape[0] // 2, slot_body, 0)
    own_keep[...] = grad[me, pl.ds(0, t), pl.ds(0, t)]
    own_send[...] = grad[1 - me, pl.ds(0, t), pl.ds(0, t)].astype(bf16)
    base = 0
    for _, top, left, high, wide in blocks(t, n, (None,) * 3):
        for k in range(wide // LANES):
            rows, lanes = pl.ds(top, high), pl.ds(left + k * LANES, LANES)
            edge_keep[pl.ds(base, high), :] = grad[me, rows, lanes]
            edge_send[pl.ds(base, high), :] = grad[1 - me, rows, lanes].astype(bf16)
            base += high
    for m in range(half):
        pgm[m] = acc[m]
        pgo[m] = acc[half + m].astype(bf16)


def call(kernel, outs, *args, smem=0, scratch=(), limit=4 * 1024 * 1024):
    return pl.pallas_call(
        kernel,
        out_shape=tuple(jax.ShapeDtypeStruct(shape, dtype) for shape, dtype in outs),
        in_specs=[SM] * smem + [VM] * (len(args) - smem),
        out_specs=(VM,) * len(outs),
        scratch_shapes=list(scratch),
        compiler_params=pltpu.CompilerParams(vmem_limit_bytes=limit),
        name="kernel",
    )(*args)


def patches(live, corner, kind, wm, wo, mine, other, meas, pm, po, one, two):
    n = pm.shape[-1]
    t = mine[0].shape[-1]
    f = n + t
    modes = 2 * pm.shape[0]
    rows = sum(packed_rows(t, n))
    return call(
        patch_kernel,
        (
            ((t, t), f32),
            ((t, t), bf16),
            ((rows, LANES), f32),
            ((rows, LANES), bf16),
            (pm.shape, f32),
            (pm.shape, bf16),
        ),
        live, corner, kind, wm, wo, *mine, *other, meas, pm, po, one, two,
        smem=5,
        scratch=[
            pltpu.VMEM((2, f, f), f32),
            pltpu.VMEM((2, f, f), f32),
            pltpu.VMEM((modes * n, 2 * n), f32),
            pltpu.VMEM((modes, 2 * n, n), bf16),
            pltpu.VMEM((modes * n, 2 * n), bf16),
            pltpu.VMEM((n, n), f32),
            pltpu.VMEM((n, n), f32),
            pltpu.VMEM((2, n + 8, n + 128), f32),
            pltpu.VMEM((modes, 2, n, n), f32),
        ],
        limit=24 * 1024 * 1024,
    )


def pack_edges(value, t, n, outs):
    for out, _, _, high, wide in blocks(t, n, outs):
        for k in range(wide // LANES):
            out[pl.ds(k * high, high), :] = value[:high, k * LANES : (k + 1) * LANES]


def enter_kernel(obj, state, half, rest, hr, hl, hd):
    me = lax.axis_index("mode")
    t = obj.shape[-1]
    n = hl.shape[0] * LANES // t
    value = obj[me]
    state[...] = value
    small = value.astype(bf16)
    half[...] = small
    pack_edges(small, t, n, (hr, hl, hd))
    rest[...] = obj[1 - me].astype(bf16)


def edge_shapes(t, n):
    return tuple(((rows, LANES), bf16) for rows in packed_rows(t, n))


def enter(obj, n):
    t = obj.shape[-1]
    outs = (((t, t), f32), ((t, t), bf16), ((t, t), bf16)) + edge_shapes(t, n)
    return call(enter_kernel, outs, obj)


def margin_kernel(keep, got, right, low, diag):
    base = 0
    for out in (right, low, diag):
        rows = pl.ds(base, out.shape[0])
        out[...] = (keep[rows, :] + got[rows, :].astype(f32)).astype(bf16)
        base += out.shape[0]


def margins(keep, got, t, n):
    return call(margin_kernel, edge_shapes(t, n), keep, got)


def update_kernel(state, keep, got, right, low, diag, new, half, hr, hl, hd):
    t = state.shape[0]
    n = low.shape[0] * LANES // t
    new[...] = keep[...] + got[...].astype(f32)
    for ref, _, _, high, wide in blocks(t, n, (right, low, diag)):
        for k in range(wide // LANES):
            lanes = pl.ds(k * LANES, LANES)
            new[pl.ds(0, high), lanes] += ref[pl.ds(k * high, high), :].astype(f32)
    value = state[...] - step_object * new[...]
    new[...] = value
    small = value.astype(bf16)
    half[...] = small
    pack_edges(small, t, n, (hr, hl, hd))


def update(state, keep, got, right, low, diag):
    t = state.shape[0]
    n = low.shape[0] * LANES // t
    outs = (((t, t), f32), ((t, t), bf16)) + edge_shapes(t, n)
    return call(update_kernel, outs, state, keep, got, right, low, diag)


def leave_kernel(state, rest, out):
    me = lax.axis_index("mode")
    out[me] = state[...]
    out[1 - me] = rest[...]


def leave(state, rest):
    outs = (((2, *state.shape), f32),)
    return call(leave_kernel, outs, state, rest)[0]


def digits(peers):
    out, shift = [], 0
    while 1 << shift < peers:
        radix = 4 if (4 << shift) <= peers else 2
        out.append((shift, radix))
        shift += radix.bit_length() - 1
    return out


def spot_of(shift, radix):
    return (lax.axis_index("tile") >> shift) & (radix - 1)


def first_kernel(place, keep, got, own, *sends):
    i = spot_of(*place)
    own[...] = keep[i] + got[i].astype(f32)
    for k, out in enumerate(sends):
        j = i ^ (k + 1)
        out[...] = (keep[j] + got[j].astype(f32)).astype(bf16)


def stage_kernel(before, place, have, *refs):
    after = place[1]
    got = refs[: before - 1]
    own, sends = refs[before - 1], refs[before:]
    total = refs[-1]
    sends = sends[:-1]
    value = have[...]
    for ref in got:
        value = value + ref[...].astype(f32)
    if after == 1:
        own[...] = value.astype(bf16)
        return
    total[...] = value
    rows = own.shape[0]
    i = spot_of(*place)
    own[...] = total[pl.ds(pl.multiple_of(i * rows, rows), rows), :]
    for k, out in enumerate(sends):
        j = i ^ (k + 1)
        out[...] = total[pl.ds(pl.multiple_of(j * rows, rows), rows), :].astype(bf16)


def join_kernel(place, have, *refs):
    got, out = refs[:-1], refs[-1]
    rows = have.shape[0]
    i = spot_of(*place)
    out[pl.ds(pl.multiple_of(i * rows, rows), rows), :] = have[...]
    for k, ref in enumerate(got):
        j = i ^ (k + 1)
        out[pl.ds(pl.multiple_of(j * rows, rows), rows), :] = ref[...]


def apply_kernel(rate, place, probe, have, *refs):
    got, out = refs[:-1], refs[-1]
    i = spot_of(*place)
    for k, ref in enumerate((have, *got)):
        j = i ^ k
        out[j] = probe[j] - rate * ref[...].astype(f32)


def probe_sum(keep, got):
    n = keep.shape[-1]
    stages = digits(lax.axis_size("tile"))
    shift, radix = stages[0]
    keep = keep.reshape(radix, -1, n)
    got = got.reshape(keep.shape)
    rows = keep.shape[1]
    own, *sends = call(
        functools.partial(first_kernel, (shift, radix)),
        (((rows, n), f32),) + (((rows, n), bf16),) * (radix - 1),
        keep, got,
    )
    for at, (shift, radix) in enumerate(stages):
        got = [flipped(part, (k + 1) << shift) for k, part in enumerate(sends)]
        if at + 1 < len(stages):
            place = stages[at + 1]
            small = rows // place[1]
            outs = (((small, n), f32),) + (((small, n), bf16),) * (place[1] - 1)
        else:
            place, small = (0, 1), rows
            outs = (((rows, n), bf16),)
        own, *sends = call(
            functools.partial(stage_kernel, radix, place),
            outs, own, *got,
            scratch=[pltpu.VMEM((rows, n), f32)],
        )
        rows = small
    for at, (shift, radix) in reversed(list(enumerate(stages))):
        got = [flipped(own, k << shift) for k in range(1, radix)]
        if at:
            outs = (((rows * radix, n), bf16),)
            join = functools.partial(join_kernel, (shift, radix))
            (own,) = call(join, outs, own, *got)
            rows = rows * radix
    return (own, *got)


def probe_step(rate, probe, pieces):
    place = digits(lax.axis_size("tile"))[0]
    chunks = probe.reshape(place[1], -1, probe.shape[-1])
    (out,) = call(
        functools.partial(apply_kernel, rate, place),
        ((chunks.shape, f32),), chunks, *pieces,
    )
    return out.reshape(probe.shape)


def steps(obj, probe, mode_weights, measured, corner, counts, weight_index):
    n = probe.shape[-1]
    t = obj.shape[-1]
    one, two = dft_tables(n)
    rate = step_probe / (POS_DEV * lax.axis_size("tile"))
    state, half, rest, *edges = enter(obj[0], n)
    pm = probe
    po = swapped(probe)
    wm = mode_weights.T
    wo = swapped(wm)
    spots = corner.T
    for sweep in range(ITERS):
        low = shifted(edges[1], -GC)
        diag = shifted(edges[2], -(GC + 1))
        right = shifted(edges[0], -1)
        mine = (half, right, low, diag)
        other = (rest, swapped(right), swapped(low), swapped(diag))
        own_keep, own_send, edge_keep, edge_send, pgm, pgo = patches(
            counts, spots, weight_index, wm, wo, mine, other, measured, pm, po, one, two
        )
        edge_got = swapped(edge_send)
        right, low, diag = margins(edge_keep, edge_got, t, n)
        low = shifted(low, GC)
        diag = shifted(diag, GC + 1)
        right = shifted(right, 1)
        pieces = probe_sum(pgm, swapped(pgo))
        own_got = swapped(own_send)
        state, half, *edges = update(state, own_keep, own_got, right, low, diag)
        pm = probe_step(rate, pm, pieces)
        if sweep < ITERS - 1:
            rest = swapped(half)
            others = [swapped(piece) for piece in pieces]
            po = probe_step(rate, po, others)
    return (leave(state, swapped(state))[None], pm)


def solution(mesh):
    placed = (
        P("tile", None, None, None),
        P("mode", None, None, None),
        P(None, "mode"),
        P("tile", None, None),
        P("tile", None),
        P("tile"),
        P("tile"),
    )
    return jax.shard_map(
        steps,
        mesh=mesh,
        in_specs=placed,
        out_specs=(P("tile", None, None, None), P("mode", None, None, None)),
        check_vma=False,
    )
```

profile of v0, /device:TPU:0, one launch (start us, length us, event | category | flops | bytes accessed | tf_op | source)
XLA Modules:
  0.0 162.6 jit_solution(16365730236281939993)
XLA Ops:
  1.2 1.3 copy-done.2
  2.6 6.5 %collective-permute-start.1 = (bf16[768,128]{1,0:T(8,128)(2,1)S(1)}, bf16[768,128]{1,0:T(8,128)(2,1)S(1)}, u32[]{:S(2)}, u32[]{:S(2)}) collective-permute-start(bf16[768,128]{1,0:T(8,128)(2,1)S(1)} %get-tuple-element.50), channel_id=1, source_target_pairs={{0,30},{2,0},{4,2},{6,4},{8,6},{10,8},{12,10},{14,12},{16,14},{18,... | collective-permute-start | bytes 589832 | tf_op jit(solution)/shard_map/ppermute | solution.py:28
  10.3 1.1 negate_convert_fusion
  11.4 3.2 %collective-permute-done.1.rm = bf16[768,128]{1,0:T(8,128)(2,1)S(1)} collective-permute-done((bf16[768,128]{1,0:T(8,128)(2,1)S(1)}, bf16[768,128]{1,0:T(8,128)(2,1)S(1)}, u32[]{:S(2)}, u32[]{:S(2)}) %collective-permute-start.1) | collective-permute-done | bytes 196640 | tf_op jit(solution)/shard_map/ppermute | solution.py:28
  14.6 10.6 %collective-permute-done.2.bm = bf16[768,128]{1,0:T(8,128)(2,1)S(1)} collective-permute-done((bf16[768,128]{1,0:T(8,128)(2,1)S(1)}, bf16[768,128]{1,0:T(8,128)(2,1)S(1)}, u32[]{:S(2)}, u32[]{:S(2)}) %collective-permute-start.2) | collective-permute-done | bytes 196640 | tf_op jit(solution)/shard_map/ppermute | solution.py:28
  25.1 1.0 fusion.8
  27.7 9.0 %kernel.20 = (f32[384,384]{1,0:T(8,128)S(1)}, bf16[384,384]{1,0:T(8,128)(2,1)S(1)}, f32[2048,128]{1,0:T(8,128)S(1)}, bf16[2048,128]{1,0:T(8,128)(2,1)S(1)}, f32[...) custom-call(s32[1]{0:T(128)S(6)} %copy.9.live, s32[2,4]{1,0:T(2,128)S(1)} %bitcast.22, s32[4]{0:T(128)S(1)} %copy-done.5, ...), custom_call_target="tpu_custom_call" | custom-call | tf_op jit(solution)/shard_map/kernel/pallas_call | solution.py:182
  37.4 1.4 collective-permute-done.20
  39.4 3.1 %collective-permute-start.23 = (bf16[256,256]{1,0:T(8,128)(2,1)S(1)}, bf16[256,256]{1,0:T(8,128)(2,1)S(1)}, u32[]{:S(2)}, u32[]{:S(2)}) collective-permute-start(bf16[256,256]{1,0:T(8,128)(2,1)S(1)} %get-tuple-element.71), channel_id=1, source_target_pairs={{0,6},{2,4},{4,2},{6,0},{8,14},{10,12},{12,10},{14,8},{16,22},{18,... | collective-permute-start | bytes 393224 | tf_op jit(solution)/shard_map/ppermute | solution.py:33
  43.0 2.3 %collective-permute-done.21.refs_0_ = bf16[256,256]{1,0:T(8,128)(2,1)S(1)} collective-permute-done((bf16[256,256]{1,0:T(8,128)(2,1)S(1)}, bf16[256,256]{1,0:T(8,128)(2,1)S(1)}, u32[]{:S(2)}, u32[]{:S(2)}) %collective-permute-start.21) | collective-permute-done | bytes 131104 | tf_op jit(solution)/shard_map/ppermute | solution.py:33
  45.3 2.4 %collective-permute-done.22.refs_1_ = bf16[256,256]{1,0:T(8,128)(2,1)S(1)} collective-permute-done((bf16[256,256]{1,0:T(8,128)(2,1)S(1)}, bf16[256,256]{1,0:T(8,128)(2,1)S(1)}, u32[]{:S(2)}, u32[]{:S(2)}) %collective-permute-start.22) | collective-permute-done | bytes 131104 | tf_op jit(solution)/shard_map/ppermute | solution.py:33
  47.8 2.6 %collective-permute-start.24 = (bf16[64,256]{1,0:T(8,128)(2,1)S(1)}, bf16[64,256]{1,0:T(8,128)(2,1)S(1)}, u32[]{:S(2)}, u32[]{:S(2)}) collective-permute-start(bf16[64,256]{1,0:T(8,128)(2,1)S(1)} %get-tuple-element.73), channel_id=1, source_target_pairs={{0,8},{2,10},{4,12},{6,14},{8,0},{10,2},{12,4},{14,6},{16,24},{18,... | collective-permute-start | bytes 98312 | tf_op jit(solution)/shard_map/ppermute | solution.py:33
  50.5 1.9 %collective-permute-done.24.refs_0_ = bf16[64,256]{1,0:T(8,128)(2,1)S(1)} collective-permute-done((bf16[64,256]{1,0:T(8,128)(2,1)S(1)}, bf16[64,256]{1,0:T(8,128)(2,1)S(1)}, u32[]{:S(2)}, u32[]{:S(2)}) %collective-permute-start.24) | collective-permute-done | bytes 32800 | tf_op jit(solution)/shard_map/ppermute | solution.py:33
  52.3 3.8 %collective-permute-start.25 = (bf16[64,256]{1,0:T(8,128)(2,1)S(1)}, bf16[64,256]{1,0:T(8,128)(2,1)S(1)}, u32[]{:S(2)}, u32[]{:S(2)}) collective-permute-start(bf16[64,256]{1,0:T(8,128)(2,1)S(1)} %get-tuple-element.74), channel_id=1, source_target_pairs={{0,16},{2,18},{4,20},{6,22},{8,24},{10,26},{12,28},{14,30},{16,0},... | collective-permute-start | bytes 98312 | tf_op jit(solution)/shard_map/ppermute | solution.py:33
  56.1 2.6 %collective-permute-done.25.refs_1_ = bf16[64,256]{1,0:T(8,128)(2,1)S(1)} collective-permute-done((bf16[64,256]{1,0:T(8,128)(2,1)S(1)}, bf16[64,256]{1,0:T(8,128)(2,1)S(1)}, u32[]{:S(2)}, u32[]{:S(2)}) %collective-permute-start.25) | collective-permute-done | bytes 32800 | tf_op jit(solution)/shard_map/ppermute | solution.py:33
  58.7 1.9 %collective-permute-start.26 = (bf16[64,256]{1,0:T(8,128)(2,1)S(1)}, bf16[64,256]{1,0:T(8,128)(2,1)S(1)}, u32[]{:S(2)}, u32[]{:S(2)}) collective-permute-start(bf16[64,256]{1,0:T(8,128)(2,1)S(1)} %get-tuple-element.75), channel_id=1, source_target_pairs={{0,24},{2,26},{4,28},{6,30},{8,16},{10,18},{12,20},{14,22},{16,8},... | collective-permute-start | bytes 98312 | tf_op jit(solution)/shard_map/ppermute | solution.py:33
  60.6 3.8 %collective-permute-done.26.refs_2_ = bf16[64,256]{1,0:T(8,128)(2,1)S(1)} collective-permute-done((bf16[64,256]{1,0:T(8,128)(2,1)S(1)}, bf16[64,256]{1,0:T(8,128)(2,1)S(1)}, u32[]{:S(2)}, u32[]{:S(2)}) %collective-permute-start.26) | collective-permute-done | bytes 32800 | tf_op jit(solution)/shard_map/ppermute | solution.py:33
  64.4 2.0 %collective-permute-start.29 = (bf16[64,256]{1,0:T(8,128)(2,1)S(1)}, bf16[64,256]{1,0:T(8,128)(2,1)S(1)}, u32[]{:S(2)}, u32[]{:S(2)}) collective-permute-start(bf16[64,256]{1,0:T(8,128)(2,1)S(1)} %kernel.25.have), channel_id=1, source_target_pairs={{0,24},{2,26},{4,28},{6,30},{8,16},{10,18},{12,20},{14,22},{16,8},... | collective-permute-start | bytes 98312 | tf_op jit(solution)/shard_map/ppermute | solution.py:33
  66.4 2.5 %collective-permute-start.27 = (bf16[64,256]{1,0:T(8,128)(2,1)S(1)}, bf16[64,256]{1,0:T(8,128)(2,1)S(1)}, u32[]{:S(2)}, u32[]{:S(2)}) collective-permute-start(bf16[64,256]{1,0:T(8,128)(2,1)S(1)} %kernel.25.have), channel_id=1, source_target_pairs={{0,8},{2,10},{4,12},{6,14},{8,0},{10,2},{12,4},{14,6},{16,24},{18,... | collective-permute-start | bytes 98312 | tf_op jit(solution)/shard_map/ppermute | solution.py:33
  69.2 6.8 %collective-permute-start.15 = (bf16[512,128]{1,0:T(8,128)(2,1)S(1)}, bf16[512,128]{1,0:T(8,128)(2,1)S(1)}, u32[]{:S(2)}, u32[]{:S(2)}) collective-permute-start(bf16[512,128]{1,0:T(8,128)(2,1)S(1)} %get-tuple-element.65), channel_id=1, source_target_pairs={{0,14},{2,16},{4,18},{6,20},{8,22},{10,24},{12,26},{14,28},{16,30}... | collective-permute-start | bytes 393224 | tf_op jit(solution)/shard_map/ppermute | solution.py:28
  76.2 3.3 %collective-permute-start.32 = (bf16[256,256]{1,0:T(8,128)(2,1)S(1)}, bf16[256,256]{1,0:T(8,128)(2,1)S(1)}, u32[]{:S(2)}, u32[]{:S(2)}) collective-permute-start(bf16[256,256]{1,0:T(8,128)(2,1)S(1)} %kernel.26.have), channel_id=1, source_target_pairs={{0,6},{2,4},{4,2},{6,0},{8,14},{10,12},{12,10},{14,8},{16,22},{18,... | collective-permute-start | bytes 393224 | tf_op jit(solution)/shard_map/ppermute | solution.py:33
  80.1 5.2 %collective-permute-start.13 = (bf16[768,128]{1,0:T(8,128)(2,1)S(1)}, bf16[768,128]{1,0:T(8,128)(2,1)S(1)}, u32[]{:S(2)}, u32[]{:S(2)}) collective-permute-start(bf16[768,128]{1,0:T(8,128)(2,1)S(1)} %get-tuple-element.63), channel_id=1, source_target_pairs={{0,30},{2,0},{4,2},{6,4},{8,6},{10,8},{12,10},{14,12},{16,14},{18,... | collective-permute-start | bytes 589832 | tf_op jit(solution)/shard_map/ppermute | solution.py:28
  85.4 1.5 collective-permute-done.31.refs_1_
  86.9 3.3 %collective-permute-done.30.refs_0_ = bf16[256,256]{1,0:T(8,128)(2,1)S(1)} collective-permute-done((bf16[256,256]{1,0:T(8,128)(2,1)S(1)}, bf16[256,256]{1,0:T(8,128)(2,1)S(1)}, u32[]{:S(2)}, u32[]{:S(2)}) %collective-permute-start.30) | collective-permute-done | bytes 131104 | tf_op jit(solution)/shard_map/ppermute | solution.py:33
  90.7 5.7 %collective-permute-done.14.bm = bf16[768,128]{1,0:T(8,128)(2,1)S(1)} collective-permute-done((bf16[768,128]{1,0:T(8,128)(2,1)S(1)}, bf16[768,128]{1,0:T(8,128)(2,1)S(1)}, u32[]{:S(2)}, u32[]{:S(2)}) %collective-permute-start.14) | collective-permute-done | bytes 196640 | tf_op jit(solution)/shard_map/ppermute | solution.py:28
  97.1 0.9 collective-permute-done.34.refs_0_
  98.3 9.0 %kernel.29 = (f32[384,384]{1,0:T(8,128)S(1)}, bf16[384,384]{1,0:T(8,128)(2,1)S(1)}, f32[2048,128]{1,0:T(8,128)S(1)}, bf16[2048,128]{1,0:T(8,128)(2,1)S(1)}, f32[...) custom-call(s32[1]{0:T(128)S(6)} %copy.9.live, s32[2,4]{1,0:T(2,128)S(1)} %bitcast.23, s32[4]{0:T(128)S(1)} %copy-done.5, ...), custom_call_target="tpu_custom_call" | custom-call | tf_op jit(solution)/shard_map/kernel/pallas_call | solution.py:182
  108.1 1.2 collective-permute-done.38.got
  109.7 13.2 %collective-permute-done.41.diag = bf16[512,128]{1,0:T(8,128)(2,1)S(1)} collective-permute-done((bf16[512,128]{1,0:T(8,128)(2,1)S(1)}, bf16[512,128]{1,0:T(8,128)(2,1)S(1)}, u32[]{:S(2)}, u32[]{:S(2)}) %collective-permute-start.41) | collective-permute-done | bytes 131104 | tf_op jit(solution)/shard_map/ppermute | solution.py:28
  122.9 1.1 kernel.31
  124.1 3.6 %collective-permute-start.44 = (bf16[256,256]{1,0:T(8,128)(2,1)S(1)}, bf16[256,256]{1,0:T(8,128)(2,1)S(1)}, u32[]{:S(2)}, u32[]{:S(2)}) collective-permute-start(bf16[256,256]{1,0:T(8,128)(2,1)S(1)} %get-tuple-element.87), channel_id=1, source_target_pairs={{0,2},{2,0},{4,6},{6,4},{8,10},{10,8},{12,14},{14,12},{16,18},{18,... | collective-permute-start | bytes 393224 | tf_op jit(solution)/shard_map/ppermute | solution.py:33
  127.7 1.1 collective-permute-start.45
  129.3 2.8 %collective-permute-done.44.refs_0_ = bf16[256,256]{1,0:T(8,128)(2,1)S(1)} collective-permute-done((bf16[256,256]{1,0:T(8,128)(2,1)S(1)}, bf16[256,256]{1,0:T(8,128)(2,1)S(1)}, u32[]{:S(2)}, u32[]{:S(2)}) %collective-permute-start.44) | collective-permute-done | bytes 131104 | tf_op jit(solution)/shard_map/ppermute | solution.py:33
  132.0 4.1 %collective-permute-done.45.refs_1_ = bf16[256,256]{1,0:T(8,128)(2,1)S(1)} collective-permute-done((bf16[256,256]{1,0:T(8,128)(2,1)S(1)}, bf16[256,256]{1,0:T(8,128)(2,1)S(1)}, u32[]{:S(2)}, u32[]{:S(2)}) %collective-permute-start.45) | collective-permute-done | bytes 131104 | tf_op jit(solution)/shard_map/ppermute | solution.py:33
  136.2 3.0 %collective-permute-start.47 = (bf16[64,256]{1,0:T(8,128)(2,1)S(1)}, bf16[64,256]{1,0:T(8,128)(2,1)S(1)}, u32[]{:S(2)}, u32[]{:S(2)}) collective-permute-start(bf16[64,256]{1,0:T(8,128)(2,1)S(1)} %get-tuple-element.91), channel_id=1, source_target_pairs={{0,8},{2,10},{4,12},{6,14},{8,0},{10,2},{12,4},{14,6},{16,24},{18,... | collective-permute-start | bytes 98312 | tf_op jit(solution)/shard_map/ppermute | solution.py:33
  139.5 2.1 %collective-permute-start.49 = (bf16[64,256]{1,0:T(8,128)(2,1)S(1)}, bf16[64,256]{1,0:T(8,128)(2,1)S(1)}, u32[]{:S(2)}, u32[]{:S(2)}) collective-permute-start(bf16[64,256]{1,0:T(8,128)(2,1)S(1)} %get-tuple-element.93), channel_id=1, source_target_pairs={{0,24},{2,26},{4,28},{6,30},{8,16},{10,18},{12,20},{14,22},{16,8},... | collective-permute-start | bytes 98312 | tf_op jit(solution)/shard_map/ppermute | solution.py:33
  141.6 2.4 %collective-permute-done.48.refs_1_ = bf16[64,256]{1,0:T(8,128)(2,1)S(1)} collective-permute-done((bf16[64,256]{1,0:T(8,128)(2,1)S(1)}, bf16[64,256]{1,0:T(8,128)(2,1)S(1)}, u32[]{:S(2)}, u32[]{:S(2)}) %collective-permute-start.48) | collective-permute-done | bytes 32800 | tf_op jit(solution)/shard_map/ppermute | solution.py:33
  144.0 1.2 collective-permute-done.49.refs_2_
  145.2 2.2 %collective-permute-start.52 = (bf16[64,256]{1,0:T(8,128)(2,1)S(1)}, bf16[64,256]{1,0:T(8,128)(2,1)S(1)}, u32[]{:S(2)}, u32[]{:S(2)}) collective-permute-start(bf16[64,256]{1,0:T(8,128)(2,1)S(1)} %kernel.35.have), channel_id=1, source_target_pairs={{0,24},{2,26},{4,28},{6,30},{8,16},{10,18},{12,20},{14,22},{16,8},... | collective-permute-start | bytes 98312 | tf_op jit(solution)/shard_map/ppermute | solution.py:33
  147.4 2.2 %collective-permute-start.50 = (bf16[64,256]{1,0:T(8,128)(2,1)S(1)}, bf16[64,256]{1,0:T(8,128)(2,1)S(1)}, u32[]{:S(2)}, u32[]{:S(2)}) collective-permute-start(bf16[64,256]{1,0:T(8,128)(2,1)S(1)} %kernel.35.have), channel_id=1, source_target_pairs={{0,8},{2,10},{4,12},{6,14},{8,0},{10,2},{12,4},{14,6},{16,24},{18,... | collective-permute-start | bytes 98312 | tf_op jit(solution)/shard_map/ppermute | solution.py:33
  149.7 1.3 collective-permute-done.52.refs_2_
  151.0 1.2 collective-permute-done.51.refs_1_
  152.3 1.5 collective-permute-start.55
  153.8 1.7 %collective-permute-start.54 = (bf16[256,256]{1,0:T(8,128)(2,1)S(1)}, bf16[256,256]{1,0:T(8,128)(2,1)S(1)}, u32[]{:S(2)}, u32[]{:S(2)}) collective-permute-start(bf16[256,256]{1,0:T(8,128)(2,1)S(1)} %kernel.36.have), channel_id=1, source_target_pairs={{0,4},{2,6},{4,0},{6,2},{8,12},{10,14},{12,8},{14,10},{16,20},{18,... | collective-permute-start | bytes 393224 | tf_op jit(solution)/shard_map/ppermute | solution.py:33
  155.8 2.5 %collective-permute-done.55.refs_2_ = bf16[256,256]{1,0:T(8,128)(2,1)S(1)} collective-permute-done((bf16[256,256]{1,0:T(8,128)(2,1)S(1)}, bf16[256,256]{1,0:T(8,128)(2,1)S(1)}, u32[]{:S(2)}, u32[]{:S(2)}) %collective-permute-start.55) | collective-permute-done | bytes 131104 | tf_op jit(solution)/shard_map/ppermute | solution.py:33
  158.3 1.3 collective-permute-done.54.refs_1_
  160.5 1.1 kernel.37
  161.5 1.1 kernel.32
  (98 shorter events, 10.4 us)
Async XLA Ops:
  0.6 27.1 %collective-permute-start.7 = (f32[2,2,256,256]{3,2,1,0:T(8,128)}, f32[2,2,256,256]{3,2,1,0:T(8,128)S(1)}, u32[]{:S(2)}, u32[]{:S(2)}) collective-permute-start(f32[2,2,256,256]{3,2,1,0:T(8,128)} %pm.1), channel_id=1, source_target_pairs={{0,1},{1,0},{2,3},{3,2},{4,5},{5,4},{6,7},{7,6},{8,9},{9,8},{10,11... | collective-permute-start | bytes 3145736 | tf_op jit(solution)/shard_map/ppermute | solution.py:37
  2.6 11.9 %collective-permute-start.1 = (bf16[768,128]{1,0:T(8,128)(2,1)S(1)}, bf16[768,128]{1,0:T(8,128)(2,1)S(1)}, u32[]{:S(2)}, u32[]{:S(2)}) collective-permute-start(bf16[768,128]{1,0:T(8,128)(2,1)S(1)} %get-tuple-element.50), channel_id=1, source_target_pairs={{0,30},{2,0},{4,2},{6,4},{8,6},{10,8},{12,10},{14,12},{16,14},{18,... | collective-permute-start | bytes 589832 | tf_op jit(solution)/shard_map/ppermute | solution.py:28
  9.2 15.9 %collective-permute-start.2 = (bf16[768,128]{1,0:T(8,128)(2,1)S(1)}, bf16[768,128]{1,0:T(8,128)(2,1)S(1)}, u32[]{:S(2)}, u32[]{:S(2)}) collective-permute-start(bf16[768,128]{1,0:T(8,128)(2,1)S(1)} %get-tuple-element.51), channel_id=1, source_target_pairs={{0,16},{2,18},{4,20},{6,22},{8,24},{10,26},{12,28},{14,30},{16,0},... | collective-permute-start | bytes 589832 | tf_op jit(solution)/shard_map/ppermute | solution.py:28
  9.2 18.3 %collective-permute-start = (f32[2,8]{1,0:T(2,128)S(1)}, f32[2,8]{1,0:T(2,128)S(1)}, u32[]{:S(2)}, u32[]{:S(2)}) collective-permute-start(f32[2,8]{1,0:T(2,128)S(1)} %bitcast.24), channel_id=1, source_target_pairs={{0,1},{1,0},{2,3},{3,2},{4,5},{5,4},{6,7},{7,6},{8,9},{9,8},{10,11... | collective-permute-start | bytes 200 | tf_op jit(solution)/shard_map/ppermute | solution.py:37
  9.4 16.7 %collective-permute-start.3 = (bf16[512,128]{1,0:T(8,128)(2,1)S(1)}, bf16[512,128]{1,0:T(8,128)(2,1)S(1)}, u32[]{:S(2)}, u32[]{:S(2)}) collective-permute-start(bf16[512,128]{1,0:T(8,128)(2,1)S(1)} %get-tuple-element.52), channel_id=1, source_target_pairs={{0,14},{2,16},{4,18},{6,20},{8,22},{10,24},{12,26},{14,28},{16,30}... | collective-permute-start | bytes 393224 | tf_op jit(solution)/shard_map/ppermute | solution.py:28
  14.6 13.1 %collective-permute-start.4 = (bf16[768,128]{1,0:T(8,128)(2,1)S(1)}, bf16[768,128]{1,0:T(8,128)(2,1)S(1)}, u32[]{:S(2)}, u32[]{:S(2)}) collective-permute-start(bf16[768,128]{1,0:T(8,128)(2,1)S(1)} %collective-permute-done.1.rm), channel_id=1, source_target_pairs={{0,1},{1,0},{2,3},{3,2},{4,5},{5,4},{6,7},{7,6},{8,9},{9,8},{10,11... | collective-permute-start | bytes 589832 | tf_op jit(solution)/shard_map/ppermute | solution.py:37
  37.2 5.3 %collective-permute-start.9 = (bf16[2048,128]{1,0:T(8,128)(2,1)S(1)}, bf16[2048,128]{1,0:T(8,128)(2,1)S(1)}, u32[]{:S(2)}, u32[]{:S(2)}) collective-permute-start(bf16[2048,128]{1,0:T(8,128)(2,1)S(1)} %get-tuple-element.57), channel_id=1, source_target_pairs={{0,1},{1,0},{2,3},{3,2},{4,5},{5,4},{6,7},{7,6},{8,9},{9,8},{10,11... | collective-permute-start | bytes 1572872 | tf_op jit(solution)/shard_map/ppermute | solution.py:37
  38.9 6.4 %collective-permute-start.21 = (bf16[256,256]{1,0:T(8,128)(2,1)S(1)}, bf16[256,256]{1,0:T(8,128)(2,1)S(1)}, u32[]{:S(2)}, u32[]{:S(2)}) collective-permute-start(bf16[256,256]{1,0:T(8,128)(2,1)S(1)} %get-tuple-element.69), channel_id=1, source_target_pairs={{0,2},{2,0},{4,6},{6,4},{8,10},{10,8},{12,14},{14,12},{16,18},{18,... | collective-permute-start | bytes 393224 | tf_op jit(solution)/shard_map/ppermute | solution.py:33
  38.9 27.5 %collective-permute-start.8 = (bf16[384,384]{1,0:T(8,128)(2,1)S(1)}, bf16[384,384]{1,0:T(8,128)(2,1)S(1)}, u32[]{:S(2)}, u32[]{:S(2)}) collective-permute-start(bf16[384,384]{1,0:T(8,128)(2,1)S(1)} %get-tuple-element.55), channel_id=1, source_target_pairs={{0,1},{1,0},{2,3},{3,2},{4,5},{5,4},{6,7},{7,6},{8,9},{9,8},{10,11... | collective-permute-start | bytes 884744 | tf_op jit(solution)/shard_map/ppermute | solution.py:37
  39.4 8.4 %collective-permute-start.22 = (bf16[256,256]{1,0:T(8,128)(2,1)S(1)}, bf16[256,256]{1,0:T(8,128)(2,1)S(1)}, u32[]{:S(2)}, u32[]{:S(2)}) collective-permute-start(bf16[256,256]{1,0:T(8,128)(2,1)S(1)} %get-tuple-element.70), channel_id=1, source_target_pairs={{0,4},{2,6},{4,0},{6,2},{8,12},{10,14},{12,8},{14,10},{16,20},{18,... | collective-permute-start | bytes 393224 | tf_op jit(solution)/shard_map/ppermute | solution.py:33
  39.4 8.4 %collective-permute-start.23 = (bf16[256,256]{1,0:T(8,128)(2,1)S(1)}, bf16[256,256]{1,0:T(8,128)(2,1)S(1)}, u32[]{:S(2)}, u32[]{:S(2)}) collective-permute-start(bf16[256,256]{1,0:T(8,128)(2,1)S(1)} %get-tuple-element.71), channel_id=1, source_target_pairs={{0,6},{2,4},{4,2},{6,0},{8,14},{10,12},{12,10},{14,8},{16,22},{18,... | collective-permute-start | bytes 393224 | tf_op jit(solution)/shard_map/ppermute | solution.py:33
  42.6 26.3 %collective-permute-start.10 = (bf16[768,128]{1,0:T(8,128)(2,1)S(1)}, bf16[768,128]{1,0:T(8,128)(2,1)S(1)}, u32[]{:S(2)}, u32[]{:S(2)}) collective-permute-start(bf16[768,128]{1,0:T(8,128)(2,1)S(1)} %get-tuple-element.58), channel_id=1, source_target_pairs={{0,2},{2,4},{4,6},{6,8},{8,10},{10,12},{12,14},{14,16},{16,18},{18... | collective-permute-start | bytes 589832 | tf_op jit(solution)/shard_map/ppermute | solution.py:28
  45.3 23.6 %collective-permute-start.11 = (bf16[768,128]{1,0:T(8,128)(2,1)S(1)}, bf16[768,128]{1,0:T(8,128)(2,1)S(1)}, u32[]{:S(2)}, u32[]{:S(2)}) collective-permute-start(bf16[768,128]{1,0:T(8,128)(2,1)S(1)} %get-tuple-element.59), channel_id=1, source_target_pairs={{0,16},{2,18},{4,20},{6,22},{8,24},{10,26},{12,28},{14,30},{16,0},... | collective-permute-start | bytes 589832 | tf_op jit(solution)/shard_map/ppermute | solution.py:28
  47.7 18.7 %collective-permute-start.12 = (bf16[512,128]{1,0:T(8,128)(2,1)S(1)}, bf16[512,128]{1,0:T(8,128)(2,1)S(1)}, u32[]{:S(2)}, u32[]{:S(2)}) collective-permute-start(bf16[512,128]{1,0:T(8,128)(2,1)S(1)} %get-tuple-element.60), channel_id=1, source_target_pairs={{0,18},{2,20},{4,22},{6,24},{8,26},{10,28},{12,30},{14,0},{16,2},{... | collective-permute-start | bytes 393224 | tf_op jit(solution)/shard_map/ppermute | solution.py:28
  47.8 4.5 %collective-permute-start.24 = (bf16[64,256]{1,0:T(8,128)(2,1)S(1)}, bf16[64,256]{1,0:T(8,128)(2,1)S(1)}, u32[]{:S(2)}, u32[]{:S(2)}) collective-permute-start(bf16[64,256]{1,0:T(8,128)(2,1)S(1)} %get-tuple-element.73), channel_id=1, source_target_pairs={{0,8},{2,10},{4,12},{6,14},{8,0},{10,2},{12,4},{14,6},{16,24},{18,... | collective-permute-start | bytes 98312 | tf_op jit(solution)/shard_map/ppermute | solution.py:33
  52.3 6.3 %collective-permute-start.25 = (bf16[64,256]{1,0:T(8,128)(2,1)S(1)}, bf16[64,256]{1,0:T(8,128)(2,1)S(1)}, u32[]{:S(2)}, u32[]{:S(2)}) collective-permute-start(bf16[64,256]{1,0:T(8,128)(2,1)S(1)} %get-tuple-element.74), channel_id=1, source_target_pairs={{0,16},{2,18},{4,20},{6,22},{8,24},{10,26},{12,28},{14,30},{16,0},... | collective-permute-start | bytes 98312 | tf_op jit(solution)/shard_map/ppermute | solution.py:33
  58.7 5.7 %collective-permute-start.26 = (bf16[64,256]{1,0:T(8,128)(2,1)S(1)}, bf16[64,256]{1,0:T(8,128)(2,1)S(1)}, u32[]{:S(2)}, u32[]{:S(2)}) collective-permute-start(bf16[64,256]{1,0:T(8,128)(2,1)S(1)} %get-tuple-element.75), channel_id=1, source_target_pairs={{0,24},{2,26},{4,28},{6,30},{8,16},{10,18},{12,20},{14,22},{16,8},... | collective-permute-start | bytes 98312 | tf_op jit(solution)/shard_map/ppermute | solution.py:33
  64.4 11.6 %collective-permute-start.29 = (bf16[64,256]{1,0:T(8,128)(2,1)S(1)}, bf16[64,256]{1,0:T(8,128)(2,1)S(1)}, u32[]{:S(2)}, u32[]{:S(2)}) collective-permute-start(bf16[64,256]{1,0:T(8,128)(2,1)S(1)} %kernel.25.have), channel_id=1, source_target_pairs={{0,24},{2,26},{4,28},{6,30},{8,16},{10,18},{12,20},{14,22},{16,8},... | collective-permute-start | bytes 98312 | tf_op jit(solution)/shard_map/ppermute | solution.py:33
  66.4 9.6 %collective-permute-start.28 = (bf16[64,256]{1,0:T(8,128)(2,1)S(1)}, bf16[64,256]{1,0:T(8,128)(2,1)S(1)}, u32[]{:S(2)}, u32[]{:S(2)}) collective-permute-start(bf16[64,256]{1,0:T(8,128)(2,1)S(1)} %kernel.25.have), channel_id=1, source_target_pairs={{0,16},{2,18},{4,20},{6,22},{8,24},{10,26},{12,28},{14,30},{16,0},... | collective-permute-start | bytes 98312 | tf_op jit(solution)/shard_map/ppermute | solution.py:33
  66.4 9.6 %collective-permute-start.27 = (bf16[64,256]{1,0:T(8,128)(2,1)S(1)}, bf16[64,256]{1,0:T(8,128)(2,1)S(1)}, u32[]{:S(2)}, u32[]{:S(2)}) collective-permute-start(bf16[64,256]{1,0:T(8,128)(2,1)S(1)} %kernel.25.have), channel_id=1, source_target_pairs={{0,8},{2,10},{4,12},{6,14},{8,0},{10,2},{12,4},{14,6},{16,24},{18,... | collective-permute-start | bytes 98312 | tf_op jit(solution)/shard_map/ppermute | solution.py:33
  69.2 10.9 %collective-permute-start.15 = (bf16[512,128]{1,0:T(8,128)(2,1)S(1)}, bf16[512,128]{1,0:T(8,128)(2,1)S(1)}, u32[]{:S(2)}, u32[]{:S(2)}) collective-permute-start(bf16[512,128]{1,0:T(8,128)(2,1)S(1)} %get-tuple-element.65), channel_id=1, source_target_pairs={{0,14},{2,16},{4,18},{6,20},{8,22},{10,24},{12,26},{14,28},{16,30}... | collective-permute-start | bytes 393224 | tf_op jit(solution)/shard_map/ppermute | solution.py:28
  76.1 9.2 %collective-permute-start.33 = (bf16[256,256]{1,0:T(8,128)(2,1)S(1)}, bf16[256,256]{1,0:T(8,128)(2,1)S(1)}, u32[]{:S(2)}, u32[]{:S(2)}) collective-permute-start(bf16[256,256]{1,0:T(8,128)(2,1)S(1)} %kernel.26.have), channel_id=1, source_target_pairs={{0,1},{1,0},{2,3},{3,2},{4,5},{5,4},{6,7},{7,6},{8,9},{9,8},{10,11... | collective-permute-start | bytes 393224 | tf_op jit(solution)/shard_map/ppermute | solution.py:37
  76.2 9.1 %collective-permute-start.32 = (bf16[256,256]{1,0:T(8,128)(2,1)S(1)}, bf16[256,256]{1,0:T(8,128)(2,1)S(1)}, u32[]{:S(2)}, u32[]{:S(2)}) collective-permute-start(bf16[256,256]{1,0:T(8,128)(2,1)S(1)} %kernel.26.have), channel_id=1, source_target_pairs={{0,6},{2,4},{4,2},{6,0},{8,14},{10,12},{12,10},{14,8},{16,22},{18,... | collective-permute-start | bytes 393224 | tf_op jit(solution)/shard_map/ppermute | solution.py:33
  79.5 7.4 %collective-permute-start.31 = (bf16[256,256]{1,0:T(8,128)(2,1)S(1)}, bf16[256,256]{1,0:T(8,128)(2,1)S(1)}, u32[]{:S(2)}, u32[]{:S(2)}) collective-permute-start(bf16[256,256]{1,0:T(8,128)(2,1)S(1)} %kernel.26.have), channel_id=1, source_target_pairs={{0,4},{2,6},{4,0},{6,2},{8,12},{10,14},{12,8},{14,10},{16,20},{18,... | collective-permute-start | bytes 393224 | tf_op jit(solution)/shard_map/ppermute | solution.py:33
  79.5 10.7 %collective-permute-start.30 = (bf16[256,256]{1,0:T(8,128)(2,1)S(1)}, bf16[256,256]{1,0:T(8,128)(2,1)S(1)}, u32[]{:S(2)}, u32[]{:S(2)}) collective-permute-start(bf16[256,256]{1,0:T(8,128)(2,1)S(1)} %kernel.26.have), channel_id=1, source_target_pairs={{0,2},{2,0},{4,6},{6,4},{8,10},{10,8},{12,14},{14,12},{16,18},{18,... | collective-permute-start | bytes 393224 | tf_op jit(solution)/shard_map/ppermute | solution.py:33
  80.1 10.1 %collective-permute-start.13 = (bf16[768,128]{1,0:T(8,128)(2,1)S(1)}, bf16[768,128]{1,0:T(8,128)(2,1)S(1)}, u32[]{:S(2)}, u32[]{:S(2)}) collective-permute-start(bf16[768,128]{1,0:T(8,128)(2,1)S(1)} %get-tuple-element.63), channel_id=1, source_target_pairs={{0,30},{2,0},{4,2},{6,4},{8,6},{10,8},{12,10},{14,12},{16,14},{18,... | collective-permute-start | bytes 589832 | tf_op jit(solution)/shard_map/ppermute | solution.py:28
  85.3 11.1 %collective-permute-start.14 = (bf16[768,128]{1,0:T(8,128)(2,1)S(1)}, bf16[768,128]{1,0:T(8,128)(2,1)S(1)}, u32[]{:S(2)}, u32[]{:S(2)}) collective-permute-start(bf16[768,128]{1,0:T(8,128)(2,1)S(1)} %get-tuple-element.64), channel_id=1, source_target_pairs={{0,16},{2,18},{4,20},{6,22},{8,24},{10,26},{12,28},{14,30},{16,0},... | collective-permute-start | bytes 589832 | tf_op jit(solution)/shard_map/ppermute | solution.py:28
  85.3 13.0 %collective-permute-start.16 = (bf16[384,384]{1,0:T(8,128)(2,1)S(1)}, bf16[384,384]{1,0:T(8,128)(2,1)S(1)}, u32[]{:S(2)}, u32[]{:S(2)}) collective-permute-start(bf16[384,384]{1,0:T(8,128)(2,1)S(1)} %get-tuple-element.62.tm), channel_id=1, source_target_pairs={{0,1},{1,0},{2,3},{3,2},{4,5},{5,4},{6,7},{7,6},{8,9},{9,8},{10,11... | collective-permute-start | bytes 884744 | tf_op jit(solution)/shard_map/ppermute | solution.py:37
  86.9 9.6 %collective-permute-start.36 = (bf16[256,256]{1,0:T(8,128)(2,1)S(1)}, bf16[256,256]{1,0:T(8,128)(2,1)S(1)}, u32[]{:S(2)}, u32[]{:S(2)}) collective-permute-start(bf16[256,256]{1,0:T(8,128)(2,1)S(1)} %collective-permute-done.32.refs_2_), channel_id=1, source_target_pairs={{0,1},{1,0},{2,3},{3,2},{4,5},{5,4},{6,7},{7,6},{8,9},{9,8},{10,11... | collective-permute-start | bytes 393224 | tf_op jit(solution)/shard_map/ppermute | solution.py:37
  90.2 6.7 %collective-permute-start.35 = (bf16[256,256]{1,0:T(8,128)(2,1)S(1)}, bf16[256,256]{1,0:T(8,128)(2,1)S(1)}, u32[]{:S(2)}, u32[]{:S(2)}) collective-permute-start(bf16[256,256]{1,0:T(8,128)(2,1)S(1)} %collective-permute-done.31.refs_1_), channel_id=1, source_target_pairs={{0,1},{1,0},{2,3},{3,2},{4,5},{5,4},{6,7},{7,6},{8,9},{9,8},{10,11... | collective-permute-start | bytes 393224 | tf_op jit(solution)/shard_map/ppermute | solution.py:37
  90.2 8.1 %collective-permute-start.17 = (bf16[768,128]{1,0:T(8,128)(2,1)S(1)}, bf16[768,128]{1,0:T(8,128)(2,1)S(1)}, u32[]{:S(2)}, u32[]{:S(2)}) collective-permute-start(bf16[768,128]{1,0:T(8,128)(2,1)S(1)} %collective-permute-done.13.rm), channel_id=1, source_target_pairs={{0,1},{1,0},{2,3},{3,2},{4,5},{5,4},{6,7},{7,6},{8,9},{9,8},{10,11... | collective-permute-start | bytes 589832 | tf_op jit(solution)/shard_map/ppermute | solution.py:37
  107.9 16.1 %collective-permute-start.43 = (bf16[2,2,256,256]{3,2,1,0:T(8,128)(2,1)S(1)}, bf16[2,2,256,256]{3,2,1,0:T(8,128)(2,1)S(1)}, u32[]{:S(2)}, u32[]{:S(2)}) collective-permute-start(bf16[2,2,256,256]{3,2,1,0:T(8,128)(2,1)S(1)} %get-tuple-element.85), channel_id=1, source_target_pairs={{0,1},{1,0},{2,3},{3,2},{4,5},{5,4},{6,7},{7,6},{8,9},{9,8},{10,11... | collective-permute-start | bytes 1572872 | tf_op jit(solution)/shard_map/ppermute | solution.py:37
  109.4 13.5 %collective-permute-start.39 = (bf16[768,128]{1,0:T(8,128)(2,1)S(1)}, bf16[768,128]{1,0:T(8,128)(2,1)S(1)}, u32[]{:S(2)}, u32[]{:S(2)}) collective-permute-start(bf16[768,128]{1,0:T(8,128)(2,1)S(1)} %get-tuple-element.80), channel_id=1, source_target_pairs={{0,2},{2,4},{4,6},{6,8},{8,10},{10,12},{12,14},{14,16},{16,18},{18... | collective-permute-start | bytes 589832 | tf_op jit(solution)/shard_map/ppermute | solution.py:28
  109.5 13.5 %collective-permute-start.40 = (bf16[768,128]{1,0:T(8,128)(2,1)S(1)}, bf16[768,128]{1,0:T(8,128)(2,1)S(1)}, u32[]{:S(2)}, u32[]{:S(2)}) collective-permute-start(bf16[768,128]{1,0:T(8,128)(2,1)S(1)} %get-tuple-element.81), channel_id=1, source_target_pairs={{0,16},{2,18},{4,20},{6,22},{8,24},{10,26},{12,28},{14,30},{16,0},... | collective-permute-start | bytes 589832 | tf_op jit(solution)/shard_map/ppermute | solution.py:28
  109.5 13.4 %collective-permute-start.41 = (bf16[512,128]{1,0:T(8,128)(2,1)S(1)}, bf16[512,128]{1,0:T(8,128)(2,1)S(1)}, u32[]{:S(2)}, u32[]{:S(2)}) collective-permute-start(bf16[512,128]{1,0:T(8,128)(2,1)S(1)} %get-tuple-element.82), channel_id=1, source_target_pairs={{0,18},{2,20},{4,22},{6,24},{8,26},{10,28},{12,30},{14,0},{16,2},{... | collective-permute-start | bytes 393224 | tf_op jit(solution)/shard_map/ppermute | solution.py:28
  124.0 37.5 %collective-permute-start.42 = (f32[384,384]{1,0:T(8,128)S(1)}, f32[384,384]{1,0:T(8,128)S(1)}, u32[]{:S(2)}, u32[]{:S(2)}) collective-permute-start(f32[384,384]{1,0:T(8,128)S(1)} %get-tuple-element.83.state), channel_id=1, source_target_pairs={{0,1},{1,0},{2,3},{3,2},{4,5},{5,4},{6,7},{7,6},{8,9},{9,8},{10,11... | collective-permute-start | bytes 1769480 | tf_op jit(solution)/shard_map/ppermute | solution.py:37
  124.1 7.9 %collective-permute-start.44 = (bf16[256,256]{1,0:T(8,128)(2,1)S(1)}, bf16[256,256]{1,0:T(8,128)(2,1)S(1)}, u32[]{:S(2)}, u32[]{:S(2)}) collective-permute-start(bf16[256,256]{1,0:T(8,128)(2,1)S(1)} %get-tuple-element.87), channel_id=1, source_target_pairs={{0,2},{2,0},{4,6},{6,4},{8,10},{10,8},{12,14},{14,12},{16,18},{18,... | collective-permute-start | bytes 393224 | tf_op jit(solution)/shard_map/ppermute | solution.py:33
  127.7 8.4 %collective-permute-start.45 = (bf16[256,256]{1,0:T(8,128)(2,1)S(1)}, bf16[256,256]{1,0:T(8,128)(2,1)S(1)}, u32[]{:S(2)}, u32[]{:S(2)}) collective-permute-start(bf16[256,256]{1,0:T(8,128)(2,1)S(1)} %get-tuple-element.88), channel_id=1, source_target_pairs={{0,4},{2,6},{4,0},{6,2},{8,12},{10,14},{12,8},{14,10},{16,20},{18,... | collective-permute-start | bytes 393224 | tf_op jit(solution)/shard_map/ppermute | solution.py:33
  128.8 7.3 %collective-permute-start.46 = (bf16[256,256]{1,0:T(8,128)(2,1)S(1)}, bf16[256,256]{1,0:T(8,128)(2,1)S(1)}, u32[]{:S(2)}, u32[]{:S(2)}) collective-permute-start(bf16[256,256]{1,0:T(8,128)(2,1)S(1)} %get-tuple-element.89), channel_id=1, source_target_pairs={{0,6},{2,4},{4,2},{6,0},{8,14},{10,12},{12,10},{14,8},{16,22},{18,... | collective-permute-start | bytes 393224 | tf_op jit(solution)/shard_map/ppermute | solution.py:33
  136.2 5.4 %collective-permute-start.47 = (bf16[64,256]{1,0:T(8,128)(2,1)S(1)}, bf16[64,256]{1,0:T(8,128)(2,1)S(1)}, u32[]{:S(2)}, u32[]{:S(2)}) collective-permute-start(bf16[64,256]{1,0:T(8,128)(2,1)S(1)} %get-tuple-element.91), channel_id=1, source_target_pairs={{0,8},{2,10},{4,12},{6,14},{8,0},{10,2},{12,4},{14,6},{16,24},{18,... | collective-permute-start | bytes 98312 | tf_op jit(solution)/shard_map/ppermute | solution.py:33
  139.2 4.8 %collective-permute-start.48 = (bf16[64,256]{1,0:T(8,128)(2,1)S(1)}, bf16[64,256]{1,0:T(8,128)(2,1)S(1)}, u32[]{:S(2)}, u32[]{:S(2)}) collective-permute-start(bf16[64,256]{1,0:T(8,128)(2,1)S(1)} %get-tuple-element.92), channel_id=1, source_target_pairs={{0,16},{2,18},{4,20},{6,22},{8,24},{10,26},{12,28},{14,30},{16,0},... | collective-permute-start | bytes 98312 | tf_op jit(solution)/shard_map/ppermute | solution.py:33
  139.5 5.7 %collective-permute-start.49 = (bf16[64,256]{1,0:T(8,128)(2,1)S(1)}, bf16[64,256]{1,0:T(8,128)(2,1)S(1)}, u32[]{:S(2)}, u32[]{:S(2)}) collective-permute-start(bf16[64,256]{1,0:T(8,128)(2,1)S(1)} %get-tuple-element.93), channel_id=1, source_target_pairs={{0,24},{2,26},{4,28},{6,30},{8,16},{10,18},{12,20},{14,22},{16,8},... | collective-permute-start | bytes 98312 | tf_op jit(solution)/shard_map/ppermute | solution.py:33
  145.2 5.8 %collective-permute-start.52 = (bf16[64,256]{1,0:T(8,128)(2,1)S(1)}, bf16[64,256]{1,0:T(8,128)(2,1)S(1)}, u32[]{:S(2)}, u32[]{:S(2)}) collective-permute-start(bf16[64,256]{1,0:T(8,128)(2,1)S(1)} %kernel.35.have), channel_id=1, source_target_pairs={{0,24},{2,26},{4,28},{6,30},{8,16},{10,18},{12,20},{14,22},{16,8},... | collective-permute-start | bytes 98312 | tf_op jit(solution)/shard_map/ppermute | solution.py:33
  147.4 4.8 %collective-permute-start.51 = (bf16[64,256]{1,0:T(8,128)(2,1)S(1)}, bf16[64,256]{1,0:T(8,128)(2,1)S(1)}, u32[]{:S(2)}, u32[]{:S(2)}) collective-permute-start(bf16[64,256]{1,0:T(8,128)(2,1)S(1)} %kernel.35.have), channel_id=1, source_target_pairs={{0,16},{2,18},{4,20},{6,22},{8,24},{10,26},{12,28},{14,30},{16,0},... | collective-permute-start | bytes 98312 | tf_op jit(solution)/shard_map/ppermute | solution.py:33
  147.4 4.8 %collective-permute-start.50 = (bf16[64,256]{1,0:T(8,128)(2,1)S(1)}, bf16[64,256]{1,0:T(8,128)(2,1)S(1)}, u32[]{:S(2)}, u32[]{:S(2)}) collective-permute-start(bf16[64,256]{1,0:T(8,128)(2,1)S(1)} %kernel.35.have), channel_id=1, source_target_pairs={{0,8},{2,10},{4,12},{6,14},{8,0},{10,2},{12,4},{14,6},{16,24},{18,... | collective-permute-start | bytes 98312 | tf_op jit(solution)/shard_map/ppermute | solution.py:33
  152.3 6.0 %collective-permute-start.55 = (bf16[256,256]{1,0:T(8,128)(2,1)S(1)}, bf16[256,256]{1,0:T(8,128)(2,1)S(1)}, u32[]{:S(2)}, u32[]{:S(2)}) collective-permute-start(bf16[256,256]{1,0:T(8,128)(2,1)S(1)} %kernel.36.have), channel_id=1, source_target_pairs={{0,6},{2,4},{4,2},{6,0},{8,14},{10,12},{12,10},{14,8},{16,22},{18,... | collective-permute-start | bytes 393224 | tf_op jit(solution)/shard_map/ppermute | solution.py:33
  153.8 5.9 %collective-permute-start.54 = (bf16[256,256]{1,0:T(8,128)(2,1)S(1)}, bf16[256,256]{1,0:T(8,128)(2,1)S(1)}, u32[]{:S(2)}, u32[]{:S(2)}) collective-permute-start(bf16[256,256]{1,0:T(8,128)(2,1)S(1)} %kernel.36.have), channel_id=1, source_target_pairs={{0,4},{2,6},{4,0},{6,2},{8,12},{10,14},{12,8},{14,10},{16,20},{18,... | collective-permute-start | bytes 393224 | tf_op jit(solution)/shard_map/ppermute | solution.py:33
  155.5 5.0 %collective-permute-start.53 = (bf16[256,256]{1,0:T(8,128)(2,1)S(1)}, bf16[256,256]{1,0:T(8,128)(2,1)S(1)}, u32[]{:S(2)}, u32[]{:S(2)}) collective-permute-start(bf16[256,256]{1,0:T(8,128)(2,1)S(1)} %kernel.36.have), channel_id=1, source_target_pairs={{0,2},{2,0},{4,6},{6,4},{8,10},{10,8},{12,14},{14,12},{16,18},{18,... | collective-permute-start | bytes 393224 | tf_op jit(solution)/shard_map/ppermute | solution.py:33
  (14 other events, 125.5 us)
where the time goes:
time: 163 us
  waiting for transfers between devices  72.2 us (44%)
  starting transfers between devices  62.8 us (39%)
  Pallas kernels  22.6 us (14%)
  other arithmetic  2.17 us (1%)
    ppermute x24, starting transfers between devices, flipped(): return lax.ppermute(array, 'tile', [(i, i ^ mask) for i in range(peers)])  38.5 us
    ppermute x24, waiting for transfers between devices, flipped(): return lax.ppermute(array, 'tile', [(i, i ^ mask) for i in range(peers)])  35.4 us
    ppermute x12, waiting for transfers between devices, shifted(): lax.ppermute(array, 'tile', [(i, (i + by) % peers) for i in range(peers)])  32.6 us
    pallas_call x19, Pallas kernels, call(): pl.pallas_call(kernel, out_shape=tuple((jax.ShapeDtypeStruct(shape, dtype...  22.6 us
    ppermute x12, starting transfers between devices, shifted(): lax.ppermute(array, 'tile', [(i, (i + by) % peers) for i in range(peers)])  20 us
    ppermute x20, starting transfers between devices, swapped(): return lax.ppermute(array, 'mode', [(0, 1), (1, 0)])  4.36 us
    ppermute x20, waiting for transfers between devices, swapped(): return lax.ppermute(array, 'mode', [(0, 1), (1, 0)])  4.1 us
  transfers between devices with their start and end apart: 56, of which 26 were waited for; matrix products, arithmetic and copies ran while one was open for 1% of the time, Pallas kernels for 2%

commit v1 on v0

--- a/solution.py
+++ b/solution.py
@@ -38,19 +38,21 @@
 
 
 def dft_tables(length):
-    index = jnp.arange(length, dtype=jnp.int32)
-    product = index[:, None] * index[None, :] % length
-    angle = product.astype(f32) * (2.0 * math.pi / length)
+    half = jnp.arange(length // 2, dtype=jnp.int32)
     factor = 1.0 / math.sqrt(length)
-    real = jnp.cos(angle) * factor
-    imag = -(jnp.sin(angle) * factor)
-    one = jnp.concatenate(
-        [jnp.concatenate([real, -imag], 1), jnp.concatenate([imag, real], 1)], 0
-    ).astype(bf16)
-    two = jnp.concatenate(
-        [jnp.concatenate([real, imag], 1), jnp.concatenate([-imag, real], 1)], 0
-    ).astype(bf16)
-    return one, two
+    tall, wide = [], []
+    for parity in (0, 1):
+        product = (2 * half[:, None] + parity) * half[None, :] % length
+        for value, out in ((product, tall), (product.T, wide)):
+            angle = value.astype(f32) * (2.0 * math.pi / length)
+            real = jnp.cos(angle) * factor
+            imag = -(jnp.sin(angle) * factor)
+            if out is tall:
+                rows = [[real, -imag], [imag, real]]
+            else:
+                rows = [[real, imag], [-imag, real]]
+            out.append(jnp.concatenate([jnp.concatenate(row, 1) for row in rows], 0))
+    return jnp.stack(tall).astype(bf16), jnp.stack(wide).astype(bf16)
 
 
 def dot(a, b):
@@ -71,7 +73,7 @@
 
 def patch_kernel(
     live, corner, kind, wm, wo,
-    tm, rm, bm, dm, to, ro, bo, do, meas, pm, po, one, two,
+    tm, rm, bm, dm, to, ro, bo, do, meas, pm, po, tall, wide_table,
     own_keep, own_send, edge_keep, edge_send, pgm, pgo,
     frame, grad, psi, xs, ts, orr, oii, term, acc,
 ):
@@ -80,6 +82,7 @@
     half = pm.shape[0]
     modes = 2 * half
     me = lax.axis_index("mode")
+    h = n // 2
     for plane, (a, b, c, d) in ((me, (tm, rm, bm, dm)), (1 - me, (to, ro, bo, do))):
         frame[plane, pl.ds(0, t), pl.ds(0, t)] = a[...].astype(f32)
         for ref, top, left, high, wide in blocks(t, n, (b, c, d)):
@@ -88,10 +91,11 @@
                 frame[plane, pl.ds(top, high), pl.ds(left + k * LANES, LANES)] = part
     grad[...] = jnp.zeros_like(grad)
     acc[...] = jnp.zeros_like(acc)
-
-    def probe_at(m, c, rows):
+    term[...] = jnp.zeros_like(term)
+
+    def probe_at(m, c, rows, cols=slice(None)):
         ref = pm if m < half else po
-        return ref[m % half, c, rows, :]
+        return ref[m % half, c, rows, cols]
 
     def slot_body(g, carry):
         s = me + 2 * g
@@ -110,60 +114,85 @@
                 win = pltpu.roll(win, lax.rem(wide - cc, wide), 1)[:, :n]
                 win = pltpu.roll(win, lax.rem(high - rr, high), 0)[:n]
                 out[...] = win
-            strips = [pl.ds(i * STRIP, STRIP) for i in range(n // STRIP)]
-            lower = [pl.ds(n + i * STRIP, STRIP) for i in range(n // STRIP)]
+            lanes = [pl.ds(q * h, h) for q in range(2)]
             w = [wm[m, kind[s]] if m < half else wo[m - half, kind[s]] for m in range(modes)]
             for m in range(modes):
-                for up, lo in zip(strips, lower):
-                    a, b = orr[up, :], oii[up, :]
-                    pr, pi = probe_at(m, 0, up), probe_at(m, 1, up)
-                    xs[m, up, :] = (pr * a - pi * b).astype(bf16)
-                    xs[m, lo, :] = (pr * b + pi * a).astype(bf16)
+                for i in range(h // STRIP):
+                    up, low = pl.ds(i * STRIP, STRIP), pl.ds(h + i * STRIP, STRIP)
+                    parts = []
+                    for rows in (up, low):
+                        a, b = orr[rows, :], oii[rows, :]
+                        pr, pi = probe_at(m, 0, rows), probe_at(m, 1, rows)
+                        parts.append((pr * a - pi * b, pr * b + pi * a))
+                    (r0, i0), (r1, i1) = parts
+                    xs[m, 0, up, :] = (r0 + r1).astype(bf16)
+                    xs[m, 0, low, :] = (i0 + i1).astype(bf16)
+                    xs[m, 1, up, :] = (r0 - r1).astype(bf16)
+                    xs[m, 1, low, :] = (i0 - i1).astype(bf16)
             for m in range(modes):
-                y = dot(one[...], xs[m])
-                ts[pl.ds(m * n, n), pl.ds(0, n)] = y[:n].astype(bf16)
-                ts[pl.ds(m * n, n), pl.ds(n, n)] = y[n:].astype(bf16)
-            psi[...] = dot(ts[...], two[...])
-            for i, (up, lo) in enumerate(zip(strips, lower)):
-                total = jnp.zeros((STRIP, n), f32)
-                for m in range(modes):
-                    rows = pl.ds(m * n + i * STRIP, STRIP)
-                    a, b = psi[rows, pl.ds(0, n)], psi[rows, pl.ds(n, n)]
-                    total = total + w[m] * (a * a + b * b)
-                resid = total - meas[s, up, :]
-                for m in range(modes):
-                    rows = pl.ds(m * n + i * STRIP, STRIP)
-                    scale = w[m] * resid
-                    xs[m, up, :] = (scale * psi[rows, pl.ds(0, n)]).astype(bf16)
-                    xs[m, lo, :] = (scale * psi[rows, pl.ds(n, n)]).astype(bf16)
+                for p in range(2):
+                    y = dot(tall[p], xs[m, p])
+                    rows = pl.ds(m * n + p * h, h)
+                    for c in range(2):
+                        part = y[c * h : (c + 1) * h]
+                        ts[0, rows, lanes[c]] = (part[:, :h] + part[:, h:]).astype(bf16)
+                        ts[1, rows, lanes[c]] = (part[:, :h] - part[:, h:]).astype(bf16)
+            for q in range(2):
+                psi[q] = dot(ts[q], wide_table[q])
+            for i in range(n // STRIP):
+                p, base = divmod(i * STRIP, h)
+                for q in range(2):
+                    total = jnp.zeros((STRIP, h), f32)
+                    for m in range(modes):
+                        rows = pl.ds(m * n + i * STRIP, STRIP)
+                        a, b = psi[q, rows, lanes[0]], psi[q, rows, lanes[1]]
+                        total = total + w[m] * (a * a + b * b)
+                    resid = total - meas[g, pl.ds(i * STRIP, STRIP), lanes[q]]
+                    for m in range(modes):
+                        rows = pl.ds(m * n + i * STRIP, STRIP)
+                        scale = w[m] * resid
+                        for c in range(2):
+                            value = scale * psi[q, rows, lanes[c]]
+                            xs[m, p, pl.ds(c * h + base, STRIP), lanes[q]] = value.astype(bf16)
             for m in range(modes):
-                y = dot(two[...], xs[m])
-                ts[pl.ds(m * n, n), pl.ds(0, n)] = y[:n].astype(bf16)
-                ts[pl.ds(m * n, n), pl.ds(n, n)] = y[n:].astype(bf16)
-            psi[...] = dot(ts[...], one[...])
-            for i, up in enumerate(strips):
-                a, b = orr[up, :], oii[up, :]
-                tr = jnp.zeros((STRIP, n), f32)
-                ti = jnp.zeros((STRIP, n), f32)
-                for m in range(modes):
-                    rows = pl.ds(m * n + i * STRIP, STRIP)
-                    cr, ci = psi[rows, pl.ds(0, n)], psi[rows, pl.ds(n, n)]
-                    pr, pi = probe_at(m, 0, up), probe_at(m, 1, up)
-                    tr = tr + (pr * cr + pi * ci)
-                    ti = ti + (pr * ci - pi * cr)
-                    acc[m, 0, up, :] += a * cr + b * ci
-                    acc[m, 1, up, :] += a * ci - b * cr
-                term[0, up, pl.ds(0, n)] = tr
-                term[1, up, pl.ds(0, n)] = ti
+                even = dot(wide_table[0], xs[m, 0])
+                odd = dot(wide_table[1], xs[m, 1])
+                for side, y in enumerate((even + odd, even - odd)):
+                    rows = pl.ds(m * n + side * h, h)
+                    for c in range(2):
+                        part = y[c * h : (c + 1) * h].astype(bf16)
+                        ts[0, rows, lanes[c]] = part[:, :h]
+                        ts[1, rows, lanes[c]] = part[:, h:]
+            for q in range(2):
+                psi[q] = dot(ts[q], tall[q])
+            for i in range(n // STRIP):
+                up = pl.ds(i * STRIP, STRIP)
+                for side in range(2):
+                    cols = lanes[side]
+                    a, b = orr[up, cols], oii[up, cols]
+                    tr = jnp.zeros((STRIP, h), f32)
+                    ti = jnp.zeros((STRIP, h), f32)
+                    for m in range(modes):
+                        rows = pl.ds(m * n + i * STRIP, STRIP)
+                        sums = []
+                        for c in range(2):
+                            first, second = psi[0, rows, lanes[c]], psi[1, rows, lanes[c]]
+                            sums.append(first - second if side else first + second)
+                        cr, ci = sums
+                        pr, pi = probe_at(m, 0, up, cols), probe_at(m, 1, up, cols)
+                        tr = tr + (pr * cr + pi * ci)
+                        ti = ti + (pr * ci - pi * cr)
+                        acc[m, 0, up, cols] += a * cr + b * ci
+                        acc[m, 1, up, cols] += a * ci - b * cr
+                    term[0, up, cols] = tr
+                    term[1, up, cols] = ti
             for p in range(2):
-                term[p, pl.ds(n, 8), :] = jnp.zeros((8, wide), f32)
-                term[p, pl.ds(0, n), pl.ds(n, 128)] = jnp.zeros((n, 128), f32)
                 moved = pltpu.roll(pltpu.roll(term[p], rr, 0), cc, 1)
                 grad[p, pl.ds(rb, high), pl.ds(cb, wide)] += moved
 
         return carry
 
-    lax.fori_loop(0, meas.shape[0] // 2, slot_body, 0)
+    lax.fori_loop(0, meas.shape[0], slot_body, 0)
     own_keep[...] = grad[me, pl.ds(0, t), pl.ds(0, t)]
     own_send[...] = grad[1 - me, pl.ds(0, t), pl.ds(0, t)].astype(bf16)
     base = 0
@@ -190,7 +219,37 @@
     )(*args)
 
 
-def patches(live, corner, kind, wm, wo, mine, other, meas, pm, po, one, two):
+def sort_kernel(meas, out):
+    me = lax.axis_index("mode")
+    n = out.shape[-1]
+    h = n // 2
+    row = lax.broadcasted_iota(jnp.int32, (n, n), 0)
+    col = lax.broadcasted_iota(jnp.int32, (n, n), 1)
+
+    def source(i):
+        return jnp.where(i < h, 2 * i, 2 * i - (n - 1))
+
+    def exact(product, value):
+        total = jnp.zeros_like(value)
+        for _ in range(3):
+            part = value.astype(bf16)
+            total = total + product(part)
+            value = value - part.astype(f32)
+        return total
+
+    right = (row == source(col)).astype(f32).astype(bf16)
+    left = (col == source(row)).astype(f32).astype(bf16)
+    for g in range(out.shape[0]):
+        value = exact(lambda part: dot(part, right), meas[me + 2 * g])
+        out[g] = exact(lambda part: dot(left, part), value)
+
+
+def sort(meas):
+    outs = (((meas.shape[0] // 2, *meas.shape[1:]), f32),)
+    return call(sort_kernel, outs, meas)[0]
+
+
+def patches(live, corner, kind, wm, wo, mine, other, meas, pm, po, tall, wide):
     n = pm.shape[-1]
     t = mine[0].shape[-1]
     f = n + t
@@ -206,14 +265,14 @@
             (pm.shape, f32),
             (pm.shape, bf16),
         ),
-        live, corner, kind, wm, wo, *mine, *other, meas, pm, po, one, two,
+        live, corner, kind, wm, wo, *mine, *other, meas, pm, po, tall, wide,
         smem=5,
         scratch=[
             pltpu.VMEM((2, f, f), f32),
             pltpu.VMEM((2, f, f), f32),
-            pltpu.VMEM((modes * n, 2 * n), f32),
-            pltpu.VMEM((modes, 2 * n, n), bf16),
-            pltpu.VMEM((modes * n, 2 * n), bf16),
+            pltpu.VMEM((2, modes * n, n), f32),
+            pltpu.VMEM((modes, 2, n, n), bf16),
+            pltpu.VMEM((2, modes * n, n), bf16),
             pltpu.VMEM((n, n), f32),
             pltpu.VMEM((n, n), f32),
             pltpu.VMEM((2, n + 8, n + 128), f32),
@@ -406,7 +465,7 @@
 def steps(obj, probe, mode_weights, measured, corner, counts, weight_index):
     n = probe.shape[-1]
     t = obj.shape[-1]
-    one, two = dft_tables(n)
+    tall, wide = dft_tables(n)
     rate = step_probe / (POS_DEV * lax.axis_size("tile"))
     state, half, rest, *edges = enter(obj[0], n)
     pm = probe
@@ -414,6 +473,7 @@
     wm = mode_weights.T
     wo = swapped(wm)
     spots = corner.T
+    meas = sort(measured)
     for sweep in range(ITERS):
         low = shifted(edges[1], -GC)
         diag = shifted(edges[2], -(GC + 1))
@@ -421,7 +481,7 @@
         mine = (half, right, low, diag)
         other = (rest, swapped(right), swapped(low), swapped(diag))
         own_keep, own_send, edge_keep, edge_send, pgm, pgo = patches(
-            counts, spots, weight_index, wm, wo, mine, other, measured, pm, po, one, two
+            counts, spots, weight_index, wm, wo, mine, other, meas, pm, po, tall, wide
         )
         edge_got = swapped(edge_send)
         right, low, diag = margins(edge_keep, edge_got, t, n)

time: 163 us -> 161 us (0.988)
  Pallas kernels: 22.6 us -> 20.7 us
  starting transfers between devices: 62.8 us -> 64.5 us
    pallas_call x19 -> x20, Pallas kernels: 22.6 us -> 20.7 us  [call(): pl.pallas_call(kernel, out_shape=tuple((jax.ShapeDtypeStruct(shape, dtype...]
    ppermute x12, starting transfers between devices: 20 us -> 21.6 us  [shifted(): lax.ppermute(array, 'tile', [(i, (i + by) % peers) for i in range(peers)])]
  transfers between devices with their start and end apart: 56 -> 56, of which waited for: 26 -> 26; matrix products, arithmetic and copies ran while one was open for 1% -> 1% of each run, Pallas kernels for 2% -> 3%
where the time goes in v1:
time: 161 us
  waiting for transfers between devices  71 us (44%)
  starting transfers between devices  64.5 us (40%)
  Pallas kernels  20.7 us (13%)
  between operations  1.71 us (1%)
    ppermute x24, starting transfers between devices, flipped(): return lax.ppermute(array, 'tile', [(i, i ^ mask) for i in range(peers)])  38.7 us
    ppermute x24, waiting for transfers between devices, flipped(): return lax.ppermute(array, 'tile', [(i, i ^ mask) for i in range(peers)])  35.5 us
    ppermute x12, waiting for transfers between devices, shifted(): lax.ppermute(array, 'tile', [(i, (i + by) % peers) for i in range(peers)])  31.5 us
    ppermute x12, starting transfers between devices, shifted(): lax.ppermute(array, 'tile', [(i, (i + by) % peers) for i in range(peers)])  21.6 us
    pallas_call x20, Pallas kernels, call(): pl.pallas_call(kernel, out_shape=tuple((jax.ShapeDtypeStruct(shape, dtype...  20.7 us
    ppermute x20, starting transfers between devices, swapped(): return lax.ppermute(array, 'mode', [(0, 1), (1, 0)])  4.23 us
    ppermute x20, waiting for transfers between devices, swapped(): return lax.ppermute(array, 'mode', [(0, 1), (1, 0)])  3.92 us
  transfers between devices with their start and end apart: 56, of which 26 were waited for; matrix products, arithmetic and copies ran while one was open for 1% of the time, Pallas kernels for 3%

profile of v1, /device:TPU:0, one launch (start us, length us, event | category | flops | bytes accessed | tf_op | source)
XLA Modules:
  0.0 160.6 jit_solution(9469495500925638226)
XLA Ops:
  1.3 1.3 copy-done.1
  2.7 4.9 %collective-permute-start.3 = (bf16[512,128]{1,0:T(8,128)(2,1)S(1)}, bf16[512,128]{1,0:T(8,128)(2,1)S(1)}, u32[]{:S(2)}, u32[]{:S(2)}) collective-permute-start(bf16[512,128]{1,0:T(8,128)(2,1)S(1)} %get-tuple-element.52), channel_id=1, source_target_pairs={{0,14},{2,16},{4,18},{6,20},{8,22},{10,24},{12,26},{14,28},{16,30}... | collective-permute-start | bytes 393224 | tf_op jit(solution)/shard_map/ppermute | solution.py:28
  7.6 2.3 %collective-permute-start.1 = (bf16[768,128]{1,0:T(8,128)(2,1)S(1)}, bf16[768,128]{1,0:T(8,128)(2,1)S(1)}, u32[]{:S(2)}, u32[]{:S(2)}) collective-permute-start(bf16[768,128]{1,0:T(8,128)(2,1)S(1)} %get-tuple-element.50), channel_id=1, source_target_pairs={{0,30},{2,0},{4,2},{6,4},{8,6},{10,8},{12,10},{14,12},{16,14},{18,... | collective-permute-start | bytes 589832 | tf_op jit(solution)/shard_map/ppermute | solution.py:28
  9.9 1.7 %collective-permute-start.2 = (bf16[768,128]{1,0:T(8,128)(2,1)S(1)}, bf16[768,128]{1,0:T(8,128)(2,1)S(1)}, u32[]{:S(2)}, u32[]{:S(2)}) collective-permute-start(bf16[768,128]{1,0:T(8,128)(2,1)S(1)} %get-tuple-element.51), channel_id=1, source_target_pairs={{0,16},{2,18},{4,20},{6,22},{8,24},{10,26},{12,28},{14,30},{16,0},... | collective-permute-start | bytes 589832 | tf_op jit(solution)/shard_map/ppermute | solution.py:28
  12.9 6.2 %collective-permute-done.3.dm = bf16[512,128]{1,0:T(8,128)(2,1)S(1)} collective-permute-done((bf16[512,128]{1,0:T(8,128)(2,1)S(1)}, bf16[512,128]{1,0:T(8,128)(2,1)S(1)}, u32[]{:S(2)}, u32[]{:S(2)}) %collective-permute-start.3) | collective-permute-done | bytes 131104 | tf_op jit(solution)/shard_map/ppermute | solution.py:28
  19.5 6.4 %collective-permute-done.2.bm = bf16[768,128]{1,0:T(8,128)(2,1)S(1)} collective-permute-done((bf16[768,128]{1,0:T(8,128)(2,1)S(1)}, bf16[768,128]{1,0:T(8,128)(2,1)S(1)}, u32[]{:S(2)}, u32[]{:S(2)}) %collective-permute-start.2) | collective-permute-done | bytes 196640 | tf_op jit(solution)/shard_map/ppermute | solution.py:28
  26.8 0.9 kernel.21.meas
  27.8 7.7 %kernel.22 = (f32[384,384]{1,0:T(8,128)S(1)}, bf16[384,384]{1,0:T(8,128)(2,1)S(1)}, f32[2048,128]{1,0:T(8,128)S(1)}, bf16[2048,128]{1,0:T(8,128)(2,1)S(1)}, f32[...) custom-call(s32[1]{0:T(128)S(6)} %copy.9.live, s32[2,4]{1,0:T(2,128)S(1)} %bitcast.30, s32[4]{0:T(128)S(1)} %copy-done.5, ...), custom_call_target="tpu_custom_call" | custom-call | tf_op jit(solution)/shard_map/kernel/pallas_call | solution.py:211
  36.1 1.5 collective-permute-done.20
  38.2 3.1 %collective-permute-start.23 = (bf16[256,256]{1,0:T(8,128)(2,1)S(1)}, bf16[256,256]{1,0:T(8,128)(2,1)S(1)}, u32[]{:S(2)}, u32[]{:S(2)}) collective-permute-start(bf16[256,256]{1,0:T(8,128)(2,1)S(1)} %get-tuple-element.71), channel_id=1, source_target_pairs={{0,6},{2,4},{4,2},{6,0},{8,14},{10,12},{12,10},{14,8},{16,22},{18,... | collective-permute-start | bytes 393224 | tf_op jit(solution)/shard_map/ppermute | solution.py:33
  41.8 2.3 %collective-permute-done.21.refs_0_ = bf16[256,256]{1,0:T(8,128)(2,1)S(1)} collective-permute-done((bf16[256,256]{1,0:T(8,128)(2,1)S(1)}, bf16[256,256]{1,0:T(8,128)(2,1)S(1)}, u32[]{:S(2)}, u32[]{:S(2)}) %collective-permute-start.21) | collective-permute-done | bytes 131104 | tf_op jit(solution)/shard_map/ppermute | solution.py:33
  44.1 2.4 %collective-permute-done.22.refs_1_ = bf16[256,256]{1,0:T(8,128)(2,1)S(1)} collective-permute-done((bf16[256,256]{1,0:T(8,128)(2,1)S(1)}, bf16[256,256]{1,0:T(8,128)(2,1)S(1)}, u32[]{:S(2)}, u32[]{:S(2)}) %collective-permute-start.22) | collective-permute-done | bytes 131104 | tf_op jit(solution)/shard_map/ppermute | solution.py:33
  46.6 2.5 %collective-permute-start.24 = (bf16[64,256]{1,0:T(8,128)(2,1)S(1)}, bf16[64,256]{1,0:T(8,128)(2,1)S(1)}, u32[]{:S(2)}, u32[]{:S(2)}) collective-permute-start(bf16[64,256]{1,0:T(8,128)(2,1)S(1)} %get-tuple-element.73), channel_id=1, source_target_pairs={{0,8},{2,10},{4,12},{6,14},{8,0},{10,2},{12,4},{14,6},{16,24},{18,... | collective-permute-start | bytes 98312 | tf_op jit(solution)/shard_map/ppermute | solution.py:33
  49.1 2.6 %collective-permute-done.24.refs_0_ = bf16[64,256]{1,0:T(8,128)(2,1)S(1)} collective-permute-done((bf16[64,256]{1,0:T(8,128)(2,1)S(1)}, bf16[64,256]{1,0:T(8,128)(2,1)S(1)}, u32[]{:S(2)}, u32[]{:S(2)}) %collective-permute-start.24) | collective-permute-done | bytes 32800 | tf_op jit(solution)/shard_map/ppermute | solution.py:33
  51.7 3.2 %collective-permute-start.25 = (bf16[64,256]{1,0:T(8,128)(2,1)S(1)}, bf16[64,256]{1,0:T(8,128)(2,1)S(1)}, u32[]{:S(2)}, u32[]{:S(2)}) collective-permute-start(bf16[64,256]{1,0:T(8,128)(2,1)S(1)} %get-tuple-element.74), channel_id=1, source_target_pairs={{0,16},{2,18},{4,20},{6,22},{8,24},{10,26},{12,28},{14,30},{16,0},... | collective-permute-start | bytes 98312 | tf_op jit(solution)/shard_map/ppermute | solution.py:33
  54.9 2.7 %collective-permute-done.25.refs_1_ = bf16[64,256]{1,0:T(8,128)(2,1)S(1)} collective-permute-done((bf16[64,256]{1,0:T(8,128)(2,1)S(1)}, bf16[64,256]{1,0:T(8,128)(2,1)S(1)}, u32[]{:S(2)}, u32[]{:S(2)}) %collective-permute-start.25) | collective-permute-done | bytes 32800 | tf_op jit(solution)/shard_map/ppermute | solution.py:33
  57.6 2.6 %collective-permute-start.26 = (bf16[64,256]{1,0:T(8,128)(2,1)S(1)}, bf16[64,256]{1,0:T(8,128)(2,1)S(1)}, u32[]{:S(2)}, u32[]{:S(2)}) collective-permute-start(bf16[64,256]{1,0:T(8,128)(2,1)S(1)} %get-tuple-element.75), channel_id=1, source_target_pairs={{0,24},{2,26},{4,28},{6,30},{8,16},{10,18},{12,20},{14,22},{16,8},... | collective-permute-start | bytes 98312 | tf_op jit(solution)/shard_map/ppermute | solution.py:33
  60.2 3.1 %collective-permute-done.26.refs_2_ = bf16[64,256]{1,0:T(8,128)(2,1)S(1)} collective-permute-done((bf16[64,256]{1,0:T(8,128)(2,1)S(1)}, bf16[64,256]{1,0:T(8,128)(2,1)S(1)}, u32[]{:S(2)}, u32[]{:S(2)}) %collective-permute-start.26) | collective-permute-done | bytes 32800 | tf_op jit(solution)/shard_map/ppermute | solution.py:33
  63.3 2.7 %collective-permute-start.29 = (bf16[64,256]{1,0:T(8,128)(2,1)S(1)}, bf16[64,256]{1,0:T(8,128)(2,1)S(1)}, u32[]{:S(2)}, u32[]{:S(2)}) collective-permute-start(bf16[64,256]{1,0:T(8,128)(2,1)S(1)} %kernel.27.have), channel_id=1, source_target_pairs={{0,24},{2,26},{4,28},{6,30},{8,16},{10,18},{12,20},{14,22},{16,8},... | collective-permute-start | bytes 98312 | tf_op jit(solution)/shard_map/ppermute | solution.py:33
  66.0 1.8 %collective-permute-start.27 = (bf16[64,256]{1,0:T(8,128)(2,1)S(1)}, bf16[64,256]{1,0:T(8,128)(2,1)S(1)}, u32[]{:S(2)}, u32[]{:S(2)}) collective-permute-start(bf16[64,256]{1,0:T(8,128)(2,1)S(1)} %kernel.27.have), channel_id=1, source_target_pairs={{0,8},{2,10},{4,12},{6,14},{8,0},{10,2},{12,4},{14,6},{16,24},{18,... | collective-permute-start | bytes 98312 | tf_op jit(solution)/shard_map/ppermute | solution.py:33
  68.1 6.7 %collective-permute-start.15 = (bf16[512,128]{1,0:T(8,128)(2,1)S(1)}, bf16[512,128]{1,0:T(8,128)(2,1)S(1)}, u32[]{:S(2)}, u32[]{:S(2)}) collective-permute-start(bf16[512,128]{1,0:T(8,128)(2,1)S(1)} %get-tuple-element.65), channel_id=1, source_target_pairs={{0,14},{2,16},{4,18},{6,20},{8,22},{10,24},{12,26},{14,28},{16,30}... | collective-permute-start | bytes 393224 | tf_op jit(solution)/shard_map/ppermute | solution.py:28
  74.9 3.0 %collective-permute-start.32 = (bf16[256,256]{1,0:T(8,128)(2,1)S(1)}, bf16[256,256]{1,0:T(8,128)(2,1)S(1)}, u32[]{:S(2)}, u32[]{:S(2)}) collective-permute-start(bf16[256,256]{1,0:T(8,128)(2,1)S(1)} %kernel.28.have), channel_id=1, source_target_pairs={{0,6},{2,4},{4,2},{6,0},{8,14},{10,12},{12,10},{14,8},{16,22},{18,... | collective-permute-start | bytes 393224 | tf_op jit(solution)/shard_map/ppermute | solution.py:33
  78.6 5.4 %collective-permute-start.13 = (bf16[768,128]{1,0:T(8,128)(2,1)S(1)}, bf16[768,128]{1,0:T(8,128)(2,1)S(1)}, u32[]{:S(2)}, u32[]{:S(2)}) collective-permute-start(bf16[768,128]{1,0:T(8,128)(2,1)S(1)} %get-tuple-element.63), channel_id=1, source_target_pairs={{0,30},{2,0},{4,2},{6,4},{8,6},{10,8},{12,10},{14,12},{16,14},{18,... | collective-permute-start | bytes 589832 | tf_op jit(solution)/shard_map/ppermute | solution.py:28
  84.8 4.2 %collective-permute-done.30.refs_0_ = bf16[256,256]{1,0:T(8,128)(2,1)S(1)} collective-permute-done((bf16[256,256]{1,0:T(8,128)(2,1)S(1)}, bf16[256,256]{1,0:T(8,128)(2,1)S(1)}, u32[]{:S(2)}, u32[]{:S(2)}) %collective-permute-start.30) | collective-permute-done | bytes 131104 | tf_op jit(solution)/shard_map/ppermute | solution.py:33
  89.5 5.6 %collective-permute-done.14.bm = bf16[768,128]{1,0:T(8,128)(2,1)S(1)} collective-permute-done((bf16[768,128]{1,0:T(8,128)(2,1)S(1)}, bf16[768,128]{1,0:T(8,128)(2,1)S(1)}, u32[]{:S(2)}, u32[]{:S(2)}) %collective-permute-start.14) | collective-permute-done | bytes 196640 | tf_op jit(solution)/shard_map/ppermute | solution.py:28
  95.8 0.9 collective-permute-done.34.refs_0_
  97.0 7.7 %kernel.31 = (f32[384,384]{1,0:T(8,128)S(1)}, bf16[384,384]{1,0:T(8,128)(2,1)S(1)}, f32[2048,128]{1,0:T(8,128)S(1)}, bf16[2048,128]{1,0:T(8,128)(2,1)S(1)}, f32[...) custom-call(s32[1]{0:T(128)S(6)} %copy.9.live, s32[2,4]{1,0:T(2,128)S(1)} %bitcast.31, s32[4]{0:T(128)S(1)} %copy-done.5, ...), custom_call_target="tpu_custom_call" | custom-call | tf_op jit(solution)/shard_map/kernel/pallas_call | solution.py:211
  105.4 1.2 collective-permute-done.38.got
  107.1 13.2 %collective-permute-done.41.diag = bf16[512,128]{1,0:T(8,128)(2,1)S(1)} collective-permute-done((bf16[512,128]{1,0:T(8,128)(2,1)S(1)}, bf16[512,128]{1,0:T(8,128)(2,1)S(1)}, u32[]{:S(2)}, u32[]{:S(2)}) %collective-permute-start.41) | collective-permute-done | bytes 131104 | tf_op jit(solution)/shard_map/ppermute | solution.py:28
  120.3 1.1 kernel.33
  121.5 4.1 %collective-permute-start.44 = (bf16[256,256]{1,0:T(8,128)(2,1)S(1)}, bf16[256,256]{1,0:T(8,128)(2,1)S(1)}, u32[]{:S(2)}, u32[]{:S(2)}) collective-permute-start(bf16[256,256]{1,0:T(8,128)(2,1)S(1)} %get-tuple-element.87), channel_id=1, source_target_pairs={{0,2},{2,0},{4,6},{6,4},{8,10},{10,8},{12,14},{14,12},{16,18},{18,... | collective-permute-start | bytes 393224 | tf_op jit(solution)/shard_map/ppermute | solution.py:33
  125.7 1.1 collective-permute-start.45
  127.2 2.8 %collective-permute-done.44.refs_0_ = bf16[256,256]{1,0:T(8,128)(2,1)S(1)} collective-permute-done((bf16[256,256]{1,0:T(8,128)(2,1)S(1)}, bf16[256,256]{1,0:T(8,128)(2,1)S(1)}, u32[]{:S(2)}, u32[]{:S(2)}) %collective-permute-start.44) | collective-permute-done | bytes 131104 | tf_op jit(solution)/shard_map/ppermute | solution.py:33
  130.0 4.1 %collective-permute-done.45.refs_1_ = bf16[256,256]{1,0:T(8,128)(2,1)S(1)} collective-permute-done((bf16[256,256]{1,0:T(8,128)(2,1)S(1)}, bf16[256,256]{1,0:T(8,128)(2,1)S(1)}, u32[]{:S(2)}, u32[]{:S(2)}) %collective-permute-start.45) | collective-permute-done | bytes 131104 | tf_op jit(solution)/shard_map/ppermute | solution.py:33
  134.1 3.0 %collective-permute-start.47 = (bf16[64,256]{1,0:T(8,128)(2,1)S(1)}, bf16[64,256]{1,0:T(8,128)(2,1)S(1)}, u32[]{:S(2)}, u32[]{:S(2)}) collective-permute-start(bf16[64,256]{1,0:T(8,128)(2,1)S(1)} %get-tuple-element.91), channel_id=1, source_target_pairs={{0,8},{2,10},{4,12},{6,14},{8,0},{10,2},{12,4},{14,6},{16,24},{18,... | collective-permute-start | bytes 98312 | tf_op jit(solution)/shard_map/ppermute | solution.py:33
  137.4 2.1 %collective-permute-start.49 = (bf16[64,256]{1,0:T(8,128)(2,1)S(1)}, bf16[64,256]{1,0:T(8,128)(2,1)S(1)}, u32[]{:S(2)}, u32[]{:S(2)}) collective-permute-start(bf16[64,256]{1,0:T(8,128)(2,1)S(1)} %get-tuple-element.93), channel_id=1, source_target_pairs={{0,24},{2,26},{4,28},{6,30},{8,16},{10,18},{12,20},{14,22},{16,8},... | collective-permute-start | bytes 98312 | tf_op jit(solution)/shard_map/ppermute | solution.py:33
  139.6 2.4 %collective-permute-done.48.refs_1_ = bf16[64,256]{1,0:T(8,128)(2,1)S(1)} collective-permute-done((bf16[64,256]{1,0:T(8,128)(2,1)S(1)}, bf16[64,256]{1,0:T(8,128)(2,1)S(1)}, u32[]{:S(2)}, u32[]{:S(2)}) %collective-permute-start.48) | collective-permute-done | bytes 32800 | tf_op jit(solution)/shard_map/ppermute | solution.py:33
  141.9 1.2 collective-permute-done.49.refs_2_
  143.2 2.2 %collective-permute-start.52 = (bf16[64,256]{1,0:T(8,128)(2,1)S(1)}, bf16[64,256]{1,0:T(8,128)(2,1)S(1)}, u32[]{:S(2)}, u32[]{:S(2)}) collective-permute-start(bf16[64,256]{1,0:T(8,128)(2,1)S(1)} %kernel.37.have), channel_id=1, source_target_pairs={{0,24},{2,26},{4,28},{6,30},{8,16},{10,18},{12,20},{14,22},{16,8},... | collective-permute-start | bytes 98312 | tf_op jit(solution)/shard_map/ppermute | solution.py:33
  145.4 2.2 %collective-permute-start.50 = (bf16[64,256]{1,0:T(8,128)(2,1)S(1)}, bf16[64,256]{1,0:T(8,128)(2,1)S(1)}, u32[]{:S(2)}, u32[]{:S(2)}) collective-permute-start(bf16[64,256]{1,0:T(8,128)(2,1)S(1)} %kernel.37.have), channel_id=1, source_target_pairs={{0,8},{2,10},{4,12},{6,14},{8,0},{10,2},{12,4},{14,6},{16,24},{18,... | collective-permute-start | bytes 98312 | tf_op jit(solution)/shard_map/ppermute | solution.py:33
  147.6 1.3 collective-permute-done.52.refs_2_
  148.9 1.2 collective-permute-done.51.refs_1_
  150.2 1.6 collective-permute-start.55
  151.8 1.6 %collective-permute-start.54 = (bf16[256,256]{1,0:T(8,128)(2,1)S(1)}, bf16[256,256]{1,0:T(8,128)(2,1)S(1)}, u32[]{:S(2)}, u32[]{:S(2)}) collective-permute-start(bf16[256,256]{1,0:T(8,128)(2,1)S(1)} %kernel.38.have), channel_id=1, source_target_pairs={{0,4},{2,6},{4,0},{6,2},{8,12},{10,14},{12,8},{14,10},{16,20},{18,... | collective-permute-start | bytes 393224 | tf_op jit(solution)/shard_map/ppermute | solution.py:33
  153.8 2.5 %collective-permute-done.55.refs_2_ = bf16[256,256]{1,0:T(8,128)(2,1)S(1)} collective-permute-done((bf16[256,256]{1,0:T(8,128)(2,1)S(1)}, bf16[256,256]{1,0:T(8,128)(2,1)S(1)}, u32[]{:S(2)}, u32[]{:S(2)}) %collective-permute-start.55) | collective-permute-done | bytes 131104 | tf_op jit(solution)/shard_map/ppermute | solution.py:33
  156.2 1.3 collective-permute-done.54.refs_1_
  158.4 1.1 kernel.39
  159.5 1.1 kernel.34
  (104 shorter events, 11.1 us)
Async XLA Ops:
  0.6 27.1 %collective-permute-start = (f32[2,8]{1,0:T(2,128)}, f32[2,8]{1,0:T(2,128)S(1)}, u32[]{:S(2)}, u32[]{:S(2)}) collective-permute-start(f32[2,8]{1,0:T(2,128)} %bitcast.32), channel_id=1, source_target_pairs={{0,1},{1,0},{2,3},{3,2},{4,5},{5,4},{6,7},{7,6},{8,9},{9,8},{10,11... | collective-permute-start | bytes 200 | tf_op jit(solution)/shard_map/ppermute | solution.py:37
  1.2 26.5 %collective-permute-start.7 = (f32[2,2,256,256]{3,2,1,0:T(8,128)}, f32[2,2,256,256]{3,2,1,0:T(8,128)S(1)}, u32[]{:S(2)}, u32[]{:S(2)}) collective-permute-start(f32[2,2,256,256]{3,2,1,0:T(8,128)} %pm.1), channel_id=1, source_target_pairs={{0,1},{1,0},{2,3},{3,2},{4,5},{5,4},{6,7},{7,6},{8,9},{9,8},{10,11... | collective-permute-start | bytes 3145736 | tf_op jit(solution)/shard_map/ppermute | solution.py:37
  2.7 16.4 %collective-permute-start.3 = (bf16[512,128]{1,0:T(8,128)(2,1)S(1)}, bf16[512,128]{1,0:T(8,128)(2,1)S(1)}, u32[]{:S(2)}, u32[]{:S(2)}) collective-permute-start(bf16[512,128]{1,0:T(8,128)(2,1)S(1)} %get-tuple-element.52), channel_id=1, source_target_pairs={{0,14},{2,16},{4,18},{6,20},{8,22},{10,24},{12,26},{14,28},{16,30}... | collective-permute-start | bytes 393224 | tf_op jit(solution)/shard_map/ppermute | solution.py:28
  7.6 11.4 %collective-permute-start.1 = (bf16[768,128]{1,0:T(8,128)(2,1)S(1)}, bf16[768,128]{1,0:T(8,128)(2,1)S(1)}, u32[]{:S(2)}, u32[]{:S(2)}) collective-permute-start(bf16[768,128]{1,0:T(8,128)(2,1)S(1)} %get-tuple-element.50), channel_id=1, source_target_pairs={{0,30},{2,0},{4,2},{6,4},{8,6},{10,8},{12,10},{14,12},{16,14},{18,... | collective-permute-start | bytes 589832 | tf_op jit(solution)/shard_map/ppermute | solution.py:28
  9.9 16.0 %collective-permute-start.2 = (bf16[768,128]{1,0:T(8,128)(2,1)S(1)}, bf16[768,128]{1,0:T(8,128)(2,1)S(1)}, u32[]{:S(2)}, u32[]{:S(2)}) collective-permute-start(bf16[768,128]{1,0:T(8,128)(2,1)S(1)} %get-tuple-element.51), channel_id=1, source_target_pairs={{0,16},{2,18},{4,20},{6,22},{8,24},{10,26},{12,28},{14,30},{16,0},... | collective-permute-start | bytes 589832 | tf_op jit(solution)/shard_map/ppermute | solution.py:28
  19.0 8.7 %collective-permute-start.6 = (bf16[512,128]{1,0:T(8,128)(2,1)S(1)}, bf16[512,128]{1,0:T(8,128)(2,1)S(1)}, u32[]{:S(2)}, u32[]{:S(2)}) collective-permute-start(bf16[512,128]{1,0:T(8,128)(2,1)S(1)} %collective-permute-done.3.dm), channel_id=1, source_target_pairs={{0,1},{1,0},{2,3},{3,2},{4,5},{5,4},{6,7},{7,6},{8,9},{9,8},{10,11... | collective-permute-start | bytes 393224 | tf_op jit(solution)/shard_map/ppermute | solution.py:37
  19.0 8.7 %collective-permute-start.4 = (bf16[768,128]{1,0:T(8,128)(2,1)S(1)}, bf16[768,128]{1,0:T(8,128)(2,1)S(1)}, u32[]{:S(2)}, u32[]{:S(2)}) collective-permute-start(bf16[768,128]{1,0:T(8,128)(2,1)S(1)} %collective-permute-done.1.rm), channel_id=1, source_target_pairs={{0,1},{1,0},{2,3},{3,2},{4,5},{5,4},{6,7},{7,6},{8,9},{9,8},{10,11... | collective-permute-start | bytes 589832 | tf_op jit(solution)/shard_map/ppermute | solution.py:37
  36.0 5.3 %collective-permute-start.9 = (bf16[2048,128]{1,0:T(8,128)(2,1)S(1)}, bf16[2048,128]{1,0:T(8,128)(2,1)S(1)}, u32[]{:S(2)}, u32[]{:S(2)}) collective-permute-start(bf16[2048,128]{1,0:T(8,128)(2,1)S(1)} %get-tuple-element.57), channel_id=1, source_target_pairs={{0,1},{1,0},{2,3},{3,2},{4,5},{5,4},{6,7},{7,6},{8,9},{9,8},{10,11... | collective-permute-start | bytes 1572872 | tf_op jit(solution)/shard_map/ppermute | solution.py:37
  37.6 6.4 %collective-permute-start.21 = (bf16[256,256]{1,0:T(8,128)(2,1)S(1)}, bf16[256,256]{1,0:T(8,128)(2,1)S(1)}, u32[]{:S(2)}, u32[]{:S(2)}) collective-permute-start(bf16[256,256]{1,0:T(8,128)(2,1)S(1)} %get-tuple-element.69), channel_id=1, source_target_pairs={{0,2},{2,0},{4,6},{6,4},{8,10},{10,8},{12,14},{14,12},{16,18},{18,... | collective-permute-start | bytes 393224 | tf_op jit(solution)/shard_map/ppermute | solution.py:33
  37.7 28.3 %collective-permute-start.8 = (bf16[384,384]{1,0:T(8,128)(2,1)S(1)}, bf16[384,384]{1,0:T(8,128)(2,1)S(1)}, u32[]{:S(2)}, u32[]{:S(2)}) collective-permute-start(bf16[384,384]{1,0:T(8,128)(2,1)S(1)} %get-tuple-element.55), channel_id=1, source_target_pairs={{0,1},{1,0},{2,3},{3,2},{4,5},{5,4},{6,7},{7,6},{8,9},{9,8},{10,11... | collective-permute-start | bytes 884744 | tf_op jit(solution)/shard_map/ppermute | solution.py:37
  38.2 8.3 %collective-permute-start.22 = (bf16[256,256]{1,0:T(8,128)(2,1)S(1)}, bf16[256,256]{1,0:T(8,128)(2,1)S(1)}, u32[]{:S(2)}, u32[]{:S(2)}) collective-permute-start(bf16[256,256]{1,0:T(8,128)(2,1)S(1)} %get-tuple-element.70), channel_id=1, source_target_pairs={{0,4},{2,6},{4,0},{6,2},{8,12},{10,14},{12,8},{14,10},{16,20},{18,... | collective-permute-start | bytes 393224 | tf_op jit(solution)/shard_map/ppermute | solution.py:33
  38.2 8.4 %collective-permute-start.23 = (bf16[256,256]{1,0:T(8,128)(2,1)S(1)}, bf16[256,256]{1,0:T(8,128)(2,1)S(1)}, u32[]{:S(2)}, u32[]{:S(2)}) collective-permute-start(bf16[256,256]{1,0:T(8,128)(2,1)S(1)} %get-tuple-element.71), channel_id=1, source_target_pairs={{0,6},{2,4},{4,2},{6,0},{8,14},{10,12},{12,10},{14,8},{16,22},{18,... | collective-permute-start | bytes 393224 | tf_op jit(solution)/shard_map/ppermute | solution.py:33
  41.4 26.4 %collective-permute-start.10 = (bf16[768,128]{1,0:T(8,128)(2,1)S(1)}, bf16[768,128]{1,0:T(8,128)(2,1)S(1)}, u32[]{:S(2)}, u32[]{:S(2)}) collective-permute-start(bf16[768,128]{1,0:T(8,128)(2,1)S(1)} %get-tuple-element.58), channel_id=1, source_target_pairs={{0,2},{2,4},{4,6},{6,8},{8,10},{10,12},{12,14},{14,16},{16,18},{18... | collective-permute-start | bytes 589832 | tf_op jit(solution)/shard_map/ppermute | solution.py:28
  44.1 23.7 %collective-permute-start.11 = (bf16[768,128]{1,0:T(8,128)(2,1)S(1)}, bf16[768,128]{1,0:T(8,128)(2,1)S(1)}, u32[]{:S(2)}, u32[]{:S(2)}) collective-permute-start(bf16[768,128]{1,0:T(8,128)(2,1)S(1)} %get-tuple-element.59), channel_id=1, source_target_pairs={{0,16},{2,18},{4,20},{6,22},{8,24},{10,26},{12,28},{14,30},{16,0},... | collective-permute-start | bytes 589832 | tf_op jit(solution)/shard_map/ppermute | solution.py:28
  46.5 19.5 %collective-permute-start.12 = (bf16[512,128]{1,0:T(8,128)(2,1)S(1)}, bf16[512,128]{1,0:T(8,128)(2,1)S(1)}, u32[]{:S(2)}, u32[]{:S(2)}) collective-permute-start(bf16[512,128]{1,0:T(8,128)(2,1)S(1)} %get-tuple-element.60), channel_id=1, source_target_pairs={{0,18},{2,20},{4,22},{6,24},{8,26},{10,28},{12,30},{14,0},{16,2},{... | collective-permute-start | bytes 393224 | tf_op jit(solution)/shard_map/ppermute | solution.py:28
  46.6 5.1 %collective-permute-start.24 = (bf16[64,256]{1,0:T(8,128)(2,1)S(1)}, bf16[64,256]{1,0:T(8,128)(2,1)S(1)}, u32[]{:S(2)}, u32[]{:S(2)}) collective-permute-start(bf16[64,256]{1,0:T(8,128)(2,1)S(1)} %get-tuple-element.73), channel_id=1, source_target_pairs={{0,8},{2,10},{4,12},{6,14},{8,0},{10,2},{12,4},{14,6},{16,24},{18,... | collective-permute-start | bytes 98312 | tf_op jit(solution)/shard_map/ppermute | solution.py:33
  51.7 5.9 %collective-permute-start.25 = (bf16[64,256]{1,0:T(8,128)(2,1)S(1)}, bf16[64,256]{1,0:T(8,128)(2,1)S(1)}, u32[]{:S(2)}, u32[]{:S(2)}) collective-permute-start(bf16[64,256]{1,0:T(8,128)(2,1)S(1)} %get-tuple-element.74), channel_id=1, source_target_pairs={{0,16},{2,18},{4,20},{6,22},{8,24},{10,26},{12,28},{14,30},{16,0},... | collective-permute-start | bytes 98312 | tf_op jit(solution)/shard_map/ppermute | solution.py:33
  57.6 5.7 %collective-permute-start.26 = (bf16[64,256]{1,0:T(8,128)(2,1)S(1)}, bf16[64,256]{1,0:T(8,128)(2,1)S(1)}, u32[]{:S(2)}, u32[]{:S(2)}) collective-permute-start(bf16[64,256]{1,0:T(8,128)(2,1)S(1)} %get-tuple-element.75), channel_id=1, source_target_pairs={{0,24},{2,26},{4,28},{6,30},{8,16},{10,18},{12,20},{14,22},{16,8},... | collective-permute-start | bytes 98312 | tf_op jit(solution)/shard_map/ppermute | solution.py:33
  63.3 11.5 %collective-permute-start.29 = (bf16[64,256]{1,0:T(8,128)(2,1)S(1)}, bf16[64,256]{1,0:T(8,128)(2,1)S(1)}, u32[]{:S(2)}, u32[]{:S(2)}) collective-permute-start(bf16[64,256]{1,0:T(8,128)(2,1)S(1)} %kernel.27.have), channel_id=1, source_target_pairs={{0,24},{2,26},{4,28},{6,30},{8,16},{10,18},{12,20},{14,22},{16,8},... | collective-permute-start | bytes 98312 | tf_op jit(solution)/shard_map/ppermute | solution.py:33
  66.0 8.8 %collective-permute-start.28 = (bf16[64,256]{1,0:T(8,128)(2,1)S(1)}, bf16[64,256]{1,0:T(8,128)(2,1)S(1)}, u32[]{:S(2)}, u32[]{:S(2)}) collective-permute-start(bf16[64,256]{1,0:T(8,128)(2,1)S(1)} %kernel.27.have), channel_id=1, source_target_pairs={{0,16},{2,18},{4,20},{6,22},{8,24},{10,26},{12,28},{14,30},{16,0},... | collective-permute-start | bytes 98312 | tf_op jit(solution)/shard_map/ppermute | solution.py:33
  66.0 8.8 %collective-permute-start.27 = (bf16[64,256]{1,0:T(8,128)(2,1)S(1)}, bf16[64,256]{1,0:T(8,128)(2,1)S(1)}, u32[]{:S(2)}, u32[]{:S(2)}) collective-permute-start(bf16[64,256]{1,0:T(8,128)(2,1)S(1)} %kernel.27.have), channel_id=1, source_target_pairs={{0,8},{2,10},{4,12},{6,14},{8,0},{10,2},{12,4},{14,6},{16,24},{18,... | collective-permute-start | bytes 98312 | tf_op jit(solution)/shard_map/ppermute | solution.py:33
  68.1 10.5 %collective-permute-start.15 = (bf16[512,128]{1,0:T(8,128)(2,1)S(1)}, bf16[512,128]{1,0:T(8,128)(2,1)S(1)}, u32[]{:S(2)}, u32[]{:S(2)}) collective-permute-start(bf16[512,128]{1,0:T(8,128)(2,1)S(1)} %get-tuple-element.65), channel_id=1, source_target_pairs={{0,14},{2,16},{4,18},{6,20},{8,22},{10,24},{12,26},{14,28},{16,30}... | collective-permute-start | bytes 393224 | tf_op jit(solution)/shard_map/ppermute | solution.py:28
  74.8 9.2 %collective-permute-start.33 = (bf16[256,256]{1,0:T(8,128)(2,1)S(1)}, bf16[256,256]{1,0:T(8,128)(2,1)S(1)}, u32[]{:S(2)}, u32[]{:S(2)}) collective-permute-start(bf16[256,256]{1,0:T(8,128)(2,1)S(1)} %kernel.28.have), channel_id=1, source_target_pairs={{0,1},{1,0},{2,3},{3,2},{4,5},{5,4},{6,7},{7,6},{8,9},{9,8},{10,11... | collective-permute-start | bytes 393224 | tf_op jit(solution)/shard_map/ppermute | solution.py:37
  74.9 9.1 %collective-permute-start.32 = (bf16[256,256]{1,0:T(8,128)(2,1)S(1)}, bf16[256,256]{1,0:T(8,128)(2,1)S(1)}, u32[]{:S(2)}, u32[]{:S(2)}) collective-permute-start(bf16[256,256]{1,0:T(8,128)(2,1)S(1)} %kernel.28.have), channel_id=1, source_target_pairs={{0,6},{2,4},{4,2},{6,0},{8,14},{10,12},{12,10},{14,8},{16,22},{18,... | collective-permute-start | bytes 393224 | tf_op jit(solution)/shard_map/ppermute | solution.py:33
  77.9 6.9 %collective-permute-start.31 = (bf16[256,256]{1,0:T(8,128)(2,1)S(1)}, bf16[256,256]{1,0:T(8,128)(2,1)S(1)}, u32[]{:S(2)}, u32[]{:S(2)}) collective-permute-start(bf16[256,256]{1,0:T(8,128)(2,1)S(1)} %kernel.28.have), channel_id=1, source_target_pairs={{0,4},{2,6},{4,0},{6,2},{8,12},{10,14},{12,8},{14,10},{16,20},{18,... | collective-permute-start | bytes 393224 | tf_op jit(solution)/shard_map/ppermute | solution.py:33
  77.9 11.1 %collective-permute-start.30 = (bf16[256,256]{1,0:T(8,128)(2,1)S(1)}, bf16[256,256]{1,0:T(8,128)(2,1)S(1)}, u32[]{:S(2)}, u32[]{:S(2)}) collective-permute-start(bf16[256,256]{1,0:T(8,128)(2,1)S(1)} %kernel.28.have), channel_id=1, source_target_pairs={{0,2},{2,0},{4,6},{6,4},{8,10},{10,8},{12,14},{14,12},{16,18},{18,... | collective-permute-start | bytes 393224 | tf_op jit(solution)/shard_map/ppermute | solution.py:33
  78.6 10.4 %collective-permute-start.13 = (bf16[768,128]{1,0:T(8,128)(2,1)S(1)}, bf16[768,128]{1,0:T(8,128)(2,1)S(1)}, u32[]{:S(2)}, u32[]{:S(2)}) collective-permute-start(bf16[768,128]{1,0:T(8,128)(2,1)S(1)} %get-tuple-element.63), channel_id=1, source_target_pairs={{0,30},{2,0},{4,2},{6,4},{8,6},{10,8},{12,10},{14,12},{16,14},{18,... | collective-permute-start | bytes 589832 | tf_op jit(solution)/shard_map/ppermute | solution.py:28
  84.0 11.1 %collective-permute-start.14 = (bf16[768,128]{1,0:T(8,128)(2,1)S(1)}, bf16[768,128]{1,0:T(8,128)(2,1)S(1)}, u32[]{:S(2)}, u32[]{:S(2)}) collective-permute-start(bf16[768,128]{1,0:T(8,128)(2,1)S(1)} %get-tuple-element.64), channel_id=1, source_target_pairs={{0,16},{2,18},{4,20},{6,22},{8,24},{10,26},{12,28},{14,30},{16,0},... | collective-permute-start | bytes 589832 | tf_op jit(solution)/shard_map/ppermute | solution.py:28
  84.0 13.0 %collective-permute-start.16 = (bf16[384,384]{1,0:T(8,128)(2,1)S(1)}, bf16[384,384]{1,0:T(8,128)(2,1)S(1)}, u32[]{:S(2)}, u32[]{:S(2)}) collective-permute-start(bf16[384,384]{1,0:T(8,128)(2,1)S(1)} %get-tuple-element.62.tm), channel_id=1, source_target_pairs={{0,1},{1,0},{2,3},{3,2},{4,5},{5,4},{6,7},{7,6},{8,9},{9,8},{10,11... | collective-permute-start | bytes 884744 | tf_op jit(solution)/shard_map/ppermute | solution.py:37
  84.8 10.4 %collective-permute-start.36 = (bf16[256,256]{1,0:T(8,128)(2,1)S(1)}, bf16[256,256]{1,0:T(8,128)(2,1)S(1)}, u32[]{:S(2)}, u32[]{:S(2)}) collective-permute-start(bf16[256,256]{1,0:T(8,128)(2,1)S(1)} %collective-permute-done.32.refs_2_), channel_id=1, source_target_pairs={{0,1},{1,0},{2,3},{3,2},{4,5},{5,4},{6,7},{7,6},{8,9},{9,8},{10,11... | collective-permute-start | bytes 393224 | tf_op jit(solution)/shard_map/ppermute | solution.py:37
  89.0 6.7 %collective-permute-start.35 = (bf16[256,256]{1,0:T(8,128)(2,1)S(1)}, bf16[256,256]{1,0:T(8,128)(2,1)S(1)}, u32[]{:S(2)}, u32[]{:S(2)}) collective-permute-start(bf16[256,256]{1,0:T(8,128)(2,1)S(1)} %collective-permute-done.31.refs_1_), channel_id=1, source_target_pairs={{0,1},{1,0},{2,3},{3,2},{4,5},{5,4},{6,7},{7,6},{8,9},{9,8},{10,11... | collective-permute-start | bytes 393224 | tf_op jit(solution)/shard_map/ppermute | solution.py:37
  89.0 8.0 %collective-permute-start.17 = (bf16[768,128]{1,0:T(8,128)(2,1)S(1)}, bf16[768,128]{1,0:T(8,128)(2,1)S(1)}, u32[]{:S(2)}, u32[]{:S(2)}) collective-permute-start(bf16[768,128]{1,0:T(8,128)(2,1)S(1)} %collective-permute-done.13.rm), channel_id=1, source_target_pairs={{0,1},{1,0},{2,3},{3,2},{4,5},{5,4},{6,7},{7,6},{8,9},{9,8},{10,11... | collective-permute-start | bytes 589832 | tf_op jit(solution)/shard_map/ppermute | solution.py:37
  105.3 16.1 %collective-permute-start.43 = (bf16[2,2,256,256]{3,2,1,0:T(8,128)(2,1)S(1)}, bf16[2,2,256,256]{3,2,1,0:T(8,128)(2,1)S(1)}, u32[]{:S(2)}, u32[]{:S(2)}) collective-permute-start(bf16[2,2,256,256]{3,2,1,0:T(8,128)(2,1)S(1)} %get-tuple-element.85), channel_id=1, source_target_pairs={{0,1},{1,0},{2,3},{3,2},{4,5},{5,4},{6,7},{7,6},{8,9},{9,8},{10,11... | collective-permute-start | bytes 1572872 | tf_op jit(solution)/shard_map/ppermute | solution.py:37
  106.8 13.5 %collective-permute-start.39 = (bf16[768,128]{1,0:T(8,128)(2,1)S(1)}, bf16[768,128]{1,0:T(8,128)(2,1)S(1)}, u32[]{:S(2)}, u32[]{:S(2)}) collective-permute-start(bf16[768,128]{1,0:T(8,128)(2,1)S(1)} %get-tuple-element.80), channel_id=1, source_target_pairs={{0,2},{2,4},{4,6},{6,8},{8,10},{10,12},{12,14},{14,16},{16,18},{18... | collective-permute-start | bytes 589832 | tf_op jit(solution)/shard_map/ppermute | solution.py:28
  106.8 13.5 %collective-permute-start.40 = (bf16[768,128]{1,0:T(8,128)(2,1)S(1)}, bf16[768,128]{1,0:T(8,128)(2,1)S(1)}, u32[]{:S(2)}, u32[]{:S(2)}) collective-permute-start(bf16[768,128]{1,0:T(8,128)(2,1)S(1)} %get-tuple-element.81), channel_id=1, source_target_pairs={{0,16},{2,18},{4,20},{6,22},{8,24},{10,26},{12,28},{14,30},{16,0},... | collective-permute-start | bytes 589832 | tf_op jit(solution)/shard_map/ppermute | solution.py:28
  106.9 13.4 %collective-permute-start.41 = (bf16[512,128]{1,0:T(8,128)(2,1)S(1)}, bf16[512,128]{1,0:T(8,128)(2,1)S(1)}, u32[]{:S(2)}, u32[]{:S(2)}) collective-permute-start(bf16[512,128]{1,0:T(8,128)(2,1)S(1)} %get-tuple-element.82), channel_id=1, source_target_pairs={{0,18},{2,20},{4,22},{6,24},{8,26},{10,28},{12,30},{14,0},{16,2},{... | collective-permute-start | bytes 393224 | tf_op jit(solution)/shard_map/ppermute | solution.py:28
  121.4 38.0 %collective-permute-start.42 = (f32[384,384]{1,0:T(8,128)S(1)}, f32[384,384]{1,0:T(8,128)S(1)}, u32[]{:S(2)}, u32[]{:S(2)}) collective-permute-start(f32[384,384]{1,0:T(8,128)S(1)} %get-tuple-element.83.state), channel_id=1, source_target_pairs={{0,1},{1,0},{2,3},{3,2},{4,5},{5,4},{6,7},{7,6},{8,9},{9,8},{10,11... | collective-permute-start | bytes 1769480 | tf_op jit(solution)/shard_map/ppermute | solution.py:37
  121.5 8.4 %collective-permute-start.44 = (bf16[256,256]{1,0:T(8,128)(2,1)S(1)}, bf16[256,256]{1,0:T(8,128)(2,1)S(1)}, u32[]{:S(2)}, u32[]{:S(2)}) collective-permute-start(bf16[256,256]{1,0:T(8,128)(2,1)S(1)} %get-tuple-element.87), channel_id=1, source_target_pairs={{0,2},{2,0},{4,6},{6,4},{8,10},{10,8},{12,14},{14,12},{16,18},{18,... | collective-permute-start | bytes 393224 | tf_op jit(solution)/shard_map/ppermute | solution.py:33
  125.7 8.4 %collective-permute-start.45 = (bf16[256,256]{1,0:T(8,128)(2,1)S(1)}, bf16[256,256]{1,0:T(8,128)(2,1)S(1)}, u32[]{:S(2)}, u32[]{:S(2)}) collective-permute-start(bf16[256,256]{1,0:T(8,128)(2,1)S(1)} %get-tuple-element.88), channel_id=1, source_target_pairs={{0,4},{2,6},{4,0},{6,2},{8,12},{10,14},{12,8},{14,10},{16,20},{18,... | collective-permute-start | bytes 393224 | tf_op jit(solution)/shard_map/ppermute | solution.py:33
  126.7 7.3 %collective-permute-start.46 = (bf16[256,256]{1,0:T(8,128)(2,1)S(1)}, bf16[256,256]{1,0:T(8,128)(2,1)S(1)}, u32[]{:S(2)}, u32[]{:S(2)}) collective-permute-start(bf16[256,256]{1,0:T(8,128)(2,1)S(1)} %get-tuple-element.89), channel_id=1, source_target_pairs={{0,6},{2,4},{4,2},{6,0},{8,14},{10,12},{12,10},{14,8},{16,22},{18,... | collective-permute-start | bytes 393224 | tf_op jit(solution)/shard_map/ppermute | solution.py:33
  134.1 5.4 %collective-permute-start.47 = (bf16[64,256]{1,0:T(8,128)(2,1)S(1)}, bf16[64,256]{1,0:T(8,128)(2,1)S(1)}, u32[]{:S(2)}, u32[]{:S(2)}) collective-permute-start(bf16[64,256]{1,0:T(8,128)(2,1)S(1)} %get-tuple-element.91), channel_id=1, source_target_pairs={{0,8},{2,10},{4,12},{6,14},{8,0},{10,2},{12,4},{14,6},{16,24},{18,... | collective-permute-start | bytes 98312 | tf_op jit(solution)/shard_map/ppermute | solution.py:33
  137.1 4.8 %collective-permute-start.48 = (bf16[64,256]{1,0:T(8,128)(2,1)S(1)}, bf16[64,256]{1,0:T(8,128)(2,1)S(1)}, u32[]{:S(2)}, u32[]{:S(2)}) collective-permute-start(bf16[64,256]{1,0:T(8,128)(2,1)S(1)} %get-tuple-element.92), channel_id=1, source_target_pairs={{0,16},{2,18},{4,20},{6,22},{8,24},{10,26},{12,28},{14,30},{16,0},... | collective-permute-start | bytes 98312 | tf_op jit(solution)/shard_map/ppermute | solution.py:33
  137.4 5.7 %collective-permute-start.49 = (bf16[64,256]{1,0:T(8,128)(2,1)S(1)}, bf16[64,256]{1,0:T(8,128)(2,1)S(1)}, u32[]{:S(2)}, u32[]{:S(2)}) collective-permute-start(bf16[64,256]{1,0:T(8,128)(2,1)S(1)} %get-tuple-element.93), channel_id=1, source_target_pairs={{0,24},{2,26},{4,28},{6,30},{8,16},{10,18},{12,20},{14,22},{16,8},... | collective-permute-start | bytes 98312 | tf_op jit(solution)/shard_map/ppermute | solution.py:33
  143.2 5.8 %collective-permute-start.52 = (bf16[64,256]{1,0:T(8,128)(2,1)S(1)}, bf16[64,256]{1,0:T(8,128)(2,1)S(1)}, u32[]{:S(2)}, u32[]{:S(2)}) collective-permute-start(bf16[64,256]{1,0:T(8,128)(2,1)S(1)} %kernel.37.have), channel_id=1, source_target_pairs={{0,24},{2,26},{4,28},{6,30},{8,16},{10,18},{12,20},{14,22},{16,8},... | collective-permute-start | bytes 98312 | tf_op jit(solution)/shard_map/ppermute | solution.py:33
  145.4 4.8 %collective-permute-start.51 = (bf16[64,256]{1,0:T(8,128)(2,1)S(1)}, bf16[64,256]{1,0:T(8,128)(2,1)S(1)}, u32[]{:S(2)}, u32[]{:S(2)}) collective-permute-start(bf16[64,256]{1,0:T(8,128)(2,1)S(1)} %kernel.37.have), channel_id=1, source_target_pairs={{0,16},{2,18},{4,20},{6,22},{8,24},{10,26},{12,28},{14,30},{16,0},... | collective-permute-start | bytes 98312 | tf_op jit(solution)/shard_map/ppermute | solution.py:33
  150.2 6.0 %collective-permute-start.55 = (bf16[256,256]{1,0:T(8,128)(2,1)S(1)}, bf16[256,256]{1,0:T(8,128)(2,1)S(1)}, u32[]{:S(2)}, u32[]{:S(2)}) collective-permute-start(bf16[256,256]{1,0:T(8,128)(2,1)S(1)} %kernel.38.have), channel_id=1, source_target_pairs={{0,6},{2,4},{4,2},{6,0},{8,14},{10,12},{12,10},{14,8},{16,22},{18,... | collective-permute-start | bytes 393224 | tf_op jit(solution)/shard_map/ppermute | solution.py:33
  151.8 5.8 %collective-permute-start.54 = (bf16[256,256]{1,0:T(8,128)(2,1)S(1)}, bf16[256,256]{1,0:T(8,128)(2,1)S(1)}, u32[]{:S(2)}, u32[]{:S(2)}) collective-permute-start(bf16[256,256]{1,0:T(8,128)(2,1)S(1)} %kernel.38.have), channel_id=1, source_target_pairs={{0,4},{2,6},{4,0},{6,2},{8,12},{10,14},{12,8},{14,10},{16,20},{18,... | collective-permute-start | bytes 393224 | tf_op jit(solution)/shard_map/ppermute | solution.py:33
  153.4 5.0 %collective-permute-start.53 = (bf16[256,256]{1,0:T(8,128)(2,1)S(1)}, bf16[256,256]{1,0:T(8,128)(2,1)S(1)}, u32[]{:S(2)}, u32[]{:S(2)}) collective-permute-start(bf16[256,256]{1,0:T(8,128)(2,1)S(1)} %kernel.38.have), channel_id=1, source_target_pairs={{0,2},{2,0},{4,6},{6,4},{8,10},{10,8},{12,14},{14,12},{16,18},{18,... | collective-permute-start | bytes 393224 | tf_op jit(solution)/shard_map/ppermute | solution.py:33
  (14 other events, 41.1 us)

commit v2 on v1

--- a/solution.py
+++ b/solution.py
@@ -219,7 +219,7 @@
     )(*args)
 
 
-def sort_kernel(meas, out):
+def sort_kernel(meas, tall, wide, out):
     me = lax.axis_index("mode")
     n = out.shape[-1]
     h = n // 2
@@ -244,9 +244,9 @@
         out[g] = exact(lambda part: dot(left, part), value)
 
 
-def sort(meas):
+def sort(meas, tall, wide):
     outs = (((meas.shape[0] // 2, *meas.shape[1:]), f32),)
-    return call(sort_kernel, outs, meas)[0]
+    return call(sort_kernel, outs, meas, tall, wide)[0]
 
 
 def patches(live, corner, kind, wm, wo, mine, other, meas, pm, po, tall, wide):
@@ -473,7 +473,7 @@
     wm = mode_weights.T
     wo = swapped(wm)
     spots = corner.T
-    meas = sort(measured)
+    meas = sort(measured, tall, wide)
     for sweep in range(ITERS):
         low = shifted(edges[1], -GC)
         diag = shifted(edges[2], -(GC + 1))

time: 161 us -> 161 us (level)
  no operation moved by 1% of the time
where the time goes in v2:
time: 161 us
  waiting for transfers between devices  71 us (44%)
  starting transfers between devices  64.5 us (40%)
  Pallas kernels  20.7 us (13%)
    ppermute x24, starting transfers between devices, flipped(): return lax.ppermute(array, 'tile', [(i, i ^ mask) for i in range(peers)])  38.7 us
    ppermute x24, waiting for transfers between devices, flipped(): return lax.ppermute(array, 'tile', [(i, i ^ mask) for i in range(peers)])  35.5 us
    ppermute x12, waiting for transfers between devices, shifted(): lax.ppermute(array, 'tile', [(i, (i + by) % peers) for i in range(peers)])  31.5 us
    ppermute x12, starting transfers between devices, shifted(): lax.ppermute(array, 'tile', [(i, (i + by) % peers) for i in range(peers)])  21.6 us
    pallas_call x20, Pallas kernels, call(): pl.pallas_call(kernel, out_shape=tuple((jax.ShapeDtypeStruct(shape, dtype...  20.7 us
    ppermute x20, starting transfers between devices, swapped(): return lax.ppermute(array, 'mode', [(0, 1), (1, 0)])  4.22 us
    ppermute x20, waiting for transfers between devices, swapped(): return lax.ppermute(array, 'mode', [(0, 1), (1, 0)])  3.92 us
  transfers between devices with their start and end apart: 56, of which 26 were waited for; matrix products, arithmetic and copies ran while one was open for 1% of the time, Pallas kernels for 3%

profile of v2, /device:TPU:0, one launch (start us, length us, event | category | flops | bytes accessed | tf_op | source)
XLA Modules:
  0.0 160.7 jit_solution(8317337225284929287)
XLA Ops:
  1.3 1.3 copy-done.1
  2.7 4.9 %collective-permute-start.3 = (bf16[512,128]{1,0:T(8,128)(2,1)S(1)}, bf16[512,128]{1,0:T(8,128)(2,1)S(1)}, u32[]{:S(2)}, u32[]{:S(2)}) collective-permute-start(bf16[512,128]{1,0:T(8,128)(2,1)S(1)} %get-tuple-element.52), channel_id=1, source_target_pairs={{0,14},{2,16},{4,18},{6,20},{8,22},{10,24},{12,26},{14,28},{16,30}... | collective-permute-start | bytes 393224 | tf_op jit(solution)/shard_map/ppermute | solution.py:28
  7.6 2.3 %collective-permute-start.1 = (bf16[768,128]{1,0:T(8,128)(2,1)S(1)}, bf16[768,128]{1,0:T(8,128)(2,1)S(1)}, u32[]{:S(2)}, u32[]{:S(2)}) collective-permute-start(bf16[768,128]{1,0:T(8,128)(2,1)S(1)} %get-tuple-element.50), channel_id=1, source_target_pairs={{0,30},{2,0},{4,2},{6,4},{8,6},{10,8},{12,10},{14,12},{16,14},{18,... | collective-permute-start | bytes 589832 | tf_op jit(solution)/shard_map/ppermute | solution.py:28
  9.9 1.7 %collective-permute-start.2 = (bf16[768,128]{1,0:T(8,128)(2,1)S(1)}, bf16[768,128]{1,0:T(8,128)(2,1)S(1)}, u32[]{:S(2)}, u32[]{:S(2)}) collective-permute-start(bf16[768,128]{1,0:T(8,128)(2,1)S(1)} %get-tuple-element.51), channel_id=1, source_target_pairs={{0,16},{2,18},{4,20},{6,22},{8,24},{10,26},{12,28},{14,30},{16,0},... | collective-permute-start | bytes 589832 | tf_op jit(solution)/shard_map/ppermute | solution.py:28
  12.9 6.2 %collective-permute-done.3.dm = bf16[512,128]{1,0:T(8,128)(2,1)S(1)} collective-permute-done((bf16[512,128]{1,0:T(8,128)(2,1)S(1)}, bf16[512,128]{1,0:T(8,128)(2,1)S(1)}, u32[]{:S(2)}, u32[]{:S(2)}) %collective-permute-start.3) | collective-permute-done | bytes 131104 | tf_op jit(solution)/shard_map/ppermute | solution.py:28
  19.5 6.4 %collective-permute-done.2.bm = bf16[768,128]{1,0:T(8,128)(2,1)S(1)} collective-permute-done((bf16[768,128]{1,0:T(8,128)(2,1)S(1)}, bf16[768,128]{1,0:T(8,128)(2,1)S(1)}, u32[]{:S(2)}, u32[]{:S(2)}) %collective-permute-start.2) | collective-permute-done | bytes 196640 | tf_op jit(solution)/shard_map/ppermute | solution.py:28
  26.7 0.9 kernel.21.meas
  27.9 7.7 %kernel.22 = (f32[384,384]{1,0:T(8,128)S(1)}, bf16[384,384]{1,0:T(8,128)(2,1)S(1)}, f32[2048,128]{1,0:T(8,128)S(1)}, bf16[2048,128]{1,0:T(8,128)(2,1)S(1)}, f32[...) custom-call(s32[1]{0:T(128)S(6)} %copy.9.live, s32[2,4]{1,0:T(2,128)S(1)} %bitcast.30, s32[4]{0:T(128)S(1)} %copy-done.5, ...), custom_call_target="tpu_custom_call" | custom-call | tf_op jit(solution)/shard_map/kernel/pallas_call | solution.py:211
  36.2 1.5 collective-permute-done.20
  38.3 3.1 %collective-permute-start.23 = (bf16[256,256]{1,0:T(8,128)(2,1)S(1)}, bf16[256,256]{1,0:T(8,128)(2,1)S(1)}, u32[]{:S(2)}, u32[]{:S(2)}) collective-permute-start(bf16[256,256]{1,0:T(8,128)(2,1)S(1)} %get-tuple-element.71), channel_id=1, source_target_pairs={{0,6},{2,4},{4,2},{6,0},{8,14},{10,12},{12,10},{14,8},{16,22},{18,... | collective-permute-start | bytes 393224 | tf_op jit(solution)/shard_map/ppermute | solution.py:33
  41.9 2.3 %collective-permute-done.21.refs_0_ = bf16[256,256]{1,0:T(8,128)(2,1)S(1)} collective-permute-done((bf16[256,256]{1,0:T(8,128)(2,1)S(1)}, bf16[256,256]{1,0:T(8,128)(2,1)S(1)}, u32[]{:S(2)}, u32[]{:S(2)}) %collective-permute-start.21) | collective-permute-done | bytes 131104 | tf_op jit(solution)/shard_map/ppermute | solution.py:33
  44.2 2.4 %collective-permute-done.22.refs_1_ = bf16[256,256]{1,0:T(8,128)(2,1)S(1)} collective-permute-done((bf16[256,256]{1,0:T(8,128)(2,1)S(1)}, bf16[256,256]{1,0:T(8,128)(2,1)S(1)}, u32[]{:S(2)}, u32[]{:S(2)}) %collective-permute-start.22) | collective-permute-done | bytes 131104 | tf_op jit(solution)/shard_map/ppermute | solution.py:33
  46.7 2.5 %collective-permute-start.24 = (bf16[64,256]{1,0:T(8,128)(2,1)S(1)}, bf16[64,256]{1,0:T(8,128)(2,1)S(1)}, u32[]{:S(2)}, u32[]{:S(2)}) collective-permute-start(bf16[64,256]{1,0:T(8,128)(2,1)S(1)} %get-tuple-element.73), channel_id=1, source_target_pairs={{0,8},{2,10},{4,12},{6,14},{8,0},{10,2},{12,4},{14,6},{16,24},{18,... | collective-permute-start | bytes 98312 | tf_op jit(solution)/shard_map/ppermute | solution.py:33
  49.2 2.6 %collective-permute-done.24.refs_0_ = bf16[64,256]{1,0:T(8,128)(2,1)S(1)} collective-permute-done((bf16[64,256]{1,0:T(8,128)(2,1)S(1)}, bf16[64,256]{1,0:T(8,128)(2,1)S(1)}, u32[]{:S(2)}, u32[]{:S(2)}) %collective-permute-start.24) | collective-permute-done | bytes 32800 | tf_op jit(solution)/shard_map/ppermute | solution.py:33
  51.8 3.2 %collective-permute-start.25 = (bf16[64,256]{1,0:T(8,128)(2,1)S(1)}, bf16[64,256]{1,0:T(8,128)(2,1)S(1)}, u32[]{:S(2)}, u32[]{:S(2)}) collective-permute-start(bf16[64,256]{1,0:T(8,128)(2,1)S(1)} %get-tuple-element.74), channel_id=1, source_target_pairs={{0,16},{2,18},{4,20},{6,22},{8,24},{10,26},{12,28},{14,30},{16,0},... | collective-permute-start | bytes 98312 | tf_op jit(solution)/shard_map/ppermute | solution.py:33
  55.0 2.7 %collective-permute-done.25.refs_1_ = bf16[64,256]{1,0:T(8,128)(2,1)S(1)} collective-permute-done((bf16[64,256]{1,0:T(8,128)(2,1)S(1)}, bf16[64,256]{1,0:T(8,128)(2,1)S(1)}, u32[]{:S(2)}, u32[]{:S(2)}) %collective-permute-start.25) | collective-permute-done | bytes 32800 | tf_op jit(solution)/shard_map/ppermute | solution.py:33
  57.7 2.6 %collective-permute-start.26 = (bf16[64,256]{1,0:T(8,128)(2,1)S(1)}, bf16[64,256]{1,0:T(8,128)(2,1)S(1)}, u32[]{:S(2)}, u32[]{:S(2)}) collective-permute-start(bf16[64,256]{1,0:T(8,128)(2,1)S(1)} %get-tuple-element.75), channel_id=1, source_target_pairs={{0,24},{2,26},{4,28},{6,30},{8,16},{10,18},{12,20},{14,22},{16,8},... | collective-permute-start | bytes 98312 | tf_op jit(solution)/shard_map/ppermute | solution.py:33
  60.3 3.1 %collective-permute-done.26.refs_2_ = bf16[64,256]{1,0:T(8,128)(2,1)S(1)} collective-permute-done((bf16[64,256]{1,0:T(8,128)(2,1)S(1)}, bf16[64,256]{1,0:T(8,128)(2,1)S(1)}, u32[]{:S(2)}, u32[]{:S(2)}) %collective-permute-start.26) | collective-permute-done | bytes 32800 | tf_op jit(solution)/shard_map/ppermute | solution.py:33
  63.5 2.7 %collective-permute-start.29 = (bf16[64,256]{1,0:T(8,128)(2,1)S(1)}, bf16[64,256]{1,0:T(8,128)(2,1)S(1)}, u32[]{:S(2)}, u32[]{:S(2)}) collective-permute-start(bf16[64,256]{1,0:T(8,128)(2,1)S(1)} %kernel.27.have), channel_id=1, source_target_pairs={{0,24},{2,26},{4,28},{6,30},{8,16},{10,18},{12,20},{14,22},{16,8},... | collective-permute-start | bytes 98312 | tf_op jit(solution)/shard_map/ppermute | solution.py:33
  66.2 1.8 %collective-permute-start.27 = (bf16[64,256]{1,0:T(8,128)(2,1)S(1)}, bf16[64,256]{1,0:T(8,128)(2,1)S(1)}, u32[]{:S(2)}, u32[]{:S(2)}) collective-permute-start(bf16[64,256]{1,0:T(8,128)(2,1)S(1)} %kernel.27.have), channel_id=1, source_target_pairs={{0,8},{2,10},{4,12},{6,14},{8,0},{10,2},{12,4},{14,6},{16,24},{18,... | collective-permute-start | bytes 98312 | tf_op jit(solution)/shard_map/ppermute | solution.py:33
  68.2 6.7 %collective-permute-start.15 = (bf16[512,128]{1,0:T(8,128)(2,1)S(1)}, bf16[512,128]{1,0:T(8,128)(2,1)S(1)}, u32[]{:S(2)}, u32[]{:S(2)}) collective-permute-start(bf16[512,128]{1,0:T(8,128)(2,1)S(1)} %get-tuple-element.65), channel_id=1, source_target_pairs={{0,14},{2,16},{4,18},{6,20},{8,22},{10,24},{12,26},{14,28},{16,30}... | collective-permute-start | bytes 393224 | tf_op jit(solution)/shard_map/ppermute | solution.py:28
  75.0 3.0 %collective-permute-start.32 = (bf16[256,256]{1,0:T(8,128)(2,1)S(1)}, bf16[256,256]{1,0:T(8,128)(2,1)S(1)}, u32[]{:S(2)}, u32[]{:S(2)}) collective-permute-start(bf16[256,256]{1,0:T(8,128)(2,1)S(1)} %kernel.28.have), channel_id=1, source_target_pairs={{0,6},{2,4},{4,2},{6,0},{8,14},{10,12},{12,10},{14,8},{16,22},{18,... | collective-permute-start | bytes 393224 | tf_op jit(solution)/shard_map/ppermute | solution.py:33
  78.8 5.4 %collective-permute-start.13 = (bf16[768,128]{1,0:T(8,128)(2,1)S(1)}, bf16[768,128]{1,0:T(8,128)(2,1)S(1)}, u32[]{:S(2)}, u32[]{:S(2)}) collective-permute-start(bf16[768,128]{1,0:T(8,128)(2,1)S(1)} %get-tuple-element.63), channel_id=1, source_target_pairs={{0,30},{2,0},{4,2},{6,4},{8,6},{10,8},{12,10},{14,12},{16,14},{18,... | collective-permute-start | bytes 589832 | tf_op jit(solution)/shard_map/ppermute | solution.py:28
  84.9 4.2 %collective-permute-done.30.refs_0_ = bf16[256,256]{1,0:T(8,128)(2,1)S(1)} collective-permute-done((bf16[256,256]{1,0:T(8,128)(2,1)S(1)}, bf16[256,256]{1,0:T(8,128)(2,1)S(1)}, u32[]{:S(2)}, u32[]{:S(2)}) %collective-permute-start.30) | collective-permute-done | bytes 131104 | tf_op jit(solution)/shard_map/ppermute | solution.py:33
  89.6 5.6 %collective-permute-done.14.bm = bf16[768,128]{1,0:T(8,128)(2,1)S(1)} collective-permute-done((bf16[768,128]{1,0:T(8,128)(2,1)S(1)}, bf16[768,128]{1,0:T(8,128)(2,1)S(1)}, u32[]{:S(2)}, u32[]{:S(2)}) %collective-permute-start.14) | collective-permute-done | bytes 196640 | tf_op jit(solution)/shard_map/ppermute | solution.py:28
  96.0 0.9 collective-permute-done.34.refs_0_
  97.2 7.7 %kernel.31 = (f32[384,384]{1,0:T(8,128)S(1)}, bf16[384,384]{1,0:T(8,128)(2,1)S(1)}, f32[2048,128]{1,0:T(8,128)S(1)}, bf16[2048,128]{1,0:T(8,128)(2,1)S(1)}, f32[...) custom-call(s32[1]{0:T(128)S(6)} %copy.9.live, s32[2,4]{1,0:T(2,128)S(1)} %bitcast.31, s32[4]{0:T(128)S(1)} %copy-done.5, ...), custom_call_target="tpu_custom_call" | custom-call | tf_op jit(solution)/shard_map/kernel/pallas_call | solution.py:211
  105.6 1.2 collective-permute-done.38.got
  107.2 13.2 %collective-permute-done.41.diag = bf16[512,128]{1,0:T(8,128)(2,1)S(1)} collective-permute-done((bf16[512,128]{1,0:T(8,128)(2,1)S(1)}, bf16[512,128]{1,0:T(8,128)(2,1)S(1)}, u32[]{:S(2)}, u32[]{:S(2)}) %collective-permute-start.41) | collective-permute-done | bytes 131104 | tf_op jit(solution)/shard_map/ppermute | solution.py:28
  120.4 1.1 kernel.33
  121.6 4.1 %collective-permute-start.44 = (bf16[256,256]{1,0:T(8,128)(2,1)S(1)}, bf16[256,256]{1,0:T(8,128)(2,1)S(1)}, u32[]{:S(2)}, u32[]{:S(2)}) collective-permute-start(bf16[256,256]{1,0:T(8,128)(2,1)S(1)} %get-tuple-element.87), channel_id=1, source_target_pairs={{0,2},{2,0},{4,6},{6,4},{8,10},{10,8},{12,14},{14,12},{16,18},{18,... | collective-permute-start | bytes 393224 | tf_op jit(solution)/shard_map/ppermute | solution.py:33
  125.8 1.1 collective-permute-start.45
  127.3 2.8 %collective-permute-done.44.refs_0_ = bf16[256,256]{1,0:T(8,128)(2,1)S(1)} collective-permute-done((bf16[256,256]{1,0:T(8,128)(2,1)S(1)}, bf16[256,256]{1,0:T(8,128)(2,1)S(1)}, u32[]{:S(2)}, u32[]{:S(2)}) %collective-permute-start.44) | collective-permute-done | bytes 131104 | tf_op jit(solution)/shard_map/ppermute | solution.py:33
  130.1 4.1 %collective-permute-done.45.refs_1_ = bf16[256,256]{1,0:T(8,128)(2,1)S(1)} collective-permute-done((bf16[256,256]{1,0:T(8,128)(2,1)S(1)}, bf16[256,256]{1,0:T(8,128)(2,1)S(1)}, u32[]{:S(2)}, u32[]{:S(2)}) %collective-permute-start.45) | collective-permute-done | bytes 131104 | tf_op jit(solution)/shard_map/ppermute | solution.py:33
  134.3 3.0 %collective-permute-start.47 = (bf16[64,256]{1,0:T(8,128)(2,1)S(1)}, bf16[64,256]{1,0:T(8,128)(2,1)S(1)}, u32[]{:S(2)}, u32[]{:S(2)}) collective-permute-start(bf16[64,256]{1,0:T(8,128)(2,1)S(1)} %get-tuple-element.91), channel_id=1, source_target_pairs={{0,8},{2,10},{4,12},{6,14},{8,0},{10,2},{12,4},{14,6},{16,24},{18,... | collective-permute-start | bytes 98312 | tf_op jit(solution)/shard_map/ppermute | solution.py:33
  137.5 2.1 %collective-permute-start.49 = (bf16[64,256]{1,0:T(8,128)(2,1)S(1)}, bf16[64,256]{1,0:T(8,128)(2,1)S(1)}, u32[]{:S(2)}, u32[]{:S(2)}) collective-permute-start(bf16[64,256]{1,0:T(8,128)(2,1)S(1)} %get-tuple-element.93), channel_id=1, source_target_pairs={{0,24},{2,26},{4,28},{6,30},{8,16},{10,18},{12,20},{14,22},{16,8},... | collective-permute-start | bytes 98312 | tf_op jit(solution)/shard_map/ppermute | solution.py:33
  139.7 2.4 %collective-permute-done.48.refs_1_ = bf16[64,256]{1,0:T(8,128)(2,1)S(1)} collective-permute-done((bf16[64,256]{1,0:T(8,128)(2,1)S(1)}, bf16[64,256]{1,0:T(8,128)(2,1)S(1)}, u32[]{:S(2)}, u32[]{:S(2)}) %collective-permute-start.48) | collective-permute-done | bytes 32800 | tf_op jit(solution)/shard_map/ppermute | solution.py:33
  142.1 1.2 collective-permute-done.49.refs_2_
  143.3 2.2 %collective-permute-start.52 = (bf16[64,256]{1,0:T(8,128)(2,1)S(1)}, bf16[64,256]{1,0:T(8,128)(2,1)S(1)}, u32[]{:S(2)}, u32[]{:S(2)}) collective-permute-start(bf16[64,256]{1,0:T(8,128)(2,1)S(1)} %kernel.37.have), channel_id=1, source_target_pairs={{0,24},{2,26},{4,28},{6,30},{8,16},{10,18},{12,20},{14,22},{16,8},... | collective-permute-start | bytes 98312 | tf_op jit(solution)/shard_map/ppermute | solution.py:33
  145.5 2.2 %collective-permute-start.50 = (bf16[64,256]{1,0:T(8,128)(2,1)S(1)}, bf16[64,256]{1,0:T(8,128)(2,1)S(1)}, u32[]{:S(2)}, u32[]{:S(2)}) collective-permute-start(bf16[64,256]{1,0:T(8,128)(2,1)S(1)} %kernel.37.have), channel_id=1, source_target_pairs={{0,8},{2,10},{4,12},{6,14},{8,0},{10,2},{12,4},{14,6},{16,24},{18,... | collective-permute-start | bytes 98312 | tf_op jit(solution)/shard_map/ppermute | solution.py:33
  147.7 1.3 collective-permute-done.52.refs_2_
  149.1 1.2 collective-permute-done.51.refs_1_
  150.3 1.6 collective-permute-start.55
  151.9 1.6 %collective-permute-start.54 = (bf16[256,256]{1,0:T(8,128)(2,1)S(1)}, bf16[256,256]{1,0:T(8,128)(2,1)S(1)}, u32[]{:S(2)}, u32[]{:S(2)}) collective-permute-start(bf16[256,256]{1,0:T(8,128)(2,1)S(1)} %kernel.38.have), channel_id=1, source_target_pairs={{0,4},{2,6},{4,0},{6,2},{8,12},{10,14},{12,8},{14,10},{16,20},{18,... | collective-permute-start | bytes 393224 | tf_op jit(solution)/shard_map/ppermute | solution.py:33
  153.9 2.5 %collective-permute-done.55.refs_2_ = bf16[256,256]{1,0:T(8,128)(2,1)S(1)} collective-permute-done((bf16[256,256]{1,0:T(8,128)(2,1)S(1)}, bf16[256,256]{1,0:T(8,128)(2,1)S(1)}, u32[]{:S(2)}, u32[]{:S(2)}) %collective-permute-start.55) | collective-permute-done | bytes 131104 | tf_op jit(solution)/shard_map/ppermute | solution.py:33
  156.3 1.3 collective-permute-done.54.refs_1_
  158.5 1.1 kernel.39
  159.6 1.1 kernel.34
  (104 shorter events, 11.4 us)
Async XLA Ops:
  0.6 27.0 %collective-permute-start = (f32[2,8]{1,0:T(2,128)}, f32[2,8]{1,0:T(2,128)S(1)}, u32[]{:S(2)}, u32[]{:S(2)}) collective-permute-start(f32[2,8]{1,0:T(2,128)} %bitcast.32), channel_id=1, source_target_pairs={{0,1},{1,0},{2,3},{3,2},{4,5},{5,4},{6,7},{7,6},{8,9},{9,8},{10,11... | collective-permute-start | bytes 200 | tf_op jit(solution)/shard_map/ppermute | solution.py:37
  1.2 26.5 %collective-permute-start.7 = (f32[2,2,256,256]{3,2,1,0:T(8,128)}, f32[2,2,256,256]{3,2,1,0:T(8,128)S(1)}, u32[]{:S(2)}, u32[]{:S(2)}) collective-permute-start(f32[2,2,256,256]{3,2,1,0:T(8,128)} %pm.1), channel_id=1, source_target_pairs={{0,1},{1,0},{2,3},{3,2},{4,5},{5,4},{6,7},{7,6},{8,9},{9,8},{10,11... | collective-permute-start | bytes 3145736 | tf_op jit(solution)/shard_map/ppermute | solution.py:37
  2.7 16.4 %collective-permute-start.3 = (bf16[512,128]{1,0:T(8,128)(2,1)S(1)}, bf16[512,128]{1,0:T(8,128)(2,1)S(1)}, u32[]{:S(2)}, u32[]{:S(2)}) collective-permute-start(bf16[512,128]{1,0:T(8,128)(2,1)S(1)} %get-tuple-element.52), channel_id=1, source_target_pairs={{0,14},{2,16},{4,18},{6,20},{8,22},{10,24},{12,26},{14,28},{16,30}... | collective-permute-start | bytes 393224 | tf_op jit(solution)/shard_map/ppermute | solution.py:28
  7.6 11.4 %collective-permute-start.1 = (bf16[768,128]{1,0:T(8,128)(2,1)S(1)}, bf16[768,128]{1,0:T(8,128)(2,1)S(1)}, u32[]{:S(2)}, u32[]{:S(2)}) collective-permute-start(bf16[768,128]{1,0:T(8,128)(2,1)S(1)} %get-tuple-element.50), channel_id=1, source_target_pairs={{0,30},{2,0},{4,2},{6,4},{8,6},{10,8},{12,10},{14,12},{16,14},{18,... | collective-permute-start | bytes 589832 | tf_op jit(solution)/shard_map/ppermute | solution.py:28
  9.9 16.0 %collective-permute-start.2 = (bf16[768,128]{1,0:T(8,128)(2,1)S(1)}, bf16[768,128]{1,0:T(8,128)(2,1)S(1)}, u32[]{:S(2)}, u32[]{:S(2)}) collective-permute-start(bf16[768,128]{1,0:T(8,128)(2,1)S(1)} %get-tuple-element.51), channel_id=1, source_target_pairs={{0,16},{2,18},{4,20},{6,22},{8,24},{10,26},{12,28},{14,30},{16,0},... | collective-permute-start | bytes 589832 | tf_op jit(solution)/shard_map/ppermute | solution.py:28
  19.0 8.6 %collective-permute-start.6 = (bf16[512,128]{1,0:T(8,128)(2,1)S(1)}, bf16[512,128]{1,0:T(8,128)(2,1)S(1)}, u32[]{:S(2)}, u32[]{:S(2)}) collective-permute-start(bf16[512,128]{1,0:T(8,128)(2,1)S(1)} %collective-permute-done.3.dm), channel_id=1, source_target_pairs={{0,1},{1,0},{2,3},{3,2},{4,5},{5,4},{6,7},{7,6},{8,9},{9,8},{10,11... | collective-permute-start | bytes 393224 | tf_op jit(solution)/shard_map/ppermute | solution.py:37
  19.0 8.6 %collective-permute-start.4 = (bf16[768,128]{1,0:T(8,128)(2,1)S(1)}, bf16[768,128]{1,0:T(8,128)(2,1)S(1)}, u32[]{:S(2)}, u32[]{:S(2)}) collective-permute-start(bf16[768,128]{1,0:T(8,128)(2,1)S(1)} %collective-permute-done.1.rm), channel_id=1, source_target_pairs={{0,1},{1,0},{2,3},{3,2},{4,5},{5,4},{6,7},{7,6},{8,9},{9,8},{10,11... | collective-permute-start | bytes 589832 | tf_op jit(solution)/shard_map/ppermute | solution.py:37
  36.1 5.3 %collective-permute-start.9 = (bf16[2048,128]{1,0:T(8,128)(2,1)S(1)}, bf16[2048,128]{1,0:T(8,128)(2,1)S(1)}, u32[]{:S(2)}, u32[]{:S(2)}) collective-permute-start(bf16[2048,128]{1,0:T(8,128)(2,1)S(1)} %get-tuple-element.57), channel_id=1, source_target_pairs={{0,1},{1,0},{2,3},{3,2},{4,5},{5,4},{6,7},{7,6},{8,9},{9,8},{10,11... | collective-permute-start | bytes 1572872 | tf_op jit(solution)/shard_map/ppermute | solution.py:37
  37.8 6.4 %collective-permute-start.21 = (bf16[256,256]{1,0:T(8,128)(2,1)S(1)}, bf16[256,256]{1,0:T(8,128)(2,1)S(1)}, u32[]{:S(2)}, u32[]{:S(2)}) collective-permute-start(bf16[256,256]{1,0:T(8,128)(2,1)S(1)} %get-tuple-element.69), channel_id=1, source_target_pairs={{0,2},{2,0},{4,6},{6,4},{8,10},{10,8},{12,14},{14,12},{16,18},{18,... | collective-permute-start | bytes 393224 | tf_op jit(solution)/shard_map/ppermute | solution.py:33
  37.8 28.3 %collective-permute-start.8 = (bf16[384,384]{1,0:T(8,128)(2,1)S(1)}, bf16[384,384]{1,0:T(8,128)(2,1)S(1)}, u32[]{:S(2)}, u32[]{:S(2)}) collective-permute-start(bf16[384,384]{1,0:T(8,128)(2,1)S(1)} %get-tuple-element.55), channel_id=1, source_target_pairs={{0,1},{1,0},{2,3},{3,2},{4,5},{5,4},{6,7},{7,6},{8,9},{9,8},{10,11... | collective-permute-start | bytes 884744 | tf_op jit(solution)/shard_map/ppermute | solution.py:37
  38.3 8.3 %collective-permute-start.22 = (bf16[256,256]{1,0:T(8,128)(2,1)S(1)}, bf16[256,256]{1,0:T(8,128)(2,1)S(1)}, u32[]{:S(2)}, u32[]{:S(2)}) collective-permute-start(bf16[256,256]{1,0:T(8,128)(2,1)S(1)} %get-tuple-element.70), channel_id=1, source_target_pairs={{0,4},{2,6},{4,0},{6,2},{8,12},{10,14},{12,8},{14,10},{16,20},{18,... | collective-permute-start | bytes 393224 | tf_op jit(solution)/shard_map/ppermute | solution.py:33
  38.3 8.4 %collective-permute-start.23 = (bf16[256,256]{1,0:T(8,128)(2,1)S(1)}, bf16[256,256]{1,0:T(8,128)(2,1)S(1)}, u32[]{:S(2)}, u32[]{:S(2)}) collective-permute-start(bf16[256,256]{1,0:T(8,128)(2,1)S(1)} %get-tuple-element.71), channel_id=1, source_target_pairs={{0,6},{2,4},{4,2},{6,0},{8,14},{10,12},{12,10},{14,8},{16,22},{18,... | collective-permute-start | bytes 393224 | tf_op jit(solution)/shard_map/ppermute | solution.py:33
  41.5 26.4 %collective-permute-start.10 = (bf16[768,128]{1,0:T(8,128)(2,1)S(1)}, bf16[768,128]{1,0:T(8,128)(2,1)S(1)}, u32[]{:S(2)}, u32[]{:S(2)}) collective-permute-start(bf16[768,128]{1,0:T(8,128)(2,1)S(1)} %get-tuple-element.58), channel_id=1, source_target_pairs={{0,2},{2,4},{4,6},{6,8},{8,10},{10,12},{12,14},{14,16},{16,18},{18... | collective-permute-start | bytes 589832 | tf_op jit(solution)/shard_map/ppermute | solution.py:28
  44.2 23.7 %collective-permute-start.11 = (bf16[768,128]{1,0:T(8,128)(2,1)S(1)}, bf16[768,128]{1,0:T(8,128)(2,1)S(1)}, u32[]{:S(2)}, u32[]{:S(2)}) collective-permute-start(bf16[768,128]{1,0:T(8,128)(2,1)S(1)} %get-tuple-element.59), channel_id=1, source_target_pairs={{0,16},{2,18},{4,20},{6,22},{8,24},{10,26},{12,28},{14,30},{16,0},... | collective-permute-start | bytes 589832 | tf_op jit(solution)/shard_map/ppermute | solution.py:28
  46.6 19.5 %collective-permute-start.12 = (bf16[512,128]{1,0:T(8,128)(2,1)S(1)}, bf16[512,128]{1,0:T(8,128)(2,1)S(1)}, u32[]{:S(2)}, u32[]{:S(2)}) collective-permute-start(bf16[512,128]{1,0:T(8,128)(2,1)S(1)} %get-tuple-element.60), channel_id=1, source_target_pairs={{0,18},{2,20},{4,22},{6,24},{8,26},{10,28},{12,30},{14,0},{16,2},{... | collective-permute-start | bytes 393224 | tf_op jit(solution)/shard_map/ppermute | solution.py:28
  46.7 5.1 %collective-permute-start.24 = (bf16[64,256]{1,0:T(8,128)(2,1)S(1)}, bf16[64,256]{1,0:T(8,128)(2,1)S(1)}, u32[]{:S(2)}, u32[]{:S(2)}) collective-permute-start(bf16[64,256]{1,0:T(8,128)(2,1)S(1)} %get-tuple-element.73), channel_id=1, source_target_pairs={{0,8},{2,10},{4,12},{6,14},{8,0},{10,2},{12,4},{14,6},{16,24},{18,... | collective-permute-start | bytes 98312 | tf_op jit(solution)/shard_map/ppermute | solution.py:33
  51.8 5.9 %collective-permute-start.25 = (bf16[64,256]{1,0:T(8,128)(2,1)S(1)}, bf16[64,256]{1,0:T(8,128)(2,1)S(1)}, u32[]{:S(2)}, u32[]{:S(2)}) collective-permute-start(bf16[64,256]{1,0:T(8,128)(2,1)S(1)} %get-tuple-element.74), channel_id=1, source_target_pairs={{0,16},{2,18},{4,20},{6,22},{8,24},{10,26},{12,28},{14,30},{16,0},... | collective-permute-start | bytes 98312 | tf_op jit(solution)/shard_map/ppermute | solution.py:33
  57.7 5.7 %collective-permute-start.26 = (bf16[64,256]{1,0:T(8,128)(2,1)S(1)}, bf16[64,256]{1,0:T(8,128)(2,1)S(1)}, u32[]{:S(2)}, u32[]{:S(2)}) collective-permute-start(bf16[64,256]{1,0:T(8,128)(2,1)S(1)} %get-tuple-element.75), channel_id=1, source_target_pairs={{0,24},{2,26},{4,28},{6,30},{8,16},{10,18},{12,20},{14,22},{16,8},... | collective-permute-start | bytes 98312 | tf_op jit(solution)/shard_map/ppermute | solution.py:33
  63.5 11.5 %collective-permute-start.29 = (bf16[64,256]{1,0:T(8,128)(2,1)S(1)}, bf16[64,256]{1,0:T(8,128)(2,1)S(1)}, u32[]{:S(2)}, u32[]{:S(2)}) collective-permute-start(bf16[64,256]{1,0:T(8,128)(2,1)S(1)} %kernel.27.have), channel_id=1, source_target_pairs={{0,24},{2,26},{4,28},{6,30},{8,16},{10,18},{12,20},{14,22},{16,8},... | collective-permute-start | bytes 98312 | tf_op jit(solution)/shard_map/ppermute | solution.py:33
  66.1 8.8 %collective-permute-start.28 = (bf16[64,256]{1,0:T(8,128)(2,1)S(1)}, bf16[64,256]{1,0:T(8,128)(2,1)S(1)}, u32[]{:S(2)}, u32[]{:S(2)}) collective-permute-start(bf16[64,256]{1,0:T(8,128)(2,1)S(1)} %kernel.27.have), channel_id=1, source_target_pairs={{0,16},{2,18},{4,20},{6,22},{8,24},{10,26},{12,28},{14,30},{16,0},... | collective-permute-start | bytes 98312 | tf_op jit(solution)/shard_map/ppermute | solution.py:33
  66.2 8.8 %collective-permute-start.27 = (bf16[64,256]{1,0:T(8,128)(2,1)S(1)}, bf16[64,256]{1,0:T(8,128)(2,1)S(1)}, u32[]{:S(2)}, u32[]{:S(2)}) collective-permute-start(bf16[64,256]{1,0:T(8,128)(2,1)S(1)} %kernel.27.have), channel_id=1, source_target_pairs={{0,8},{2,10},{4,12},{6,14},{8,0},{10,2},{12,4},{14,6},{16,24},{18,... | collective-permute-start | bytes 98312 | tf_op jit(solution)/shard_map/ppermute | solution.py:33
  68.2 10.5 %collective-permute-start.15 = (bf16[512,128]{1,0:T(8,128)(2,1)S(1)}, bf16[512,128]{1,0:T(8,128)(2,1)S(1)}, u32[]{:S(2)}, u32[]{:S(2)}) collective-permute-start(bf16[512,128]{1,0:T(8,128)(2,1)S(1)} %get-tuple-element.65), channel_id=1, source_target_pairs={{0,14},{2,16},{4,18},{6,20},{8,22},{10,24},{12,26},{14,28},{16,30}... | collective-permute-start | bytes 393224 | tf_op jit(solution)/shard_map/ppermute | solution.py:28
  74.9 9.2 %collective-permute-start.33 = (bf16[256,256]{1,0:T(8,128)(2,1)S(1)}, bf16[256,256]{1,0:T(8,128)(2,1)S(1)}, u32[]{:S(2)}, u32[]{:S(2)}) collective-permute-start(bf16[256,256]{1,0:T(8,128)(2,1)S(1)} %kernel.28.have), channel_id=1, source_target_pairs={{0,1},{1,0},{2,3},{3,2},{4,5},{5,4},{6,7},{7,6},{8,9},{9,8},{10,11... | collective-permute-start | bytes 393224 | tf_op jit(solution)/shard_map/ppermute | solution.py:37
  75.0 9.1 %collective-permute-start.32 = (bf16[256,256]{1,0:T(8,128)(2,1)S(1)}, bf16[256,256]{1,0:T(8,128)(2,1)S(1)}, u32[]{:S(2)}, u32[]{:S(2)}) collective-permute-start(bf16[256,256]{1,0:T(8,128)(2,1)S(1)} %kernel.28.have), channel_id=1, source_target_pairs={{0,6},{2,4},{4,2},{6,0},{8,14},{10,12},{12,10},{14,8},{16,22},{18,... | collective-permute-start | bytes 393224 | tf_op jit(solution)/shard_map/ppermute | solution.py:33
  78.0 6.9 %collective-permute-start.31 = (bf16[256,256]{1,0:T(8,128)(2,1)S(1)}, bf16[256,256]{1,0:T(8,128)(2,1)S(1)}, u32[]{:S(2)}, u32[]{:S(2)}) collective-permute-start(bf16[256,256]{1,0:T(8,128)(2,1)S(1)} %kernel.28.have), channel_id=1, source_target_pairs={{0,4},{2,6},{4,0},{6,2},{8,12},{10,14},{12,8},{14,10},{16,20},{18,... | collective-permute-start | bytes 393224 | tf_op jit(solution)/shard_map/ppermute | solution.py:33
  78.0 11.1 %collective-permute-start.30 = (bf16[256,256]{1,0:T(8,128)(2,1)S(1)}, bf16[256,256]{1,0:T(8,128)(2,1)S(1)}, u32[]{:S(2)}, u32[]{:S(2)}) collective-permute-start(bf16[256,256]{1,0:T(8,128)(2,1)S(1)} %kernel.28.have), channel_id=1, source_target_pairs={{0,2},{2,0},{4,6},{6,4},{8,10},{10,8},{12,14},{14,12},{16,18},{18,... | collective-permute-start | bytes 393224 | tf_op jit(solution)/shard_map/ppermute | solution.py:33
  78.8 10.4 %collective-permute-start.13 = (bf16[768,128]{1,0:T(8,128)(2,1)S(1)}, bf16[768,128]{1,0:T(8,128)(2,1)S(1)}, u32[]{:S(2)}, u32[]{:S(2)}) collective-permute-start(bf16[768,128]{1,0:T(8,128)(2,1)S(1)} %get-tuple-element.63), channel_id=1, source_target_pairs={{0,30},{2,0},{4,2},{6,4},{8,6},{10,8},{12,10},{14,12},{16,14},{18,... | collective-permute-start | bytes 589832 | tf_op jit(solution)/shard_map/ppermute | solution.py:28
  84.2 11.1 %collective-permute-start.14 = (bf16[768,128]{1,0:T(8,128)(2,1)S(1)}, bf16[768,128]{1,0:T(8,128)(2,1)S(1)}, u32[]{:S(2)}, u32[]{:S(2)}) collective-permute-start(bf16[768,128]{1,0:T(8,128)(2,1)S(1)} %get-tuple-element.64), channel_id=1, source_target_pairs={{0,16},{2,18},{4,20},{6,22},{8,24},{10,26},{12,28},{14,30},{16,0},... | collective-permute-start | bytes 589832 | tf_op jit(solution)/shard_map/ppermute | solution.py:28
  84.2 13.0 %collective-permute-start.16 = (bf16[384,384]{1,0:T(8,128)(2,1)S(1)}, bf16[384,384]{1,0:T(8,128)(2,1)S(1)}, u32[]{:S(2)}, u32[]{:S(2)}) collective-permute-start(bf16[384,384]{1,0:T(8,128)(2,1)S(1)} %get-tuple-element.62.tm), channel_id=1, source_target_pairs={{0,1},{1,0},{2,3},{3,2},{4,5},{5,4},{6,7},{7,6},{8,9},{9,8},{10,11... | collective-permute-start | bytes 884744 | tf_op jit(solution)/shard_map/ppermute | solution.py:37
  84.9 10.4 %collective-permute-start.36 = (bf16[256,256]{1,0:T(8,128)(2,1)S(1)}, bf16[256,256]{1,0:T(8,128)(2,1)S(1)}, u32[]{:S(2)}, u32[]{:S(2)}) collective-permute-start(bf16[256,256]{1,0:T(8,128)(2,1)S(1)} %collective-permute-done.32.refs_2_), channel_id=1, source_target_pairs={{0,1},{1,0},{2,3},{3,2},{4,5},{5,4},{6,7},{7,6},{8,9},{9,8},{10,11... | collective-permute-start | bytes 393224 | tf_op jit(solution)/shard_map/ppermute | solution.py:37
  89.1 6.7 %collective-permute-start.35 = (bf16[256,256]{1,0:T(8,128)(2,1)S(1)}, bf16[256,256]{1,0:T(8,128)(2,1)S(1)}, u32[]{:S(2)}, u32[]{:S(2)}) collective-permute-start(bf16[256,256]{1,0:T(8,128)(2,1)S(1)} %collective-permute-done.31.refs_1_), channel_id=1, source_target_pairs={{0,1},{1,0},{2,3},{3,2},{4,5},{5,4},{6,7},{7,6},{8,9},{9,8},{10,11... | collective-permute-start | bytes 393224 | tf_op jit(solution)/shard_map/ppermute | solution.py:37
  89.2 8.0 %collective-permute-start.17 = (bf16[768,128]{1,0:T(8,128)(2,1)S(1)}, bf16[768,128]{1,0:T(8,128)(2,1)S(1)}, u32[]{:S(2)}, u32[]{:S(2)}) collective-permute-start(bf16[768,128]{1,0:T(8,128)(2,1)S(1)} %collective-permute-done.13.rm), channel_id=1, source_target_pairs={{0,1},{1,0},{2,3},{3,2},{4,5},{5,4},{6,7},{7,6},{8,9},{9,8},{10,11... | collective-permute-start | bytes 589832 | tf_op jit(solution)/shard_map/ppermute | solution.py:37
  105.4 16.1 %collective-permute-start.43 = (bf16[2,2,256,256]{3,2,1,0:T(8,128)(2,1)S(1)}, bf16[2,2,256,256]{3,2,1,0:T(8,128)(2,1)S(1)}, u32[]{:S(2)}, u32[]{:S(2)}) collective-permute-start(bf16[2,2,256,256]{3,2,1,0:T(8,128)(2,1)S(1)} %get-tuple-element.85), channel_id=1, source_target_pairs={{0,1},{1,0},{2,3},{3,2},{4,5},{5,4},{6,7},{7,6},{8,9},{9,8},{10,11... | collective-permute-start | bytes 1572872 | tf_op jit(solution)/shard_map/ppermute | solution.py:37
  106.9 13.5 %collective-permute-start.39 = (bf16[768,128]{1,0:T(8,128)(2,1)S(1)}, bf16[768,128]{1,0:T(8,128)(2,1)S(1)}, u32[]{:S(2)}, u32[]{:S(2)}) collective-permute-start(bf16[768,128]{1,0:T(8,128)(2,1)S(1)} %get-tuple-element.80), channel_id=1, source_target_pairs={{0,2},{2,4},{4,6},{6,8},{8,10},{10,12},{12,14},{14,16},{16,18},{18... | collective-permute-start | bytes 589832 | tf_op jit(solution)/shard_map/ppermute | solution.py:28
  107.0 13.5 %collective-permute-start.40 = (bf16[768,128]{1,0:T(8,128)(2,1)S(1)}, bf16[768,128]{1,0:T(8,128)(2,1)S(1)}, u32[]{:S(2)}, u32[]{:S(2)}) collective-permute-start(bf16[768,128]{1,0:T(8,128)(2,1)S(1)} %get-tuple-element.81), channel_id=1, source_target_pairs={{0,16},{2,18},{4,20},{6,22},{8,24},{10,26},{12,28},{14,30},{16,0},... | collective-permute-start | bytes 589832 | tf_op jit(solution)/shard_map/ppermute | solution.py:28
  107.1 13.4 %collective-permute-start.41 = (bf16[512,128]{1,0:T(8,128)(2,1)S(1)}, bf16[512,128]{1,0:T(8,128)(2,1)S(1)}, u32[]{:S(2)}, u32[]{:S(2)}) collective-permute-start(bf16[512,128]{1,0:T(8,128)(2,1)S(1)} %get-tuple-element.82), channel_id=1, source_target_pairs={{0,18},{2,20},{4,22},{6,24},{8,26},{10,28},{12,30},{14,0},{16,2},{... | collective-permute-start | bytes 393224 | tf_op jit(solution)/shard_map/ppermute | solution.py:28
  121.5 38.0 %collective-permute-start.42 = (f32[384,384]{1,0:T(8,128)S(1)}, f32[384,384]{1,0:T(8,128)S(1)}, u32[]{:S(2)}, u32[]{:S(2)}) collective-permute-start(f32[384,384]{1,0:T(8,128)S(1)} %get-tuple-element.83.state), channel_id=1, source_target_pairs={{0,1},{1,0},{2,3},{3,2},{4,5},{5,4},{6,7},{7,6},{8,9},{9,8},{10,11... | collective-permute-start | bytes 1769480 | tf_op jit(solution)/shard_map/ppermute | solution.py:37
  121.6 8.4 %collective-permute-start.44 = (bf16[256,256]{1,0:T(8,128)(2,1)S(1)}, bf16[256,256]{1,0:T(8,128)(2,1)S(1)}, u32[]{:S(2)}, u32[]{:S(2)}) collective-permute-start(bf16[256,256]{1,0:T(8,128)(2,1)S(1)} %get-tuple-element.87), channel_id=1, source_target_pairs={{0,2},{2,0},{4,6},{6,4},{8,10},{10,8},{12,14},{14,12},{16,18},{18,... | collective-permute-start | bytes 393224 | tf_op jit(solution)/shard_map/ppermute | solution.py:33
  125.8 8.4 %collective-permute-start.45 = (bf16[256,256]{1,0:T(8,128)(2,1)S(1)}, bf16[256,256]{1,0:T(8,128)(2,1)S(1)}, u32[]{:S(2)}, u32[]{:S(2)}) collective-permute-start(bf16[256,256]{1,0:T(8,128)(2,1)S(1)} %get-tuple-element.88), channel_id=1, source_target_pairs={{0,4},{2,6},{4,0},{6,2},{8,12},{10,14},{12,8},{14,10},{16,20},{18,... | collective-permute-start | bytes 393224 | tf_op jit(solution)/shard_map/ppermute | solution.py:33
  126.9 7.3 %collective-permute-start.46 = (bf16[256,256]{1,0:T(8,128)(2,1)S(1)}, bf16[256,256]{1,0:T(8,128)(2,1)S(1)}, u32[]{:S(2)}, u32[]{:S(2)}) collective-permute-start(bf16[256,256]{1,0:T(8,128)(2,1)S(1)} %get-tuple-element.89), channel_id=1, source_target_pairs={{0,6},{2,4},{4,2},{6,0},{8,14},{10,12},{12,10},{14,8},{16,22},{18,... | collective-permute-start | bytes 393224 | tf_op jit(solution)/shard_map/ppermute | solution.py:33
  134.3 5.4 %collective-permute-start.47 = (bf16[64,256]{1,0:T(8,128)(2,1)S(1)}, bf16[64,256]{1,0:T(8,128)(2,1)S(1)}, u32[]{:S(2)}, u32[]{:S(2)}) collective-permute-start(bf16[64,256]{1,0:T(8,128)(2,1)S(1)} %get-tuple-element.91), channel_id=1, source_target_pairs={{0,8},{2,10},{4,12},{6,14},{8,0},{10,2},{12,4},{14,6},{16,24},{18,... | collective-permute-start | bytes 98312 | tf_op jit(solution)/shard_map/ppermute | solution.py:33
  137.2 4.8 %collective-permute-start.48 = (bf16[64,256]{1,0:T(8,128)(2,1)S(1)}, bf16[64,256]{1,0:T(8,128)(2,1)S(1)}, u32[]{:S(2)}, u32[]{:S(2)}) collective-permute-start(bf16[64,256]{1,0:T(8,128)(2,1)S(1)} %get-tuple-element.92), channel_id=1, source_target_pairs={{0,16},{2,18},{4,20},{6,22},{8,24},{10,26},{12,28},{14,30},{16,0},... | collective-permute-start | bytes 98312 | tf_op jit(solution)/shard_map/ppermute | solution.py:33
  137.5 5.7 %collective-permute-start.49 = (bf16[64,256]{1,0:T(8,128)(2,1)S(1)}, bf16[64,256]{1,0:T(8,128)(2,1)S(1)}, u32[]{:S(2)}, u32[]{:S(2)}) collective-permute-start(bf16[64,256]{1,0:T(8,128)(2,1)S(1)} %get-tuple-element.93), channel_id=1, source_target_pairs={{0,24},{2,26},{4,28},{6,30},{8,16},{10,18},{12,20},{14,22},{16,8},... | collective-permute-start | bytes 98312 | tf_op jit(solution)/shard_map/ppermute | solution.py:33
  143.3 5.8 %collective-permute-start.52 = (bf16[64,256]{1,0:T(8,128)(2,1)S(1)}, bf16[64,256]{1,0:T(8,128)(2,1)S(1)}, u32[]{:S(2)}, u32[]{:S(2)}) collective-permute-start(bf16[64,256]{1,0:T(8,128)(2,1)S(1)} %kernel.37.have), channel_id=1, source_target_pairs={{0,24},{2,26},{4,28},{6,30},{8,16},{10,18},{12,20},{14,22},{16,8},... | collective-permute-start | bytes 98312 | tf_op jit(solution)/shard_map/ppermute | solution.py:33
  145.5 4.8 %collective-permute-start.51 = (bf16[64,256]{1,0:T(8,128)(2,1)S(1)}, bf16[64,256]{1,0:T(8,128)(2,1)S(1)}, u32[]{:S(2)}, u32[]{:S(2)}) collective-permute-start(bf16[64,256]{1,0:T(8,128)(2,1)S(1)} %kernel.37.have), channel_id=1, source_target_pairs={{0,16},{2,18},{4,20},{6,22},{8,24},{10,26},{12,28},{14,30},{16,0},... | collective-permute-start | bytes 98312 | tf_op jit(solution)/shard_map/ppermute | solution.py:33
  150.3 6.0 %collective-permute-start.55 = (bf16[256,256]{1,0:T(8,128)(2,1)S(1)}, bf16[256,256]{1,0:T(8,128)(2,1)S(1)}, u32[]{:S(2)}, u32[]{:S(2)}) collective-permute-start(bf16[256,256]{1,0:T(8,128)(2,1)S(1)} %kernel.38.have), channel_id=1, source_target_pairs={{0,6},{2,4},{4,2},{6,0},{8,14},{10,12},{12,10},{14,8},{16,22},{18,... | collective-permute-start | bytes 393224 | tf_op jit(solution)/shard_map/ppermute | solution.py:33
  151.9 5.8 %collective-permute-start.54 = (bf16[256,256]{1,0:T(8,128)(2,1)S(1)}, bf16[256,256]{1,0:T(8,128)(2,1)S(1)}, u32[]{:S(2)}, u32[]{:S(2)}) collective-permute-start(bf16[256,256]{1,0:T(8,128)(2,1)S(1)} %kernel.38.have), channel_id=1, source_target_pairs={{0,4},{2,6},{4,0},{6,2},{8,12},{10,14},{12,8},{14,10},{16,20},{18,... | collective-permute-start | bytes 393224 | tf_op jit(solution)/shard_map/ppermute | solution.py:33
  153.5 5.0 %collective-permute-start.53 = (bf16[256,256]{1,0:T(8,128)(2,1)S(1)}, bf16[256,256]{1,0:T(8,128)(2,1)S(1)}, u32[]{:S(2)}, u32[]{:S(2)}) collective-permute-start(bf16[256,256]{1,0:T(8,128)(2,1)S(1)} %kernel.38.have), channel_id=1, source_target_pairs={{0,2},{2,0},{4,6},{6,4},{8,10},{10,8},{12,14},{14,12},{16,18},{18,... | collective-permute-start | bytes 393224 | tf_op jit(solution)/shard_map/ppermute | solution.py:33
  (14 other events, 38.7 us)

commit v3 on v2

--- a/solution.py
+++ b/solution.py
@@ -60,6 +60,7 @@
 
 
 LANES = 128
+SUBS = 8
 
 
 def blocks(t, n, refs):
@@ -91,7 +92,6 @@
                 frame[plane, pl.ds(top, high), pl.ds(left + k * LANES, LANES)] = part
     grad[...] = jnp.zeros_like(grad)
     acc[...] = jnp.zeros_like(acc)
-    term[...] = jnp.zeros_like(term)
 
     def probe_at(m, c, rows, cols=slice(None)):
         ref = pm if m < half else po
@@ -104,16 +104,26 @@
         def _():
             row = corner[0, s]
             col = corner[1, s]
-            rb = pl.multiple_of(row // 8 * 8, 8)
+            cb = pl.multiple_of(col // LANES * LANES, LANES)
+            cc = col - cb
+            rb = pl.multiple_of(row // SUBS * SUBS, SUBS)
             rr = row - rb
-            cb = pl.multiple_of(col // 128 * 128, 128)
-            cc = col - cb
-            high, wide = n + 8, n + 128
+            count, tall_count = n // LANES, n // SUBS
+            lane = lax.broadcasted_iota(jnp.int32, (1, SUBS, LANES), 2)
+            sub = lax.broadcasted_iota(jnp.int32, (1, SUBS, LANES), 1)
+            rows = pl.ds(rb, n + SUBS)
+            left, above = lane < LANES - cc, sub < SUBS - rr
             for p, out in ((0, orr), (1, oii)):
-                win = frame[p, pl.ds(rb, high), pl.ds(cb, wide)]
-                win = pltpu.roll(win, lax.rem(wide - cc, wide), 1)[:, :n]
-                win = pltpu.roll(win, lax.rem(high - rr, high), 0)[:n]
-                out[...] = win
+                turned = []
+                for k in range(count + 1):
+                    block = frame[p, rows, pl.ds(cb + k * LANES, LANES)]
+                    block = block.reshape(tall_count + 1, SUBS, LANES)
+                    turned.append(pltpu.roll(block, lax.rem(LANES - cc, LANES), 2))
+                for k in range(count):
+                    block = jnp.where(left, turned[k], turned[k + 1])
+                    block = pltpu.roll(block, lax.rem(SUBS - rr, SUBS), 1)
+                    block = jnp.where(above, block[:-1], block[1:])
+                    out[:, pl.ds(k * LANES, LANES)] = block.reshape(n, LANES)
             lanes = [pl.ds(q * h, h) for q in range(2)]
             w = [wm[m, kind[s]] if m < half else wo[m - half, kind[s]] for m in range(modes)]
             for m in range(modes):
@@ -186,9 +196,24 @@
                         acc[m, 1, up, cols] += a * ci - b * cr
                     term[0, up, cols] = tr
                     term[1, up, cols] = ti
+            rows = pl.ds(rb, n + SUBS)
+            begun, over = lane < cc, sub < rr
             for p in range(2):
-                moved = pltpu.roll(pltpu.roll(term[p], rr, 0), cc, 1)
-                grad[p, pl.ds(rb, high), pl.ds(cb, wide)] += moved
+                turned = []
+                for k in range(count):
+                    block = term[p, :, pl.ds(k * LANES, LANES)]
+                    block = pltpu.roll(block.reshape(tall_count, SUBS, LANES), rr, 1)
+                    edge = jnp.zeros((1, SUBS, LANES), f32)
+                    before = jnp.concatenate([edge, block], 0)
+                    after = jnp.concatenate([block, edge], 0)
+                    turned.append(pltpu.roll(jnp.where(over, before, after), cc, 2))
+                nothing = jnp.zeros_like(turned[0])
+                for k in range(count + 1):
+                    low = turned[k - 1] if k else nothing
+                    high = turned[k] if k < count else nothing
+                    cols = pl.ds(cb + k * LANES, LANES)
+                    moved = jnp.where(begun, low, high)
+                    grad[p, rows, cols] += moved.reshape(n + SUBS, LANES)
 
         return carry
 
@@ -275,7 +300,7 @@
             pltpu.VMEM((2, modes * n, n), bf16),
             pltpu.VMEM((n, n), f32),
             pltpu.VMEM((n, n), f32),
-            pltpu.VMEM((2, n + 8, n + 128), f32),
+            pltpu.VMEM((2, n, n), f32),
             pltpu.VMEM((modes, 2, n, n), f32),
         ],
         limit=24 * 1024 * 1024,
@@ -358,7 +383,7 @@
 def digits(peers):
     out, shift = [], 0
     while 1 << shift < peers:
-        radix = 4 if (4 << shift) <= peers else 2
+        radix = 4 if shift == 0 and peers >= 4 else 2
         out.append((shift, radix))
         shift += radix.bit_length() - 1
     return out

time: 161 us -> 159 us (0.988)
  starting transfers between devices: 64.5 us -> 48.5 us
  waiting for transfers between devices: 71 us -> 86.4 us
    ppermute x24 -> x20, waiting for transfers between devices: 35.5 us -> 57.8 us  [flipped(): return lax.ppermute(array, 'tile', [(i, i ^ mask) for i in range(peers)])]
    ppermute x24 -> x20, starting transfers between devices: 38.7 us -> 23.9 us  [flipped(): return lax.ppermute(array, 'tile', [(i, i ^ mask) for i in range(peers)])]
    ppermute x12, waiting for transfers between devices: 31.5 us -> 24.6 us  [shifted(): lax.ppermute(array, 'tile', [(i, (i + by) % peers) for i in range(peers)])]
    pallas_call x20 -> x24, Pallas kernels: 20.7 us -> 19.3 us  [call(): pl.pallas_call(kernel, out_shape=tuple((jax.ShapeDtypeStruct(shape, dtype...]
  transfers between devices with their start and end apart: 56 -> 52, of which waited for: 26 -> 25; matrix products, arithmetic and copies ran while one was open for 1% -> 1% of each run, Pallas kernels for 3% -> 3%
where the time goes in v3:
time: 159 us
  waiting for transfers between devices  86.4 us (54%)
  starting transfers between devices  48.5 us (31%)
  Pallas kernels  19.3 us (12%)
  between operations  1.6 us (1%)
    ppermute x20, waiting for transfers between devices, flipped(): return lax.ppermute(array, 'tile', [(i, i ^ mask) for i in range(peers)])  57.8 us
    ppermute x12, waiting for transfers between devices, shifted(): lax.ppermute(array, 'tile', [(i, (i + by) % peers) for i in range(peers)])  24.6 us
    ppermute x20, starting transfers between devices, flipped(): return lax.ppermute(array, 'tile', [(i, i ^ mask) for i in range(peers)])  23.9 us
    ppermute x12, starting transfers between devices, shifted(): lax.ppermute(array, 'tile', [(i, (i + by) % peers) for i in range(peers)])  20.3 us
    pallas_call x24, Pallas kernels, call(): pl.pallas_call(kernel, out_shape=tuple((jax.ShapeDtypeStruct(shape, dtype...  19.3 us
    ppermute x20, starting transfers between devices, swapped(): return lax.ppermute(array, 'mode', [(0, 1), (1, 0)])  4.3 us
    ppermute x20, waiting for transfers between devices, swapped(): return lax.ppermute(array, 'mode', [(0, 1), (1, 0)])  4.04 us
  transfers between devices with their start and end apart: 52, of which 25 were waited for; matrix products, arithmetic and copies ran while one was open for 1% of the time, Pallas kernels for 3%

profile of v3, /device:TPU:0, one launch (start us, length us, event | category | flops | bytes accessed | tf_op | source)
XLA Modules:
  0.0 158.6 jit_solution(9753361582377609695)
XLA Ops:
  0.6 0.6 collective-permute-start
  1.3 1.3 copy-done.1
  2.7 4.9 %collective-permute-start.3 = (bf16[512,128]{1,0:T(8,128)(2,1)S(1)}, bf16[512,128]{1,0:T(8,128)(2,1)S(1)}, u32[]{:S(2)}, u32[]{:S(2)}) collective-permute-start(bf16[512,128]{1,0:T(8,128)(2,1)S(1)} %get-tuple-element.52), channel_id=1, source_target_pairs={{0,14},{2,16},{4,18},{6,20},{8,22},{10,24},{12,26},{14,28},{16,30}... | collective-permute-start | bytes 393224 | tf_op jit(solution)/shard_map/ppermute | solution.py:28
  7.6 2.3 %collective-permute-start.1 = (bf16[768,128]{1,0:T(8,128)(2,1)S(1)}, bf16[768,128]{1,0:T(8,128)(2,1)S(1)}, u32[]{:S(2)}, u32[]{:S(2)}) collective-permute-start(bf16[768,128]{1,0:T(8,128)(2,1)S(1)} %get-tuple-element.50), channel_id=1, source_target_pairs={{0,30},{2,0},{4,2},{6,4},{8,6},{10,8},{12,10},{14,12},{16,14},{18,... | collective-permute-start | bytes 589832 | tf_op jit(solution)/shard_map/ppermute | solution.py:28
  9.9 1.7 %collective-permute-start.2 = (bf16[768,128]{1,0:T(8,128)(2,1)S(1)}, bf16[768,128]{1,0:T(8,128)(2,1)S(1)}, u32[]{:S(2)}, u32[]{:S(2)}) collective-permute-start(bf16[768,128]{1,0:T(8,128)(2,1)S(1)} %get-tuple-element.51), channel_id=1, source_target_pairs={{0,16},{2,18},{4,20},{6,22},{8,24},{10,26},{12,28},{14,30},{16,0},... | collective-permute-start | bytes 589832 | tf_op jit(solution)/shard_map/ppermute | solution.py:28
  11.6 0.6 negate_convert_fusion.1
  12.2 0.6 negate_convert_fusion
  12.9 6.2 %collective-permute-done.3.dm = bf16[512,128]{1,0:T(8,128)(2,1)S(1)} collective-permute-done((bf16[512,128]{1,0:T(8,128)(2,1)S(1)}, bf16[512,128]{1,0:T(8,128)(2,1)S(1)}, u32[]{:S(2)}, u32[]{:S(2)}) %collective-permute-start.3) | collective-permute-done | bytes 131104 | tf_op jit(solution)/shard_map/ppermute | solution.py:28
  19.5 6.4 %collective-permute-done.2.bm = bf16[768,128]{1,0:T(8,128)(2,1)S(1)} collective-permute-done((bf16[768,128]{1,0:T(8,128)(2,1)S(1)}, bf16[768,128]{1,0:T(8,128)(2,1)S(1)}, u32[]{:S(2)}, u32[]{:S(2)}) %collective-permute-start.2) | collective-permute-done | bytes 196640 | tf_op jit(solution)/shard_map/ppermute | solution.py:28
  26.7 0.9 kernel.25.meas
  27.9 6.9 %kernel.26 = (f32[384,384]{1,0:T(8,128)S(1)}, bf16[384,384]{1,0:T(8,128)(2,1)S(1)}, f32[2048,128]{1,0:T(8,128)S(1)}, bf16[2048,128]{1,0:T(8,128)(2,1)S(1)}, f32[...) custom-call(s32[1]{0:T(128)S(6)} %copy.9.live, s32[2,4]{1,0:T(2,128)S(1)} %bitcast.30, s32[4]{0:T(128)S(1)} %copy-done.5, ...), custom_call_target="tpu_custom_call" | custom-call | tf_op jit(solution)/shard_map/kernel/pallas_call | solution.py:236
  34.8 0.6 collective-permute-start.20
  35.5 1.5 collective-permute-done.20
  37.6 3.1 %collective-permute-start.23 = (bf16[256,256]{1,0:T(8,128)(2,1)S(1)}, bf16[256,256]{1,0:T(8,128)(2,1)S(1)}, u32[]{:S(2)}, u32[]{:S(2)}) collective-permute-start(bf16[256,256]{1,0:T(8,128)(2,1)S(1)} %get-tuple-element.71), channel_id=1, source_target_pairs={{0,6},{2,4},{4,2},{6,0},{8,14},{10,12},{12,10},{14,8},{16,22},{18,... | collective-permute-start | bytes 393224 | tf_op jit(solution)/shard_map/ppermute | solution.py:33
  41.2 2.3 %collective-permute-done.21.refs_0_ = bf16[256,256]{1,0:T(8,128)(2,1)S(1)} collective-permute-done((bf16[256,256]{1,0:T(8,128)(2,1)S(1)}, bf16[256,256]{1,0:T(8,128)(2,1)S(1)}, u32[]{:S(2)}, u32[]{:S(2)}) %collective-permute-start.21) | collective-permute-done | bytes 131104 | tf_op jit(solution)/shard_map/ppermute | solution.py:33
  43.5 2.4 %collective-permute-done.22.refs_1_ = bf16[256,256]{1,0:T(8,128)(2,1)S(1)} collective-permute-done((bf16[256,256]{1,0:T(8,128)(2,1)S(1)}, bf16[256,256]{1,0:T(8,128)(2,1)S(1)}, u32[]{:S(2)}, u32[]{:S(2)}) %collective-permute-start.22) | collective-permute-done | bytes 131104 | tf_op jit(solution)/shard_map/ppermute | solution.py:33
  46.0 2.5 %collective-permute-start.24 = (bf16[128,256]{1,0:T(8,128)(2,1)S(1)}, bf16[128,256]{1,0:T(8,128)(2,1)S(1)}, u32[]{:S(2)}, u32[]{:S(2)}) collective-permute-start(bf16[128,256]{1,0:T(8,128)(2,1)S(1)} %get-tuple-element.73), channel_id=1, source_target_pairs={{0,8},{2,10},{4,12},{6,14},{8,0},{10,2},{12,4},{14,6},{16,24},{18,... | collective-permute-start | bytes 196616 | tf_op jit(solution)/shard_map/ppermute | solution.py:33
  48.5 4.0 %collective-permute-done.24.refs_0_ = bf16[128,256]{1,0:T(8,128)(2,1)S(1)} collective-permute-done((bf16[128,256]{1,0:T(8,128)(2,1)S(1)}, bf16[128,256]{1,0:T(8,128)(2,1)S(1)}, u32[]{:S(2)}, u32[]{:S(2)}) %collective-permute-start.24) | collective-permute-done | bytes 65568 | tf_op jit(solution)/shard_map/ppermute | solution.py:33
  52.5 2.2 %collective-permute-start.25 = (bf16[64,256]{1,0:T(8,128)(2,1)S(1)}, bf16[64,256]{1,0:T(8,128)(2,1)S(1)}, u32[]{:S(2)}, u32[]{:S(2)}) collective-permute-start(bf16[64,256]{1,0:T(8,128)(2,1)S(1)} %get-tuple-element.75), channel_id=1, source_target_pairs={{0,16},{2,18},{4,20},{6,22},{8,24},{10,26},{12,28},{14,30},{16,0},... | collective-permute-start | bytes 98312 | tf_op jit(solution)/shard_map/ppermute | solution.py:33
  55.1 7.0 %collective-permute-start.13 = (bf16[768,128]{1,0:T(8,128)(2,1)S(1)}, bf16[768,128]{1,0:T(8,128)(2,1)S(1)}, u32[]{:S(2)}, u32[]{:S(2)}) collective-permute-start(bf16[768,128]{1,0:T(8,128)(2,1)S(1)} %get-tuple-element.63), channel_id=1, source_target_pairs={{0,30},{2,0},{4,2},{6,4},{8,6},{10,8},{12,10},{14,12},{16,14},{18,... | collective-permute-start | bytes 589832 | tf_op jit(solution)/shard_map/ppermute | solution.py:28
  62.1 2.1 %collective-permute-start.26 = (bf16[64,256]{1,0:T(8,128)(2,1)S(1)}, bf16[64,256]{1,0:T(8,128)(2,1)S(1)}, u32[]{:S(2)}, u32[]{:S(2)}) collective-permute-start(bf16[64,256]{1,0:T(8,128)(2,1)S(1)} %kernel.32.have), channel_id=1, source_target_pairs={{0,16},{2,18},{4,20},{6,22},{8,24},{10,26},{12,28},{14,30},{16,0},... | collective-permute-start | bytes 98312 | tf_op jit(solution)/shard_map/ppermute | solution.py:33
  64.1 0.9 collective-permute-start.14
  65.1 9.7 %collective-permute-done.26.refs_0_ = bf16[64,256]{1,0:T(8,128)(2,1)S(1)} collective-permute-done((bf16[64,256]{1,0:T(8,128)(2,1)S(1)}, bf16[64,256]{1,0:T(8,128)(2,1)S(1)}, u32[]{:S(2)}, u32[]{:S(2)}) %collective-permute-start.26) | collective-permute-done | bytes 32800 | tf_op jit(solution)/shard_map/ppermute | solution.py:33
  75.1 7.3 %collective-permute-done.27.refs_0_ = bf16[128,256]{1,0:T(8,128)(2,1)S(1)} collective-permute-done((bf16[128,256]{1,0:T(8,128)(2,1)S(1)}, bf16[128,256]{1,0:T(8,128)(2,1)S(1)}, u32[]{:S(2)}, u32[]{:S(2)}) %collective-permute-start.27) | collective-permute-done | bytes 65568 | tf_op jit(solution)/shard_map/ppermute | solution.py:33
  82.5 0.8 collective-permute-done.15.dm
  83.3 2.7 %collective-permute-start.28 = (bf16[256,256]{1,0:T(8,128)(2,1)S(1)}, bf16[256,256]{1,0:T(8,128)(2,1)S(1)}, u32[]{:S(2)}, u32[]{:S(2)}) collective-permute-start(bf16[256,256]{1,0:T(8,128)(2,1)S(1)} %kernel.34.have), channel_id=1, source_target_pairs={{0,2},{2,0},{4,6},{6,4},{8,10},{10,8},{12,14},{14,12},{16,18},{18,... | collective-permute-start | bytes 393224 | tf_op jit(solution)/shard_map/ppermute | solution.py:33
  86.2 3.6 %collective-permute-done.30.refs_2_ = bf16[256,256]{1,0:T(8,128)(2,1)S(1)} collective-permute-done((bf16[256,256]{1,0:T(8,128)(2,1)S(1)}, bf16[256,256]{1,0:T(8,128)(2,1)S(1)}, u32[]{:S(2)}, u32[]{:S(2)}) %collective-permute-start.30) | collective-permute-done | bytes 131104 | tf_op jit(solution)/shard_map/ppermute | solution.py:33
  89.8 1.0 collective-permute-done.29.refs_1_
  93.5 6.9 %kernel.37 = (f32[384,384]{1,0:T(8,128)S(1)}, bf16[384,384]{1,0:T(8,128)(2,1)S(1)}, f32[2048,128]{1,0:T(8,128)S(1)}, bf16[2048,128]{1,0:T(8,128)(2,1)S(1)}, f32[...) custom-call(s32[1]{0:T(128)S(6)} %copy.9.live, s32[2,4]{1,0:T(2,128)S(1)} %bitcast.31, s32[4]{0:T(128)S(1)} %copy-done.5, ...), custom_call_target="tpu_custom_call" | custom-call | tf_op jit(solution)/shard_map/kernel/pallas_call | solution.py:236
  101.1 1.3 collective-permute-done.36.got
  102.8 2.4 %collective-permute-start.39 = (bf16[512,128]{1,0:T(8,128)(2,1)S(1)}, bf16[512,128]{1,0:T(8,128)(2,1)S(1)}, u32[]{:S(2)}, u32[]{:S(2)}) collective-permute-start(bf16[512,128]{1,0:T(8,128)(2,1)S(1)} %get-tuple-element.82), channel_id=1, source_target_pairs={{0,18},{2,20},{4,22},{6,24},{8,26},{10,28},{12,30},{14,0},{16,2},{... | collective-permute-start | bytes 393224 | tf_op jit(solution)/shard_map/ppermute | solution.py:28
  105.2 10.7 %collective-permute-done.39.diag = bf16[512,128]{1,0:T(8,128)(2,1)S(1)} collective-permute-done((bf16[512,128]{1,0:T(8,128)(2,1)S(1)}, bf16[512,128]{1,0:T(8,128)(2,1)S(1)}, u32[]{:S(2)}, u32[]{:S(2)}) %collective-permute-start.39) | collective-permute-done | bytes 131104 | tf_op jit(solution)/shard_map/ppermute | solution.py:28
  116.4 1.1 kernel.39
  117.6 4.3 %collective-permute-start.42 = (bf16[256,256]{1,0:T(8,128)(2,1)S(1)}, bf16[256,256]{1,0:T(8,128)(2,1)S(1)}, u32[]{:S(2)}, u32[]{:S(2)}) collective-permute-start(bf16[256,256]{1,0:T(8,128)(2,1)S(1)} %get-tuple-element.87), channel_id=1, source_target_pairs={{0,2},{2,0},{4,6},{6,4},{8,10},{10,8},{12,14},{14,12},{16,18},{18,... | collective-permute-start | bytes 393224 | tf_op jit(solution)/shard_map/ppermute | solution.py:33
  121.9 1.5 collective-permute-start.44
  123.4 2.8 %collective-permute-done.42.refs_0_ = bf16[256,256]{1,0:T(8,128)(2,1)S(1)} collective-permute-done((bf16[256,256]{1,0:T(8,128)(2,1)S(1)}, bf16[256,256]{1,0:T(8,128)(2,1)S(1)}, u32[]{:S(2)}, u32[]{:S(2)}) %collective-permute-start.42) | collective-permute-done | bytes 131104 | tf_op jit(solution)/shard_map/ppermute | solution.py:33
  126.2 4.1 %collective-permute-done.43.refs_1_ = bf16[256,256]{1,0:T(8,128)(2,1)S(1)} collective-permute-done((bf16[256,256]{1,0:T(8,128)(2,1)S(1)}, bf16[256,256]{1,0:T(8,128)(2,1)S(1)}, u32[]{:S(2)}, u32[]{:S(2)}) %collective-permute-start.43) | collective-permute-done | bytes 131104 | tf_op jit(solution)/shard_map/ppermute | solution.py:33
  130.8 4.0 %collective-permute-done.45.refs_0_ = bf16[128,256]{1,0:T(8,128)(2,1)S(1)} collective-permute-done((bf16[128,256]{1,0:T(8,128)(2,1)S(1)}, bf16[128,256]{1,0:T(8,128)(2,1)S(1)}, u32[]{:S(2)}, u32[]{:S(2)}) %collective-permute-start.45) | collective-permute-done | bytes 65568 | tf_op jit(solution)/shard_map/ppermute | solution.py:33
  134.8 0.5 collective-permute-start.46
  135.3 4.4 %collective-permute-done.46.refs_0_ = bf16[64,256]{1,0:T(8,128)(2,1)S(1)} collective-permute-done((bf16[64,256]{1,0:T(8,128)(2,1)S(1)}, bf16[64,256]{1,0:T(8,128)(2,1)S(1)}, u32[]{:S(2)}, u32[]{:S(2)}) %collective-permute-start.46) | collective-permute-done | bytes 32800 | tf_op jit(solution)/shard_map/ppermute | solution.py:33
  140.2 4.5 %collective-permute-done.47.refs_0_ = bf16[64,256]{1,0:T(8,128)(2,1)S(1)} collective-permute-done((bf16[64,256]{1,0:T(8,128)(2,1)S(1)}, bf16[64,256]{1,0:T(8,128)(2,1)S(1)}, u32[]{:S(2)}, u32[]{:S(2)}) %collective-permute-start.47) | collective-permute-done | bytes 32800 | tf_op jit(solution)/shard_map/ppermute | solution.py:33
  145.0 4.0 %collective-permute-done.48.refs_0_ = bf16[128,256]{1,0:T(8,128)(2,1)S(1)} collective-permute-done((bf16[128,256]{1,0:T(8,128)(2,1)S(1)}, bf16[128,256]{1,0:T(8,128)(2,1)S(1)}, u32[]{:S(2)}, u32[]{:S(2)}) %collective-permute-start.48) | collective-permute-done | bytes 65568 | tf_op jit(solution)/shard_map/ppermute | solution.py:33
  149.1 1.4 collective-permute-start.51
  150.8 1.8 %collective-permute-start.49 = (bf16[256,256]{1,0:T(8,128)(2,1)S(1)}, bf16[256,256]{1,0:T(8,128)(2,1)S(1)}, u32[]{:S(2)}, u32[]{:S(2)}) collective-permute-start(bf16[256,256]{1,0:T(8,128)(2,1)S(1)} %kernel.46.have), channel_id=1, source_target_pairs={{0,2},{2,0},{4,6},{6,4},{8,10},{10,8},{12,14},{14,12},{16,18},{18,... | collective-permute-start | bytes 393224 | tf_op jit(solution)/shard_map/ppermute | solution.py:33
  152.6 2.5 %collective-permute-done.51.refs_2_ = bf16[256,256]{1,0:T(8,128)(2,1)S(1)} collective-permute-done((bf16[256,256]{1,0:T(8,128)(2,1)S(1)}, bf16[256,256]{1,0:T(8,128)(2,1)S(1)}, u32[]{:S(2)}, u32[]{:S(2)}) %collective-permute-start.51) | collective-permute-done | bytes 131104 | tf_op jit(solution)/shard_map/ppermute | solution.py:33
  155.1 1.3 collective-permute-done.50.refs_1_
  156.4 1.1 kernel.47
  157.5 1.1 kernel.40
  (100 shorter events, 9.4 us)
Async XLA Ops:
  0.6 27.0 %collective-permute-start = (f32[2,8]{1,0:T(2,128)}, f32[2,8]{1,0:T(2,128)S(1)}, u32[]{:S(2)}, u32[]{:S(2)}) collective-permute-start(f32[2,8]{1,0:T(2,128)} %bitcast.32), channel_id=1, source_target_pairs={{0,1},{1,0},{2,3},{3,2},{4,5},{5,4},{6,7},{7,6},{8,9},{9,8},{10,11... | collective-permute-start | bytes 200 | tf_op jit(solution)/shard_map/ppermute | solution.py:37
  1.2 26.5 %collective-permute-start.7 = (f32[2,2,256,256]{3,2,1,0:T(8,128)}, f32[2,2,256,256]{3,2,1,0:T(8,128)S(1)}, u32[]{:S(2)}, u32[]{:S(2)}) collective-permute-start(f32[2,2,256,256]{3,2,1,0:T(8,128)} %pm.1), channel_id=1, source_target_pairs={{0,1},{1,0},{2,3},{3,2},{4,5},{5,4},{6,7},{7,6},{8,9},{9,8},{10,11... | collective-permute-start | bytes 3145736 | tf_op jit(solution)/shard_map/ppermute | solution.py:37
  2.7 16.4 %collective-permute-start.3 = (bf16[512,128]{1,0:T(8,128)(2,1)S(1)}, bf16[512,128]{1,0:T(8,128)(2,1)S(1)}, u32[]{:S(2)}, u32[]{:S(2)}) collective-permute-start(bf16[512,128]{1,0:T(8,128)(2,1)S(1)} %get-tuple-element.52), channel_id=1, source_target_pairs={{0,14},{2,16},{4,18},{6,20},{8,22},{10,24},{12,26},{14,28},{16,30}... | collective-permute-start | bytes 393224 | tf_op jit(solution)/shard_map/ppermute | solution.py:28
  7.6 11.4 %collective-permute-start.1 = (bf16[768,128]{1,0:T(8,128)(2,1)S(1)}, bf16[768,128]{1,0:T(8,128)(2,1)S(1)}, u32[]{:S(2)}, u32[]{:S(2)}) collective-permute-start(bf16[768,128]{1,0:T(8,128)(2,1)S(1)} %get-tuple-element.50), channel_id=1, source_target_pairs={{0,30},{2,0},{4,2},{6,4},{8,6},{10,8},{12,10},{14,12},{16,14},{18,... | collective-permute-start | bytes 589832 | tf_op jit(solution)/shard_map/ppermute | solution.py:28
  9.9 16.0 %collective-permute-start.2 = (bf16[768,128]{1,0:T(8,128)(2,1)S(1)}, bf16[768,128]{1,0:T(8,128)(2,1)S(1)}, u32[]{:S(2)}, u32[]{:S(2)}) collective-permute-start(bf16[768,128]{1,0:T(8,128)(2,1)S(1)} %get-tuple-element.51), channel_id=1, source_target_pairs={{0,16},{2,18},{4,20},{6,22},{8,24},{10,26},{12,28},{14,30},{16,0},... | collective-permute-start | bytes 589832 | tf_op jit(solution)/shard_map/ppermute | solution.py:28
  19.0 8.6 %collective-permute-start.6 = (bf16[512,128]{1,0:T(8,128)(2,1)S(1)}, bf16[512,128]{1,0:T(8,128)(2,1)S(1)}, u32[]{:S(2)}, u32[]{:S(2)}) collective-permute-start(bf16[512,128]{1,0:T(8,128)(2,1)S(1)} %collective-permute-done.3.dm), channel_id=1, source_target_pairs={{0,1},{1,0},{2,3},{3,2},{4,5},{5,4},{6,7},{7,6},{8,9},{9,8},{10,11... | collective-permute-start | bytes 393224 | tf_op jit(solution)/shard_map/ppermute | solution.py:37
  19.0 8.6 %collective-permute-start.4 = (bf16[768,128]{1,0:T(8,128)(2,1)S(1)}, bf16[768,128]{1,0:T(8,128)(2,1)S(1)}, u32[]{:S(2)}, u32[]{:S(2)}) collective-permute-start(bf16[768,128]{1,0:T(8,128)(2,1)S(1)} %collective-permute-done.1.rm), channel_id=1, source_target_pairs={{0,1},{1,0},{2,3},{3,2},{4,5},{5,4},{6,7},{7,6},{8,9},{9,8},{10,11... | collective-permute-start | bytes 589832 | tf_op jit(solution)/shard_map/ppermute | solution.py:37
  25.9 1.7 %collective-permute-start.5 = (bf16[768,128]{1,0:T(8,128)(2,1)S(1)}, bf16[768,128]{1,0:T(8,128)(2,1)S(1)}, u32[]{:S(2)}, u32[]{:S(2)}) collective-permute-start(bf16[768,128]{1,0:T(8,128)(2,1)S(1)} %collective-permute-done.2.bm), channel_id=1, source_target_pairs={{0,1},{1,0},{2,3},{3,2},{4,5},{5,4},{6,7},{7,6},{8,9},{9,8},{10,11... | collective-permute-start | bytes 589832 | tf_op jit(solution)/shard_map/ppermute | solution.py:37
  34.8 2.1 %collective-permute-start.20 = (bf16[2,2,256,256]{3,2,1,0:T(8,128)(2,1)S(1)}, bf16[2,2,256,256]{3,2,1,0:T(8,128)(2,1)S(1)}, u32[]{:S(2)}, u32[]{:S(2)}) collective-permute-start(bf16[2,2,256,256]{3,2,1,0:T(8,128)(2,1)S(1)} %get-tuple-element.67), channel_id=1, source_target_pairs={{0,1},{1,0},{2,3},{3,2},{4,5},{5,4},{6,7},{7,6},{8,9},{9,8},{10,11... | collective-permute-start | bytes 1572872 | tf_op jit(solution)/shard_map/ppermute | solution.py:37
  35.4 5.3 %collective-permute-start.9 = (bf16[2048,128]{1,0:T(8,128)(2,1)S(1)}, bf16[2048,128]{1,0:T(8,128)(2,1)S(1)}, u32[]{:S(2)}, u32[]{:S(2)}) collective-permute-start(bf16[2048,128]{1,0:T(8,128)(2,1)S(1)} %get-tuple-element.57), channel_id=1, source_target_pairs={{0,1},{1,0},{2,3},{3,2},{4,5},{5,4},{6,7},{7,6},{8,9},{9,8},{10,11... | collective-permute-start | bytes 1572872 | tf_op jit(solution)/shard_map/ppermute | solution.py:37
  37.0 6.4 %collective-permute-start.21 = (bf16[256,256]{1,0:T(8,128)(2,1)S(1)}, bf16[256,256]{1,0:T(8,128)(2,1)S(1)}, u32[]{:S(2)}, u32[]{:S(2)}) collective-permute-start(bf16[256,256]{1,0:T(8,128)(2,1)S(1)} %get-tuple-element.69), channel_id=1, source_target_pairs={{0,2},{2,0},{4,6},{6,4},{8,10},{10,8},{12,14},{14,12},{16,18},{18,... | collective-permute-start | bytes 393224 | tf_op jit(solution)/shard_map/ppermute | solution.py:33
  37.1 17.6 %collective-permute-start.8 = (bf16[384,384]{1,0:T(8,128)(2,1)S(1)}, bf16[384,384]{1,0:T(8,128)(2,1)S(1)}, u32[]{:S(2)}, u32[]{:S(2)}) collective-permute-start(bf16[384,384]{1,0:T(8,128)(2,1)S(1)} %get-tuple-element.55), channel_id=1, source_target_pairs={{0,1},{1,0},{2,3},{3,2},{4,5},{5,4},{6,7},{7,6},{8,9},{9,8},{10,11... | collective-permute-start | bytes 884744 | tf_op jit(solution)/shard_map/ppermute | solution.py:37
  37.5 8.3 %collective-permute-start.22 = (bf16[256,256]{1,0:T(8,128)(2,1)S(1)}, bf16[256,256]{1,0:T(8,128)(2,1)S(1)}, u32[]{:S(2)}, u32[]{:S(2)}) collective-permute-start(bf16[256,256]{1,0:T(8,128)(2,1)S(1)} %get-tuple-element.70), channel_id=1, source_target_pairs={{0,4},{2,6},{4,0},{6,2},{8,12},{10,14},{12,8},{14,10},{16,20},{18,... | collective-permute-start | bytes 393224 | tf_op jit(solution)/shard_map/ppermute | solution.py:33
  37.6 8.4 %collective-permute-start.23 = (bf16[256,256]{1,0:T(8,128)(2,1)S(1)}, bf16[256,256]{1,0:T(8,128)(2,1)S(1)}, u32[]{:S(2)}, u32[]{:S(2)}) collective-permute-start(bf16[256,256]{1,0:T(8,128)(2,1)S(1)} %get-tuple-element.71), channel_id=1, source_target_pairs={{0,6},{2,4},{4,2},{6,0},{8,14},{10,12},{12,10},{14,8},{16,22},{18,... | collective-permute-start | bytes 393224 | tf_op jit(solution)/shard_map/ppermute | solution.py:33
  40.8 14.0 %collective-permute-start.10 = (bf16[768,128]{1,0:T(8,128)(2,1)S(1)}, bf16[768,128]{1,0:T(8,128)(2,1)S(1)}, u32[]{:S(2)}, u32[]{:S(2)}) collective-permute-start(bf16[768,128]{1,0:T(8,128)(2,1)S(1)} %get-tuple-element.58), channel_id=1, source_target_pairs={{0,2},{2,4},{4,6},{6,8},{8,10},{10,12},{12,14},{14,16},{16,18},{18... | collective-permute-start | bytes 589832 | tf_op jit(solution)/shard_map/ppermute | solution.py:28
  43.5 11.3 %collective-permute-start.11 = (bf16[768,128]{1,0:T(8,128)(2,1)S(1)}, bf16[768,128]{1,0:T(8,128)(2,1)S(1)}, u32[]{:S(2)}, u32[]{:S(2)}) collective-permute-start(bf16[768,128]{1,0:T(8,128)(2,1)S(1)} %get-tuple-element.59), channel_id=1, source_target_pairs={{0,16},{2,18},{4,20},{6,22},{8,24},{10,26},{12,28},{14,30},{16,0},... | collective-permute-start | bytes 589832 | tf_op jit(solution)/shard_map/ppermute | solution.py:28
  45.9 8.8 %collective-permute-start.12 = (bf16[512,128]{1,0:T(8,128)(2,1)S(1)}, bf16[512,128]{1,0:T(8,128)(2,1)S(1)}, u32[]{:S(2)}, u32[]{:S(2)}) collective-permute-start(bf16[512,128]{1,0:T(8,128)(2,1)S(1)} %get-tuple-element.60), channel_id=1, source_target_pairs={{0,18},{2,20},{4,22},{6,24},{8,26},{10,28},{12,30},{14,0},{16,2},{... | collective-permute-start | bytes 393224 | tf_op jit(solution)/shard_map/ppermute | solution.py:28
  46.0 6.5 %collective-permute-start.24 = (bf16[128,256]{1,0:T(8,128)(2,1)S(1)}, bf16[128,256]{1,0:T(8,128)(2,1)S(1)}, u32[]{:S(2)}, u32[]{:S(2)}) collective-permute-start(bf16[128,256]{1,0:T(8,128)(2,1)S(1)} %get-tuple-element.73), channel_id=1, source_target_pairs={{0,8},{2,10},{4,12},{6,14},{8,0},{10,2},{12,4},{14,6},{16,24},{18,... | collective-permute-start | bytes 196616 | tf_op jit(solution)/shard_map/ppermute | solution.py:33
  52.5 9.6 %collective-permute-start.25 = (bf16[64,256]{1,0:T(8,128)(2,1)S(1)}, bf16[64,256]{1,0:T(8,128)(2,1)S(1)}, u32[]{:S(2)}, u32[]{:S(2)}) collective-permute-start(bf16[64,256]{1,0:T(8,128)(2,1)S(1)} %get-tuple-element.75), channel_id=1, source_target_pairs={{0,16},{2,18},{4,20},{6,22},{8,24},{10,26},{12,28},{14,30},{16,0},... | collective-permute-start | bytes 98312 | tf_op jit(solution)/shard_map/ppermute | solution.py:33
  55.1 28.2 %collective-permute-start.13 = (bf16[768,128]{1,0:T(8,128)(2,1)S(1)}, bf16[768,128]{1,0:T(8,128)(2,1)S(1)}, u32[]{:S(2)}, u32[]{:S(2)}) collective-permute-start(bf16[768,128]{1,0:T(8,128)(2,1)S(1)} %get-tuple-element.63), channel_id=1, source_target_pairs={{0,30},{2,0},{4,2},{6,4},{8,6},{10,8},{12,10},{14,12},{16,14},{18,... | collective-permute-start | bytes 589832 | tf_op jit(solution)/shard_map/ppermute | solution.py:28
  62.1 12.6 %collective-permute-start.26 = (bf16[64,256]{1,0:T(8,128)(2,1)S(1)}, bf16[64,256]{1,0:T(8,128)(2,1)S(1)}, u32[]{:S(2)}, u32[]{:S(2)}) collective-permute-start(bf16[64,256]{1,0:T(8,128)(2,1)S(1)} %kernel.32.have), channel_id=1, source_target_pairs={{0,16},{2,18},{4,20},{6,22},{8,24},{10,26},{12,28},{14,30},{16,0},... | collective-permute-start | bytes 98312 | tf_op jit(solution)/shard_map/ppermute | solution.py:33
  64.1 21.9 %collective-permute-start.14 = (bf16[768,128]{1,0:T(8,128)(2,1)S(1)}, bf16[768,128]{1,0:T(8,128)(2,1)S(1)}, u32[]{:S(2)}, u32[]{:S(2)}) collective-permute-start(bf16[768,128]{1,0:T(8,128)(2,1)S(1)} %get-tuple-element.64), channel_id=1, source_target_pairs={{0,16},{2,18},{4,20},{6,22},{8,24},{10,26},{12,28},{14,30},{16,0},... | collective-permute-start | bytes 589832 | tf_op jit(solution)/shard_map/ppermute | solution.py:28
  74.7 7.6 %collective-permute-start.27 = (bf16[128,256]{1,0:T(8,128)(2,1)S(1)}, bf16[128,256]{1,0:T(8,128)(2,1)S(1)}, u32[]{:S(2)}, u32[]{:S(2)}) collective-permute-start(bf16[128,256]{1,0:T(8,128)(2,1)S(1)} %kernel.33.have), channel_id=1, source_target_pairs={{0,8},{2,10},{4,12},{6,14},{8,0},{10,2},{12,4},{14,6},{16,24},{18,... | collective-permute-start | bytes 196616 | tf_op jit(solution)/shard_map/ppermute | solution.py:33
  74.8 8.5 %collective-permute-start.15 = (bf16[512,128]{1,0:T(8,128)(2,1)S(1)}, bf16[512,128]{1,0:T(8,128)(2,1)S(1)}, u32[]{:S(2)}, u32[]{:S(2)}) collective-permute-start(bf16[512,128]{1,0:T(8,128)(2,1)S(1)} %get-tuple-element.65), channel_id=1, source_target_pairs={{0,14},{2,16},{4,18},{6,20},{8,22},{10,24},{12,26},{14,28},{16,30}... | collective-permute-start | bytes 393224 | tf_op jit(solution)/shard_map/ppermute | solution.py:28
  82.4 7.4 %collective-permute-start.30 = (bf16[256,256]{1,0:T(8,128)(2,1)S(1)}, bf16[256,256]{1,0:T(8,128)(2,1)S(1)}, u32[]{:S(2)}, u32[]{:S(2)}) collective-permute-start(bf16[256,256]{1,0:T(8,128)(2,1)S(1)} %kernel.34.have), channel_id=1, source_target_pairs={{0,6},{2,4},{4,2},{6,0},{8,14},{10,12},{12,10},{14,8},{16,22},{18,... | collective-permute-start | bytes 393224 | tf_op jit(solution)/shard_map/ppermute | solution.py:33
  82.5 8.3 %collective-permute-start.29 = (bf16[256,256]{1,0:T(8,128)(2,1)S(1)}, bf16[256,256]{1,0:T(8,128)(2,1)S(1)}, u32[]{:S(2)}, u32[]{:S(2)}) collective-permute-start(bf16[256,256]{1,0:T(8,128)(2,1)S(1)} %kernel.34.have), channel_id=1, source_target_pairs={{0,4},{2,6},{4,0},{6,2},{8,12},{10,14},{12,8},{14,10},{16,20},{18,... | collective-permute-start | bytes 393224 | tf_op jit(solution)/shard_map/ppermute | solution.py:33
  83.3 7.5 %collective-permute-start.31 = (bf16[256,256]{1,0:T(8,128)(2,1)S(1)}, bf16[256,256]{1,0:T(8,128)(2,1)S(1)}, u32[]{:S(2)}, u32[]{:S(2)}) collective-permute-start(bf16[256,256]{1,0:T(8,128)(2,1)S(1)} %kernel.34.have), channel_id=1, source_target_pairs={{0,1},{1,0},{2,3},{3,2},{4,5},{5,4},{6,7},{7,6},{8,9},{9,8},{10,11... | collective-permute-start | bytes 393224 | tf_op jit(solution)/shard_map/ppermute | solution.py:37
  83.3 8.0 %collective-permute-start.28 = (bf16[256,256]{1,0:T(8,128)(2,1)S(1)}, bf16[256,256]{1,0:T(8,128)(2,1)S(1)}, u32[]{:S(2)}, u32[]{:S(2)}) collective-permute-start(bf16[256,256]{1,0:T(8,128)(2,1)S(1)} %kernel.34.have), channel_id=1, source_target_pairs={{0,2},{2,0},{4,6},{6,4},{8,10},{10,8},{12,14},{14,12},{16,18},{18,... | collective-permute-start | bytes 393224 | tf_op jit(solution)/shard_map/ppermute | solution.py:33
  86.0 7.4 %collective-permute-start.16 = (bf16[384,384]{1,0:T(8,128)(2,1)S(1)}, bf16[384,384]{1,0:T(8,128)(2,1)S(1)}, u32[]{:S(2)}, u32[]{:S(2)}) collective-permute-start(bf16[384,384]{1,0:T(8,128)(2,1)S(1)} %get-tuple-element.62.tm), channel_id=1, source_target_pairs={{0,1},{1,0},{2,3},{3,2},{4,5},{5,4},{6,7},{7,6},{8,9},{9,8},{10,11... | collective-permute-start | bytes 884744 | tf_op jit(solution)/shard_map/ppermute | solution.py:37
  90.8 2.7 %collective-permute-start.17 = (bf16[768,128]{1,0:T(8,128)(2,1)S(1)}, bf16[768,128]{1,0:T(8,128)(2,1)S(1)}, u32[]{:S(2)}, u32[]{:S(2)}) collective-permute-start(bf16[768,128]{1,0:T(8,128)(2,1)S(1)} %collective-permute-done.13.rm), channel_id=1, source_target_pairs={{0,1},{1,0},{2,3},{3,2},{4,5},{5,4},{6,7},{7,6},{8,9},{9,8},{10,11... | collective-permute-start | bytes 589832 | tf_op jit(solution)/shard_map/ppermute | solution.py:37
  91.3 2.2 %collective-permute-start.18 = (bf16[768,128]{1,0:T(8,128)(2,1)S(1)}, bf16[768,128]{1,0:T(8,128)(2,1)S(1)}, u32[]{:S(2)}, u32[]{:S(2)}) collective-permute-start(bf16[768,128]{1,0:T(8,128)(2,1)S(1)} %collective-permute-done.14.bm), channel_id=1, source_target_pairs={{0,1},{1,0},{2,3},{3,2},{4,5},{5,4},{6,7},{7,6},{8,9},{9,8},{10,11... | collective-permute-start | bytes 589832 | tf_op jit(solution)/shard_map/ppermute | solution.py:37
  100.4 2.0 %collective-permute-start.36 = (bf16[2048,128]{1,0:T(8,128)(2,1)S(1)}, bf16[2048,128]{1,0:T(8,128)(2,1)S(1)}, u32[]{:S(2)}, u32[]{:S(2)}) collective-permute-start(bf16[2048,128]{1,0:T(8,128)(2,1)S(1)} %get-tuple-element.79), channel_id=1, source_target_pairs={{0,1},{1,0},{2,3},{3,2},{4,5},{5,4},{6,7},{7,6},{8,9},{9,8},{10,11... | collective-permute-start | bytes 1572872 | tf_op jit(solution)/shard_map/ppermute | solution.py:37
  100.6 16.9 %collective-permute-start.41 = (bf16[2,2,256,256]{3,2,1,0:T(8,128)(2,1)S(1)}, bf16[2,2,256,256]{3,2,1,0:T(8,128)(2,1)S(1)}, u32[]{:S(2)}, u32[]{:S(2)}) collective-permute-start(bf16[2,2,256,256]{3,2,1,0:T(8,128)(2,1)S(1)} %get-tuple-element.85), channel_id=1, source_target_pairs={{0,1},{1,0},{2,3},{3,2},{4,5},{5,4},{6,7},{7,6},{8,9},{9,8},{10,11... | collective-permute-start | bytes 1572872 | tf_op jit(solution)/shard_map/ppermute | solution.py:37
  101.0 4.3 %collective-permute-start.35 = (bf16[384,384]{1,0:T(8,128)(2,1)S(1)}, bf16[384,384]{1,0:T(8,128)(2,1)S(1)}, u32[]{:S(2)}, u32[]{:S(2)}) collective-permute-start(bf16[384,384]{1,0:T(8,128)(2,1)S(1)} %get-tuple-element.77), channel_id=1, source_target_pairs={{0,1},{1,0},{2,3},{3,2},{4,5},{5,4},{6,7},{7,6},{8,9},{9,8},{10,11... | collective-permute-start | bytes 884744 | tf_op jit(solution)/shard_map/ppermute | solution.py:37
  102.5 13.5 %collective-permute-start.37 = (bf16[768,128]{1,0:T(8,128)(2,1)S(1)}, bf16[768,128]{1,0:T(8,128)(2,1)S(1)}, u32[]{:S(2)}, u32[]{:S(2)}) collective-permute-start(bf16[768,128]{1,0:T(8,128)(2,1)S(1)} %get-tuple-element.80), channel_id=1, source_target_pairs={{0,2},{2,4},{4,6},{6,8},{8,10},{10,12},{12,14},{14,16},{16,18},{18... | collective-permute-start | bytes 589832 | tf_op jit(solution)/shard_map/ppermute | solution.py:28
  102.8 13.7 %collective-permute-start.38 = (bf16[768,128]{1,0:T(8,128)(2,1)S(1)}, bf16[768,128]{1,0:T(8,128)(2,1)S(1)}, u32[]{:S(2)}, u32[]{:S(2)}) collective-permute-start(bf16[768,128]{1,0:T(8,128)(2,1)S(1)} %get-tuple-element.81), channel_id=1, source_target_pairs={{0,16},{2,18},{4,20},{6,22},{8,24},{10,26},{12,28},{14,30},{16,0},... | collective-permute-start | bytes 589832 | tf_op jit(solution)/shard_map/ppermute | solution.py:28
  102.8 13.2 %collective-permute-start.39 = (bf16[512,128]{1,0:T(8,128)(2,1)S(1)}, bf16[512,128]{1,0:T(8,128)(2,1)S(1)}, u32[]{:S(2)}, u32[]{:S(2)}) collective-permute-start(bf16[512,128]{1,0:T(8,128)(2,1)S(1)} %get-tuple-element.82), channel_id=1, source_target_pairs={{0,18},{2,20},{4,22},{6,24},{8,26},{10,28},{12,30},{14,0},{16,2},{... | collective-permute-start | bytes 393224 | tf_op jit(solution)/shard_map/ppermute | solution.py:28
  117.5 40.0 %collective-permute-start.40 = (f32[384,384]{1,0:T(8,128)S(1)}, f32[384,384]{1,0:T(8,128)S(1)}, u32[]{:S(2)}, u32[]{:S(2)}) collective-permute-start(f32[384,384]{1,0:T(8,128)S(1)} %get-tuple-element.83.state), channel_id=1, source_target_pairs={{0,1},{1,0},{2,3},{3,2},{4,5},{5,4},{6,7},{7,6},{8,9},{9,8},{10,11... | collective-permute-start | bytes 1769480 | tf_op jit(solution)/shard_map/ppermute | solution.py:37
  117.6 8.6 %collective-permute-start.42 = (bf16[256,256]{1,0:T(8,128)(2,1)S(1)}, bf16[256,256]{1,0:T(8,128)(2,1)S(1)}, u32[]{:S(2)}, u32[]{:S(2)}) collective-permute-start(bf16[256,256]{1,0:T(8,128)(2,1)S(1)} %get-tuple-element.87), channel_id=1, source_target_pairs={{0,2},{2,0},{4,6},{6,4},{8,10},{10,8},{12,14},{14,12},{16,18},{18,... | collective-permute-start | bytes 393224 | tf_op jit(solution)/shard_map/ppermute | solution.py:33
  121.9 8.4 %collective-permute-start.43 = (bf16[256,256]{1,0:T(8,128)(2,1)S(1)}, bf16[256,256]{1,0:T(8,128)(2,1)S(1)}, u32[]{:S(2)}, u32[]{:S(2)}) collective-permute-start(bf16[256,256]{1,0:T(8,128)(2,1)S(1)} %get-tuple-element.88), channel_id=1, source_target_pairs={{0,4},{2,6},{4,0},{6,2},{8,12},{10,14},{12,8},{14,10},{16,20},{18,... | collective-permute-start | bytes 393224 | tf_op jit(solution)/shard_map/ppermute | solution.py:33
  121.9 8.4 %collective-permute-start.44 = (bf16[256,256]{1,0:T(8,128)(2,1)S(1)}, bf16[256,256]{1,0:T(8,128)(2,1)S(1)}, u32[]{:S(2)}, u32[]{:S(2)}) collective-permute-start(bf16[256,256]{1,0:T(8,128)(2,1)S(1)} %get-tuple-element.89), channel_id=1, source_target_pairs={{0,6},{2,4},{4,2},{6,0},{8,14},{10,12},{12,10},{14,8},{16,22},{18,... | collective-permute-start | bytes 393224 | tf_op jit(solution)/shard_map/ppermute | solution.py:33
  130.4 4.3 %collective-permute-start.45 = (bf16[128,256]{1,0:T(8,128)(2,1)S(1)}, bf16[128,256]{1,0:T(8,128)(2,1)S(1)}, u32[]{:S(2)}, u32[]{:S(2)}) collective-permute-start(bf16[128,256]{1,0:T(8,128)(2,1)S(1)} %get-tuple-element.91), channel_id=1, source_target_pairs={{0,8},{2,10},{4,12},{6,14},{8,0},{10,2},{12,4},{14,6},{16,24},{18,... | collective-permute-start | bytes 196616 | tf_op jit(solution)/shard_map/ppermute | solution.py:33
  134.8 5.0 %collective-permute-start.46 = (bf16[64,256]{1,0:T(8,128)(2,1)S(1)}, bf16[64,256]{1,0:T(8,128)(2,1)S(1)}, u32[]{:S(2)}, u32[]{:S(2)}) collective-permute-start(bf16[64,256]{1,0:T(8,128)(2,1)S(1)} %get-tuple-element.93), channel_id=1, source_target_pairs={{0,16},{2,18},{4,20},{6,22},{8,24},{10,26},{12,28},{14,30},{16,0},... | collective-permute-start | bytes 98312 | tf_op jit(solution)/shard_map/ppermute | solution.py:33
  139.8 5.0 %collective-permute-start.47 = (bf16[64,256]{1,0:T(8,128)(2,1)S(1)}, bf16[64,256]{1,0:T(8,128)(2,1)S(1)}, u32[]{:S(2)}, u32[]{:S(2)}) collective-permute-start(bf16[64,256]{1,0:T(8,128)(2,1)S(1)} %kernel.44.have), channel_id=1, source_target_pairs={{0,16},{2,18},{4,20},{6,22},{8,24},{10,26},{12,28},{14,30},{16,0},... | collective-permute-start | bytes 98312 | tf_op jit(solution)/shard_map/ppermute | solution.py:33
  144.7 4.3 %collective-permute-start.48 = (bf16[128,256]{1,0:T(8,128)(2,1)S(1)}, bf16[128,256]{1,0:T(8,128)(2,1)S(1)}, u32[]{:S(2)}, u32[]{:S(2)}) collective-permute-start(bf16[128,256]{1,0:T(8,128)(2,1)S(1)} %kernel.45.have), channel_id=1, source_target_pairs={{0,8},{2,10},{4,12},{6,14},{8,0},{10,2},{12,4},{14,6},{16,24},{18,... | collective-permute-start | bytes 196616 | tf_op jit(solution)/shard_map/ppermute | solution.py:33
  149.1 6.0 %collective-permute-start.51 = (bf16[256,256]{1,0:T(8,128)(2,1)S(1)}, bf16[256,256]{1,0:T(8,128)(2,1)S(1)}, u32[]{:S(2)}, u32[]{:S(2)}) collective-permute-start(bf16[256,256]{1,0:T(8,128)(2,1)S(1)} %kernel.46.have), channel_id=1, source_target_pairs={{0,6},{2,4},{4,2},{6,0},{8,14},{10,12},{12,10},{14,8},{16,22},{18,... | collective-permute-start | bytes 393224 | tf_op jit(solution)/shard_map/ppermute | solution.py:33
  150.5 5.9 %collective-permute-start.50 = (bf16[256,256]{1,0:T(8,128)(2,1)S(1)}, bf16[256,256]{1,0:T(8,128)(2,1)S(1)}, u32[]{:S(2)}, u32[]{:S(2)}) collective-permute-start(bf16[256,256]{1,0:T(8,128)(2,1)S(1)} %kernel.46.have), channel_id=1, source_target_pairs={{0,4},{2,6},{4,0},{6,2},{8,12},{10,14},{12,8},{14,10},{16,20},{18,... | collective-permute-start | bytes 393224 | tf_op jit(solution)/shard_map/ppermute | solution.py:33
  150.8 5.6 %collective-permute-start.49 = (bf16[256,256]{1,0:T(8,128)(2,1)S(1)}, bf16[256,256]{1,0:T(8,128)(2,1)S(1)}, u32[]{:S(2)}, u32[]{:S(2)}) collective-permute-start(bf16[256,256]{1,0:T(8,128)(2,1)S(1)} %kernel.46.have), channel_id=1, source_target_pairs={{0,2},{2,0},{4,6},{6,4},{8,10},{10,8},{12,14},{14,12},{16,18},{18,... | collective-permute-start | bytes 393224 | tf_op jit(solution)/shard_map/ppermute | solution.py:33
  (10 other events, 27.0 us)

commit v4 on v3

--- a/solution.py
+++ b/solution.py
@@ -75,8 +75,8 @@
 def patch_kernel(
     live, corner, kind, wm, wo,
     tm, rm, bm, dm, to, ro, bo, do, meas, pm, po, tall, wide_table,
-    own_keep, own_send, edge_keep, edge_send, pgm, pgo,
-    frame, grad, psi, xs, ts, orr, oii, term, acc,
+    grad, own_send, edge_send, acc, pgo,
+    frame, psi, xs, ts, orr, oii, term,
 ):
     n = pm.shape[-1]
     t = tm.shape[-1]
@@ -218,17 +218,14 @@
         return carry
 
     lax.fori_loop(0, meas.shape[0], slot_body, 0)
-    own_keep[...] = grad[me, pl.ds(0, t), pl.ds(0, t)]
     own_send[...] = grad[1 - me, pl.ds(0, t), pl.ds(0, t)].astype(bf16)
     base = 0
     for _, top, left, high, wide in blocks(t, n, (None,) * 3):
         for k in range(wide // LANES):
             rows, lanes = pl.ds(top, high), pl.ds(left + k * LANES, LANES)
-            edge_keep[pl.ds(base, high), :] = grad[me, rows, lanes]
             edge_send[pl.ds(base, high), :] = grad[1 - me, rows, lanes].astype(bf16)
             base += high
     for m in range(half):
-        pgm[m] = acc[m]
         pgo[m] = acc[half + m].astype(bf16)
 
 
@@ -283,17 +280,15 @@
     return call(
         patch_kernel,
         (
-            ((t, t), f32),
+            ((2, f, f), f32),
             ((t, t), bf16),
-            ((rows, LANES), f32),
             ((rows, LANES), bf16),
-            (pm.shape, f32),
+            ((modes, *pm.shape[1:]), f32),
             (pm.shape, bf16),
         ),
         live, corner, kind, wm, wo, *mine, *other, meas, pm, po, tall, wide,
         smem=5,
         scratch=[
-            pltpu.VMEM((2, f, f), f32),
             pltpu.VMEM((2, f, f), f32),
             pltpu.VMEM((2, modes * n, n), f32),
             pltpu.VMEM((modes, 2, n, n), bf16),
@@ -301,9 +296,8 @@
             pltpu.VMEM((n, n), f32),
             pltpu.VMEM((n, n), f32),
             pltpu.VMEM((2, n, n), f32),
-            pltpu.VMEM((modes, 2, n, n), f32),
         ],
-        limit=24 * 1024 * 1024,
+        limit=20 * 1024 * 1024,
     )
 
 
@@ -335,22 +329,27 @@
     return call(enter_kernel, outs, obj)
 
 
-def margin_kernel(keep, got, right, low, diag):
+def margin_kernel(t, n, grad, got, right, low, diag):
+    me = lax.axis_index("mode")
     base = 0
-    for out in (right, low, diag):
-        rows = pl.ds(base, out.shape[0])
-        out[...] = (keep[rows, :] + got[rows, :].astype(f32)).astype(bf16)
-        base += out.shape[0]
-
-
-def margins(keep, got, t, n):
-    return call(margin_kernel, edge_shapes(t, n), keep, got)
-
-
-def update_kernel(state, keep, got, right, low, diag, new, half, hr, hl, hd):
+    for out, top, left, high, wide in blocks(t, n, (right, low, diag)):
+        for k in range(wide // LANES):
+            value = grad[me, pl.ds(top, high), pl.ds(left + k * LANES, LANES)]
+            value = value + got[pl.ds(base, high), :].astype(f32)
+            out[pl.ds(k * high, high), :] = value.astype(bf16)
+            base += high
+
+
+def margins(grad, got, t, n):
+    kernel = functools.partial(margin_kernel, t, n)
+    return call(kernel, edge_shapes(t, n), grad, got)
+
+
+def update_kernel(state, grad, got, right, low, diag, new, half, hr, hl, hd):
     t = state.shape[0]
     n = low.shape[0] * LANES // t
-    new[...] = keep[...] + got[...].astype(f32)
+    own = grad[lax.axis_index("mode"), pl.ds(0, t), pl.ds(0, t)]
+    new[...] = own + got[...].astype(f32)
     for ref, _, _, high, wide in blocks(t, n, (right, low, diag)):
         for k in range(wide // LANES):
             lanes = pl.ds(k * LANES, LANES)
@@ -383,7 +382,7 @@
 def digits(peers):
     out, shift = [], 0
     while 1 << shift < peers:
-        radix = 4 if shift == 0 and peers >= 4 else 2
+        radix = 4 if (4 << shift) <= peers else 2
         out.append((shift, radix))
         shift += radix.bit_length() - 1
     return out
@@ -444,9 +443,9 @@
     n = keep.shape[-1]
     stages = digits(lax.axis_size("tile"))
     shift, radix = stages[0]
-    keep = keep.reshape(radix, -1, n)
-    got = got.reshape(keep.shape)
-    rows = keep.shape[1]
+    got = got.reshape(radix, -1, n)
+    rows = got.shape[1]
+    keep = keep.reshape(-1, rows, n)
     own, *sends = call(
         functools.partial(first_kernel, (shift, radix)),
         (((rows, n), f32),) + (((rows, n), bf16),) * (radix - 1),
@@ -505,17 +504,17 @@
         right = shifted(edges[0], -1)
         mine = (half, right, low, diag)
         other = (rest, swapped(right), swapped(low), swapped(diag))
-        own_keep, own_send, edge_keep, edge_send, pgm, pgo = patches(
+        grad, own_send, edge_send, acc, pgo = patches(
             counts, spots, weight_index, wm, wo, mine, other, meas, pm, po, tall, wide
         )
         edge_got = swapped(edge_send)
-        right, low, diag = margins(edge_keep, edge_got, t, n)
+        right, low, diag = margins(grad, edge_got, t, n)
         low = shifted(low, GC)
         diag = shifted(diag, GC + 1)
         right = shifted(right, 1)
-        pieces = probe_sum(pgm, swapped(pgo))
+        pieces = probe_sum(acc, swapped(pgo))
         own_got = swapped(own_send)
-        state, half, *edges = update(state, own_keep, own_got, right, low, diag)
+        state, half, *edges = update(state, grad, own_got, right, low, diag)
         pm = probe_step(rate, pm, pieces)
         if sweep < ITERS - 1:
             rest = swapped(half)

time: 159 us -> 160 us (level)
  starting transfers between devices: 48.5 us -> 64.5 us
  waiting for transfers between devices: 86.4 us -> 71.8 us
    ppermute x20 -> x24, waiting for transfers between devices: 57.8 us -> 36.5 us  [flipped(): return lax.ppermute(array, 'tile', [(i, i ^ mask) for i in range(peers)])]
    ppermute x20 -> x24, starting transfers between devices: 23.9 us -> 38.5 us  [flipped(): return lax.ppermute(array, 'tile', [(i, i ^ mask) for i in range(peers)])]
    ppermute x12, waiting for transfers between devices: 24.6 us -> 31.4 us  [shifted(): lax.ppermute(array, 'tile', [(i, (i + by) % peers) for i in range(peers)])]
    pallas_call x24 -> x20, Pallas kernels: 19.3 us -> 18.9 us  [call(): pl.pallas_call(kernel, out_shape=tuple((jax.ShapeDtypeStruct(shape, dtype...]
  transfers between devices with their start and end apart: 52 -> 56, of which waited for: 25 -> 25; matrix products, arithmetic and copies ran while one was open for 1% -> 1% of each run, Pallas kernels for 3% -> 3%
where the time goes in v4:
time: 160 us; the launch traced here: 159 us
  waiting for transfers between devices  71.8 us (45%)
  starting transfers between devices  64.5 us (40%)
  Pallas kernels  18.9 us (12%)
  between operations  1.63 us (1%)
    ppermute x24, starting transfers between devices, flipped(): return lax.ppermute(array, 'tile', [(i, i ^ mask) for i in range(peers)])  38.5 us
    ppermute x24, waiting for transfers between devices, flipped(): return lax.ppermute(array, 'tile', [(i, i ^ mask) for i in range(peers)])  36.5 us
    ppermute x12, waiting for transfers between devices, shifted(): lax.ppermute(array, 'tile', [(i, (i + by) % peers) for i in range(peers)])  31.4 us
    ppermute x12, starting transfers between devices, shifted(): lax.ppermute(array, 'tile', [(i, (i + by) % peers) for i in range(peers)])  21.8 us
    pallas_call x20, Pallas kernels, call(): pl.pallas_call(kernel, out_shape=tuple((jax.ShapeDtypeStruct(shape, dtype...  18.9 us
    ppermute x20, starting transfers between devices, swapped(): return lax.ppermute(array, 'mode', [(0, 1), (1, 0)])  4.3 us
    ppermute x20, waiting for transfers between devices, swapped(): return lax.ppermute(array, 'mode', [(0, 1), (1, 0)])  3.88 us
  transfers between devices with their start and end apart: 56, of which 25 were waited for; matrix products, arithmetic and copies ran while one was open for 1% of the time, Pallas kernels for 3%

profile of v4, /device:TPU:0, one launch (start us, length us, event | category | flops | bytes accessed | tf_op | source)
XLA Modules:
  0.0 159.5 jit_solution(8913575887201708045)
XLA Ops:
  1.3 1.3 copy-done.1
  2.7 4.9 %collective-permute-start.3 = (bf16[512,128]{1,0:T(8,128)(2,1)S(1)}, bf16[512,128]{1,0:T(8,128)(2,1)S(1)}, u32[]{:S(2)}, u32[]{:S(2)}) collective-permute-start(bf16[512,128]{1,0:T(8,128)(2,1)S(1)} %get-tuple-element.50), channel_id=1, source_target_pairs={{0,14},{2,16},{4,18},{6,20},{8,22},{10,24},{12,26},{14,28},{16,30}... | collective-permute-start | bytes 393224 | tf_op jit(solution)/shard_map/ppermute | solution.py:28
  7.6 2.3 %collective-permute-start.1 = (bf16[768,128]{1,0:T(8,128)(2,1)S(1)}, bf16[768,128]{1,0:T(8,128)(2,1)S(1)}, u32[]{:S(2)}, u32[]{:S(2)}) collective-permute-start(bf16[768,128]{1,0:T(8,128)(2,1)S(1)} %get-tuple-element.48), channel_id=1, source_target_pairs={{0,30},{2,0},{4,2},{6,4},{8,6},{10,8},{12,10},{14,12},{16,14},{18,... | collective-permute-start | bytes 589832 | tf_op jit(solution)/shard_map/ppermute | solution.py:28
  9.9 1.7 %collective-permute-start.2 = (bf16[768,128]{1,0:T(8,128)(2,1)S(1)}, bf16[768,128]{1,0:T(8,128)(2,1)S(1)}, u32[]{:S(2)}, u32[]{:S(2)}) collective-permute-start(bf16[768,128]{1,0:T(8,128)(2,1)S(1)} %get-tuple-element.49), channel_id=1, source_target_pairs={{0,16},{2,18},{4,20},{6,22},{8,24},{10,26},{12,28},{14,30},{16,0},... | collective-permute-start | bytes 589832 | tf_op jit(solution)/shard_map/ppermute | solution.py:28
  12.9 6.1 %collective-permute-done.3.dm = bf16[512,128]{1,0:T(8,128)(2,1)S(1)} collective-permute-done((bf16[512,128]{1,0:T(8,128)(2,1)S(1)}, bf16[512,128]{1,0:T(8,128)(2,1)S(1)}, u32[]{:S(2)}, u32[]{:S(2)}) %collective-permute-start.3) | collective-permute-done | bytes 131104 | tf_op jit(solution)/shard_map/ppermute | solution.py:28
  19.5 6.4 %collective-permute-done.2.bm = bf16[768,128]{1,0:T(8,128)(2,1)S(1)} collective-permute-done((bf16[768,128]{1,0:T(8,128)(2,1)S(1)}, bf16[768,128]{1,0:T(8,128)(2,1)S(1)}, u32[]{:S(2)}, u32[]{:S(2)}) %collective-permute-start.2) | collective-permute-done | bytes 196640 | tf_op jit(solution)/shard_map/ppermute | solution.py:28
  26.7 0.9 kernel.21.meas
  27.7 6.7 %kernel.22 = (f32[2,640,640]{2,1,0:T(8,128)S(1)}, bf16[384,384]{1,0:T(8,128)(2,1)S(1)}, bf16[2048,128]{1,0:T(8,128)(2,1)S(1)}, f32[4,2,256,256]{3,2,1,0:T(8,128)S(1)}, bf16[2,2,256,256]{3,2,1,0:T(8,128)(2,1)S(1)}) custom-call(s32[1]{0:T(128)S(6)} %copy.9.live, s32[2,4]{1,0:T(2,128)S(1)} %bitcast.30, s32[4]{0:T(128)S(1)} %copy-done.5, f32[2,8]{1,0:T(2,128)S(1)} %bitcast.33, ...), custom_call_target="tpu_custom_call" | custom-call | tf_op jit(solution)/shard_map/kernel/pallas_call | solution.py:233
  35.1 1.5 collective-permute-done.20
  37.1 3.1 %collective-permute-start.23 = (bf16[256,256]{1,0:T(8,128)(2,1)S(1)}, bf16[256,256]{1,0:T(8,128)(2,1)S(1)}, u32[]{:S(2)}, u32[]{:S(2)}) collective-permute-start(bf16[256,256]{1,0:T(8,128)(2,1)S(1)} %get-tuple-element.68), channel_id=1, source_target_pairs={{0,6},{2,4},{4,2},{6,0},{8,14},{10,12},{12,10},{14,8},{16,22},{18,... | collective-permute-start | bytes 393224 | tf_op jit(solution)/shard_map/ppermute | solution.py:33
  40.8 2.3 %collective-permute-done.21.refs_0_ = bf16[256,256]{1,0:T(8,128)(2,1)S(1)} collective-permute-done((bf16[256,256]{1,0:T(8,128)(2,1)S(1)}, bf16[256,256]{1,0:T(8,128)(2,1)S(1)}, u32[]{:S(2)}, u32[]{:S(2)}) %collective-permute-start.21) | collective-permute-done | bytes 131104 | tf_op jit(solution)/shard_map/ppermute | solution.py:33
  43.1 2.4 %collective-permute-done.22.refs_1_ = bf16[256,256]{1,0:T(8,128)(2,1)S(1)} collective-permute-done((bf16[256,256]{1,0:T(8,128)(2,1)S(1)}, bf16[256,256]{1,0:T(8,128)(2,1)S(1)}, u32[]{:S(2)}, u32[]{:S(2)}) %collective-permute-start.22) | collective-permute-done | bytes 131104 | tf_op jit(solution)/shard_map/ppermute | solution.py:33
  45.6 2.5 %collective-permute-start.24 = (bf16[64,256]{1,0:T(8,128)(2,1)S(1)}, bf16[64,256]{1,0:T(8,128)(2,1)S(1)}, u32[]{:S(2)}, u32[]{:S(2)}) collective-permute-start(bf16[64,256]{1,0:T(8,128)(2,1)S(1)} %get-tuple-element.70), channel_id=1, source_target_pairs={{0,8},{2,10},{4,12},{6,14},{8,0},{10,2},{12,4},{14,6},{16,24},{18,... | collective-permute-start | bytes 98312 | tf_op jit(solution)/shard_map/ppermute | solution.py:33
  48.1 3.0 %collective-permute-done.24.refs_0_ = bf16[64,256]{1,0:T(8,128)(2,1)S(1)} collective-permute-done((bf16[64,256]{1,0:T(8,128)(2,1)S(1)}, bf16[64,256]{1,0:T(8,128)(2,1)S(1)}, u32[]{:S(2)}, u32[]{:S(2)}) %collective-permute-start.24) | collective-permute-done | bytes 32800 | tf_op jit(solution)/shard_map/ppermute | solution.py:33
  51.0 2.9 %collective-permute-start.25 = (bf16[64,256]{1,0:T(8,128)(2,1)S(1)}, bf16[64,256]{1,0:T(8,128)(2,1)S(1)}, u32[]{:S(2)}, u32[]{:S(2)}) collective-permute-start(bf16[64,256]{1,0:T(8,128)(2,1)S(1)} %get-tuple-element.71), channel_id=1, source_target_pairs={{0,16},{2,18},{4,20},{6,22},{8,24},{10,26},{12,28},{14,30},{16,0},... | collective-permute-start | bytes 98312 | tf_op jit(solution)/shard_map/ppermute | solution.py:33
  53.9 3.4 %collective-permute-done.25.refs_1_ = bf16[64,256]{1,0:T(8,128)(2,1)S(1)} collective-permute-done((bf16[64,256]{1,0:T(8,128)(2,1)S(1)}, bf16[64,256]{1,0:T(8,128)(2,1)S(1)}, u32[]{:S(2)}, u32[]{:S(2)}) %collective-permute-start.25) | collective-permute-done | bytes 32800 | tf_op jit(solution)/shard_map/ppermute | solution.py:33
  57.2 2.6 %collective-permute-start.26 = (bf16[64,256]{1,0:T(8,128)(2,1)S(1)}, bf16[64,256]{1,0:T(8,128)(2,1)S(1)}, u32[]{:S(2)}, u32[]{:S(2)}) collective-permute-start(bf16[64,256]{1,0:T(8,128)(2,1)S(1)} %get-tuple-element.72), channel_id=1, source_target_pairs={{0,24},{2,26},{4,28},{6,30},{8,16},{10,18},{12,20},{14,22},{16,8},... | collective-permute-start | bytes 98312 | tf_op jit(solution)/shard_map/ppermute | solution.py:33
  59.9 3.1 %collective-permute-done.26.refs_2_ = bf16[64,256]{1,0:T(8,128)(2,1)S(1)} collective-permute-done((bf16[64,256]{1,0:T(8,128)(2,1)S(1)}, bf16[64,256]{1,0:T(8,128)(2,1)S(1)}, u32[]{:S(2)}, u32[]{:S(2)}) %collective-permute-start.26) | collective-permute-done | bytes 32800 | tf_op jit(solution)/shard_map/ppermute | solution.py:33
  63.0 2.7 %collective-permute-start.29 = (bf16[64,256]{1,0:T(8,128)(2,1)S(1)}, bf16[64,256]{1,0:T(8,128)(2,1)S(1)}, u32[]{:S(2)}, u32[]{:S(2)}) collective-permute-start(bf16[64,256]{1,0:T(8,128)(2,1)S(1)} %kernel.27.have), channel_id=1, source_target_pairs={{0,24},{2,26},{4,28},{6,30},{8,16},{10,18},{12,20},{14,22},{16,8},... | collective-permute-start | bytes 98312 | tf_op jit(solution)/shard_map/ppermute | solution.py:33
  65.7 1.7 %collective-permute-start.27 = (bf16[64,256]{1,0:T(8,128)(2,1)S(1)}, bf16[64,256]{1,0:T(8,128)(2,1)S(1)}, u32[]{:S(2)}, u32[]{:S(2)}) collective-permute-start(bf16[64,256]{1,0:T(8,128)(2,1)S(1)} %kernel.27.have), channel_id=1, source_target_pairs={{0,8},{2,10},{4,12},{6,14},{8,0},{10,2},{12,4},{14,6},{16,24},{18,... | collective-permute-start | bytes 98312 | tf_op jit(solution)/shard_map/ppermute | solution.py:33
  67.7 6.7 %collective-permute-start.15 = (bf16[512,128]{1,0:T(8,128)(2,1)S(1)}, bf16[512,128]{1,0:T(8,128)(2,1)S(1)}, u32[]{:S(2)}, u32[]{:S(2)}) collective-permute-start(bf16[512,128]{1,0:T(8,128)(2,1)S(1)} %get-tuple-element.62), channel_id=1, source_target_pairs={{0,14},{2,16},{4,18},{6,20},{8,22},{10,24},{12,26},{14,28},{16,30}... | collective-permute-start | bytes 393224 | tf_op jit(solution)/shard_map/ppermute | solution.py:28
  74.6 3.0 %collective-permute-start.32 = (bf16[256,256]{1,0:T(8,128)(2,1)S(1)}, bf16[256,256]{1,0:T(8,128)(2,1)S(1)}, u32[]{:S(2)}, u32[]{:S(2)}) collective-permute-start(bf16[256,256]{1,0:T(8,128)(2,1)S(1)} %kernel.28.have), channel_id=1, source_target_pairs={{0,6},{2,4},{4,2},{6,0},{8,14},{10,12},{12,10},{14,8},{16,22},{18,... | collective-permute-start | bytes 393224 | tf_op jit(solution)/shard_map/ppermute | solution.py:33
  78.2 5.5 %collective-permute-start.13 = (bf16[768,128]{1,0:T(8,128)(2,1)S(1)}, bf16[768,128]{1,0:T(8,128)(2,1)S(1)}, u32[]{:S(2)}, u32[]{:S(2)}) collective-permute-start(bf16[768,128]{1,0:T(8,128)(2,1)S(1)} %get-tuple-element.60), channel_id=1, source_target_pairs={{0,30},{2,0},{4,2},{6,4},{8,6},{10,8},{12,10},{14,12},{16,14},{18,... | collective-permute-start | bytes 589832 | tf_op jit(solution)/shard_map/ppermute | solution.py:28
  84.5 4.2 %collective-permute-done.30.refs_0_ = bf16[256,256]{1,0:T(8,128)(2,1)S(1)} collective-permute-done((bf16[256,256]{1,0:T(8,128)(2,1)S(1)}, bf16[256,256]{1,0:T(8,128)(2,1)S(1)}, u32[]{:S(2)}, u32[]{:S(2)}) %collective-permute-start.30) | collective-permute-done | bytes 131104 | tf_op jit(solution)/shard_map/ppermute | solution.py:33
  89.2 5.7 %collective-permute-done.14.bm = bf16[768,128]{1,0:T(8,128)(2,1)S(1)} collective-permute-done((bf16[768,128]{1,0:T(8,128)(2,1)S(1)}, bf16[768,128]{1,0:T(8,128)(2,1)S(1)}, u32[]{:S(2)}, u32[]{:S(2)}) %collective-permute-start.14) | collective-permute-done | bytes 196640 | tf_op jit(solution)/shard_map/ppermute | solution.py:28
  95.5 0.9 collective-permute-done.34.refs_0_
  96.7 6.7 %kernel.31 = (f32[2,640,640]{2,1,0:T(8,128)S(1)}, bf16[384,384]{1,0:T(8,128)(2,1)S(1)}, bf16[2048,128]{1,0:T(8,128)(2,1)S(1)}, f32[4,2,256,256]{3,2,1,0:T(8,128)S(1)}, bf16[2,2,256,256]{3,2,1,0:T(8,128)(2,1)S(1)}) custom-call(s32[1]{0:T(128)S(6)} %copy.9.live, s32[2,4]{1,0:T(2,128)S(1)} %bitcast.31, s32[4]{0:T(128)S(1)} %copy-done.5, f32[2,8]{1,0:T(2,128)S(1)} %bitcast.34, ...), custom_call_target="tpu_custom_call" | custom-call | tf_op jit(solution)/shard_map/kernel/pallas_call | solution.py:233
  104.2 1.2 collective-permute-done.38.got
  105.9 13.2 %collective-permute-done.41.diag = bf16[512,128]{1,0:T(8,128)(2,1)S(1)} collective-permute-done((bf16[512,128]{1,0:T(8,128)(2,1)S(1)}, bf16[512,128]{1,0:T(8,128)(2,1)S(1)}, u32[]{:S(2)}, u32[]{:S(2)}) %collective-permute-start.41) | collective-permute-done | bytes 131104 | tf_op jit(solution)/shard_map/ppermute | solution.py:28
  119.1 1.1 kernel.33
  120.3 4.2 %collective-permute-start.44 = (bf16[256,256]{1,0:T(8,128)(2,1)S(1)}, bf16[256,256]{1,0:T(8,128)(2,1)S(1)}, u32[]{:S(2)}, u32[]{:S(2)}) collective-permute-start(bf16[256,256]{1,0:T(8,128)(2,1)S(1)} %get-tuple-element.83), channel_id=1, source_target_pairs={{0,2},{2,0},{4,6},{6,4},{8,10},{10,8},{12,14},{14,12},{16,18},{18,... | collective-permute-start | bytes 393224 | tf_op jit(solution)/shard_map/ppermute | solution.py:33
  124.6 1.1 collective-permute-start.45
  126.1 2.8 %collective-permute-done.44.refs_0_ = bf16[256,256]{1,0:T(8,128)(2,1)S(1)} collective-permute-done((bf16[256,256]{1,0:T(8,128)(2,1)S(1)}, bf16[256,256]{1,0:T(8,128)(2,1)S(1)}, u32[]{:S(2)}, u32[]{:S(2)}) %collective-permute-start.44) | collective-permute-done | bytes 131104 | tf_op jit(solution)/shard_map/ppermute | solution.py:33
  128.9 4.1 %collective-permute-done.45.refs_1_ = bf16[256,256]{1,0:T(8,128)(2,1)S(1)} collective-permute-done((bf16[256,256]{1,0:T(8,128)(2,1)S(1)}, bf16[256,256]{1,0:T(8,128)(2,1)S(1)}, u32[]{:S(2)}, u32[]{:S(2)}) %collective-permute-start.45) | collective-permute-done | bytes 131104 | tf_op jit(solution)/shard_map/ppermute | solution.py:33
  133.1 3.0 %collective-permute-start.47 = (bf16[64,256]{1,0:T(8,128)(2,1)S(1)}, bf16[64,256]{1,0:T(8,128)(2,1)S(1)}, u32[]{:S(2)}, u32[]{:S(2)}) collective-permute-start(bf16[64,256]{1,0:T(8,128)(2,1)S(1)} %get-tuple-element.87), channel_id=1, source_target_pairs={{0,8},{2,10},{4,12},{6,14},{8,0},{10,2},{12,4},{14,6},{16,24},{18,... | collective-permute-start | bytes 98312 | tf_op jit(solution)/shard_map/ppermute | solution.py:33
  136.3 2.1 %collective-permute-start.49 = (bf16[64,256]{1,0:T(8,128)(2,1)S(1)}, bf16[64,256]{1,0:T(8,128)(2,1)S(1)}, u32[]{:S(2)}, u32[]{:S(2)}) collective-permute-start(bf16[64,256]{1,0:T(8,128)(2,1)S(1)} %get-tuple-element.89), channel_id=1, source_target_pairs={{0,24},{2,26},{4,28},{6,30},{8,16},{10,18},{12,20},{14,22},{16,8},... | collective-permute-start | bytes 98312 | tf_op jit(solution)/shard_map/ppermute | solution.py:33
  138.5 2.4 %collective-permute-done.48.refs_1_ = bf16[64,256]{1,0:T(8,128)(2,1)S(1)} collective-permute-done((bf16[64,256]{1,0:T(8,128)(2,1)S(1)}, bf16[64,256]{1,0:T(8,128)(2,1)S(1)}, u32[]{:S(2)}, u32[]{:S(2)}) %collective-permute-start.48) | collective-permute-done | bytes 32800 | tf_op jit(solution)/shard_map/ppermute | solution.py:33
  140.8 1.2 collective-permute-done.49.refs_2_
  142.1 2.2 %collective-permute-start.52 = (bf16[64,256]{1,0:T(8,128)(2,1)S(1)}, bf16[64,256]{1,0:T(8,128)(2,1)S(1)}, u32[]{:S(2)}, u32[]{:S(2)}) collective-permute-start(bf16[64,256]{1,0:T(8,128)(2,1)S(1)} %kernel.37.have), channel_id=1, source_target_pairs={{0,24},{2,26},{4,28},{6,30},{8,16},{10,18},{12,20},{14,22},{16,8},... | collective-permute-start | bytes 98312 | tf_op jit(solution)/shard_map/ppermute | solution.py:33
  144.3 2.2 %collective-permute-start.50 = (bf16[64,256]{1,0:T(8,128)(2,1)S(1)}, bf16[64,256]{1,0:T(8,128)(2,1)S(1)}, u32[]{:S(2)}, u32[]{:S(2)}) collective-permute-start(bf16[64,256]{1,0:T(8,128)(2,1)S(1)} %kernel.37.have), channel_id=1, source_target_pairs={{0,8},{2,10},{4,12},{6,14},{8,0},{10,2},{12,4},{14,6},{16,24},{18,... | collective-permute-start | bytes 98312 | tf_op jit(solution)/shard_map/ppermute | solution.py:33
  146.5 1.3 collective-permute-done.52.refs_2_
  147.8 1.2 collective-permute-done.51.refs_1_
  149.1 1.6 collective-permute-start.55
  150.7 1.6 %collective-permute-start.54 = (bf16[256,256]{1,0:T(8,128)(2,1)S(1)}, bf16[256,256]{1,0:T(8,128)(2,1)S(1)}, u32[]{:S(2)}, u32[]{:S(2)}) collective-permute-start(bf16[256,256]{1,0:T(8,128)(2,1)S(1)} %kernel.38.have), channel_id=1, source_target_pairs={{0,4},{2,6},{4,0},{6,2},{8,12},{10,14},{12,8},{14,10},{16,20},{18,... | collective-permute-start | bytes 393224 | tf_op jit(solution)/shard_map/ppermute | solution.py:33
  152.7 2.5 %collective-permute-done.55.refs_2_ = bf16[256,256]{1,0:T(8,128)(2,1)S(1)} collective-permute-done((bf16[256,256]{1,0:T(8,128)(2,1)S(1)}, bf16[256,256]{1,0:T(8,128)(2,1)S(1)}, u32[]{:S(2)}, u32[]{:S(2)}) %collective-permute-start.55) | collective-permute-done | bytes 131104 | tf_op jit(solution)/shard_map/ppermute | solution.py:33
  155.1 1.3 collective-permute-done.54.refs_1_
  157.3 1.1 kernel.39
  158.4 1.1 kernel.34
  (104 shorter events, 11.1 us)
Async XLA Ops:
  0.6 26.9 %collective-permute-start = (f32[2,8]{1,0:T(2,128)}, f32[2,8]{1,0:T(2,128)S(1)}, u32[]{:S(2)}, u32[]{:S(2)}) collective-permute-start(f32[2,8]{1,0:T(2,128)} %bitcast.32), channel_id=1, source_target_pairs={{0,1},{1,0},{2,3},{3,2},{4,5},{5,4},{6,7},{7,6},{8,9},{9,8},{10,11... | collective-permute-start | bytes 200 | tf_op jit(solution)/shard_map/ppermute | solution.py:37
  1.2 26.4 %collective-permute-start.7 = (f32[2,2,256,256]{3,2,1,0:T(8,128)}, f32[2,2,256,256]{3,2,1,0:T(8,128)S(1)}, u32[]{:S(2)}, u32[]{:S(2)}) collective-permute-start(f32[2,2,256,256]{3,2,1,0:T(8,128)} %pm.1), channel_id=1, source_target_pairs={{0,1},{1,0},{2,3},{3,2},{4,5},{5,4},{6,7},{7,6},{8,9},{9,8},{10,11... | collective-permute-start | bytes 3145736 | tf_op jit(solution)/shard_map/ppermute | solution.py:37
  2.7 16.4 %collective-permute-start.3 = (bf16[512,128]{1,0:T(8,128)(2,1)S(1)}, bf16[512,128]{1,0:T(8,128)(2,1)S(1)}, u32[]{:S(2)}, u32[]{:S(2)}) collective-permute-start(bf16[512,128]{1,0:T(8,128)(2,1)S(1)} %get-tuple-element.50), channel_id=1, source_target_pairs={{0,14},{2,16},{4,18},{6,20},{8,22},{10,24},{12,26},{14,28},{16,30}... | collective-permute-start | bytes 393224 | tf_op jit(solution)/shard_map/ppermute | solution.py:28
  7.6 11.4 %collective-permute-start.1 = (bf16[768,128]{1,0:T(8,128)(2,1)S(1)}, bf16[768,128]{1,0:T(8,128)(2,1)S(1)}, u32[]{:S(2)}, u32[]{:S(2)}) collective-permute-start(bf16[768,128]{1,0:T(8,128)(2,1)S(1)} %get-tuple-element.48), channel_id=1, source_target_pairs={{0,30},{2,0},{4,2},{6,4},{8,6},{10,8},{12,10},{14,12},{16,14},{18,... | collective-permute-start | bytes 589832 | tf_op jit(solution)/shard_map/ppermute | solution.py:28
  9.9 16.0 %collective-permute-start.2 = (bf16[768,128]{1,0:T(8,128)(2,1)S(1)}, bf16[768,128]{1,0:T(8,128)(2,1)S(1)}, u32[]{:S(2)}, u32[]{:S(2)}) collective-permute-start(bf16[768,128]{1,0:T(8,128)(2,1)S(1)} %get-tuple-element.49), channel_id=1, source_target_pairs={{0,16},{2,18},{4,20},{6,22},{8,24},{10,26},{12,28},{14,30},{16,0},... | collective-permute-start | bytes 589832 | tf_op jit(solution)/shard_map/ppermute | solution.py:28
  19.0 8.5 %collective-permute-start.6 = (bf16[512,128]{1,0:T(8,128)(2,1)S(1)}, bf16[512,128]{1,0:T(8,128)(2,1)S(1)}, u32[]{:S(2)}, u32[]{:S(2)}) collective-permute-start(bf16[512,128]{1,0:T(8,128)(2,1)S(1)} %collective-permute-done.3.dm), channel_id=1, source_target_pairs={{0,1},{1,0},{2,3},{3,2},{4,5},{5,4},{6,7},{7,6},{8,9},{9,8},{10,11... | collective-permute-start | bytes 393224 | tf_op jit(solution)/shard_map/ppermute | solution.py:37
  19.0 8.5 %collective-permute-start.4 = (bf16[768,128]{1,0:T(8,128)(2,1)S(1)}, bf16[768,128]{1,0:T(8,128)(2,1)S(1)}, u32[]{:S(2)}, u32[]{:S(2)}) collective-permute-start(bf16[768,128]{1,0:T(8,128)(2,1)S(1)} %collective-permute-done.1.rm), channel_id=1, source_target_pairs={{0,1},{1,0},{2,3},{3,2},{4,5},{5,4},{6,7},{7,6},{8,9},{9,8},{10,11... | collective-permute-start | bytes 589832 | tf_op jit(solution)/shard_map/ppermute | solution.py:37
  35.0 5.3 %collective-permute-start.9 = (bf16[2048,128]{1,0:T(8,128)(2,1)S(1)}, bf16[2048,128]{1,0:T(8,128)(2,1)S(1)}, u32[]{:S(2)}, u32[]{:S(2)}) collective-permute-start(bf16[2048,128]{1,0:T(8,128)(2,1)S(1)} %get-tuple-element.54), channel_id=1, source_target_pairs={{0,1},{1,0},{2,3},{3,2},{4,5},{5,4},{6,7},{7,6},{8,9},{9,8},{10,11... | collective-permute-start | bytes 1572872 | tf_op jit(solution)/shard_map/ppermute | solution.py:37
  36.6 6.4 %collective-permute-start.21 = (bf16[256,256]{1,0:T(8,128)(2,1)S(1)}, bf16[256,256]{1,0:T(8,128)(2,1)S(1)}, u32[]{:S(2)}, u32[]{:S(2)}) collective-permute-start(bf16[256,256]{1,0:T(8,128)(2,1)S(1)} %get-tuple-element.66), channel_id=1, source_target_pairs={{0,2},{2,0},{4,6},{6,4},{8,10},{10,8},{12,14},{14,12},{16,18},{18,... | collective-permute-start | bytes 393224 | tf_op jit(solution)/shard_map/ppermute | solution.py:33
  36.7 29.0 %collective-permute-start.8 = (bf16[384,384]{1,0:T(8,128)(2,1)S(1)}, bf16[384,384]{1,0:T(8,128)(2,1)S(1)}, u32[]{:S(2)}, u32[]{:S(2)}) collective-permute-start(bf16[384,384]{1,0:T(8,128)(2,1)S(1)} %get-tuple-element.53), channel_id=1, source_target_pairs={{0,1},{1,0},{2,3},{3,2},{4,5},{5,4},{6,7},{7,6},{8,9},{9,8},{10,11... | collective-permute-start | bytes 884744 | tf_op jit(solution)/shard_map/ppermute | solution.py:37
  37.1 8.3 %collective-permute-start.22 = (bf16[256,256]{1,0:T(8,128)(2,1)S(1)}, bf16[256,256]{1,0:T(8,128)(2,1)S(1)}, u32[]{:S(2)}, u32[]{:S(2)}) collective-permute-start(bf16[256,256]{1,0:T(8,128)(2,1)S(1)} %get-tuple-element.67), channel_id=1, source_target_pairs={{0,4},{2,6},{4,0},{6,2},{8,12},{10,14},{12,8},{14,10},{16,20},{18,... | collective-permute-start | bytes 393224 | tf_op jit(solution)/shard_map/ppermute | solution.py:33
  37.1 8.4 %collective-permute-start.23 = (bf16[256,256]{1,0:T(8,128)(2,1)S(1)}, bf16[256,256]{1,0:T(8,128)(2,1)S(1)}, u32[]{:S(2)}, u32[]{:S(2)}) collective-permute-start(bf16[256,256]{1,0:T(8,128)(2,1)S(1)} %get-tuple-element.68), channel_id=1, source_target_pairs={{0,6},{2,4},{4,2},{6,0},{8,14},{10,12},{12,10},{14,8},{16,22},{18,... | collective-permute-start | bytes 393224 | tf_op jit(solution)/shard_map/ppermute | solution.py:33
  40.4 27.1 %collective-permute-start.10 = (bf16[768,128]{1,0:T(8,128)(2,1)S(1)}, bf16[768,128]{1,0:T(8,128)(2,1)S(1)}, u32[]{:S(2)}, u32[]{:S(2)}) collective-permute-start(bf16[768,128]{1,0:T(8,128)(2,1)S(1)} %get-tuple-element.55), channel_id=1, source_target_pairs={{0,2},{2,4},{4,6},{6,8},{8,10},{10,12},{12,14},{14,16},{16,18},{18... | collective-permute-start | bytes 589832 | tf_op jit(solution)/shard_map/ppermute | solution.py:28
  43.0 24.4 %collective-permute-start.11 = (bf16[768,128]{1,0:T(8,128)(2,1)S(1)}, bf16[768,128]{1,0:T(8,128)(2,1)S(1)}, u32[]{:S(2)}, u32[]{:S(2)}) collective-permute-start(bf16[768,128]{1,0:T(8,128)(2,1)S(1)} %get-tuple-element.56), channel_id=1, source_target_pairs={{0,16},{2,18},{4,20},{6,22},{8,24},{10,26},{12,28},{14,30},{16,0},... | collective-permute-start | bytes 589832 | tf_op jit(solution)/shard_map/ppermute | solution.py:28
  45.5 20.2 %collective-permute-start.12 = (bf16[512,128]{1,0:T(8,128)(2,1)S(1)}, bf16[512,128]{1,0:T(8,128)(2,1)S(1)}, u32[]{:S(2)}, u32[]{:S(2)}) collective-permute-start(bf16[512,128]{1,0:T(8,128)(2,1)S(1)} %get-tuple-element.57), channel_id=1, source_target_pairs={{0,18},{2,20},{4,22},{6,24},{8,26},{10,28},{12,30},{14,0},{16,2},{... | collective-permute-start | bytes 393224 | tf_op jit(solution)/shard_map/ppermute | solution.py:28
  45.6 5.4 %collective-permute-start.24 = (bf16[64,256]{1,0:T(8,128)(2,1)S(1)}, bf16[64,256]{1,0:T(8,128)(2,1)S(1)}, u32[]{:S(2)}, u32[]{:S(2)}) collective-permute-start(bf16[64,256]{1,0:T(8,128)(2,1)S(1)} %get-tuple-element.70), channel_id=1, source_target_pairs={{0,8},{2,10},{4,12},{6,14},{8,0},{10,2},{12,4},{14,6},{16,24},{18,... | collective-permute-start | bytes 98312 | tf_op jit(solution)/shard_map/ppermute | solution.py:33
  51.0 6.2 %collective-permute-start.25 = (bf16[64,256]{1,0:T(8,128)(2,1)S(1)}, bf16[64,256]{1,0:T(8,128)(2,1)S(1)}, u32[]{:S(2)}, u32[]{:S(2)}) collective-permute-start(bf16[64,256]{1,0:T(8,128)(2,1)S(1)} %get-tuple-element.71), channel_id=1, source_target_pairs={{0,16},{2,18},{4,20},{6,22},{8,24},{10,26},{12,28},{14,30},{16,0},... | collective-permute-start | bytes 98312 | tf_op jit(solution)/shard_map/ppermute | solution.py:33
  57.2 5.7 %collective-permute-start.26 = (bf16[64,256]{1,0:T(8,128)(2,1)S(1)}, bf16[64,256]{1,0:T(8,128)(2,1)S(1)}, u32[]{:S(2)}, u32[]{:S(2)}) collective-permute-start(bf16[64,256]{1,0:T(8,128)(2,1)S(1)} %get-tuple-element.72), channel_id=1, source_target_pairs={{0,24},{2,26},{4,28},{6,30},{8,16},{10,18},{12,20},{14,22},{16,8},... | collective-permute-start | bytes 98312 | tf_op jit(solution)/shard_map/ppermute | solution.py:33
  63.0 11.5 %collective-permute-start.29 = (bf16[64,256]{1,0:T(8,128)(2,1)S(1)}, bf16[64,256]{1,0:T(8,128)(2,1)S(1)}, u32[]{:S(2)}, u32[]{:S(2)}) collective-permute-start(bf16[64,256]{1,0:T(8,128)(2,1)S(1)} %kernel.27.have), channel_id=1, source_target_pairs={{0,24},{2,26},{4,28},{6,30},{8,16},{10,18},{12,20},{14,22},{16,8},... | collective-permute-start | bytes 98312 | tf_op jit(solution)/shard_map/ppermute | solution.py:33
  65.7 8.8 %collective-permute-start.28 = (bf16[64,256]{1,0:T(8,128)(2,1)S(1)}, bf16[64,256]{1,0:T(8,128)(2,1)S(1)}, u32[]{:S(2)}, u32[]{:S(2)}) collective-permute-start(bf16[64,256]{1,0:T(8,128)(2,1)S(1)} %kernel.27.have), channel_id=1, source_target_pairs={{0,16},{2,18},{4,20},{6,22},{8,24},{10,26},{12,28},{14,30},{16,0},... | collective-permute-start | bytes 98312 | tf_op jit(solution)/shard_map/ppermute | solution.py:33
  65.7 8.8 %collective-permute-start.27 = (bf16[64,256]{1,0:T(8,128)(2,1)S(1)}, bf16[64,256]{1,0:T(8,128)(2,1)S(1)}, u32[]{:S(2)}, u32[]{:S(2)}) collective-permute-start(bf16[64,256]{1,0:T(8,128)(2,1)S(1)} %kernel.27.have), channel_id=1, source_target_pairs={{0,8},{2,10},{4,12},{6,14},{8,0},{10,2},{12,4},{14,6},{16,24},{18,... | collective-permute-start | bytes 98312 | tf_op jit(solution)/shard_map/ppermute | solution.py:33
  67.7 10.5 %collective-permute-start.15 = (bf16[512,128]{1,0:T(8,128)(2,1)S(1)}, bf16[512,128]{1,0:T(8,128)(2,1)S(1)}, u32[]{:S(2)}, u32[]{:S(2)}) collective-permute-start(bf16[512,128]{1,0:T(8,128)(2,1)S(1)} %get-tuple-element.62), channel_id=1, source_target_pairs={{0,14},{2,16},{4,18},{6,20},{8,22},{10,24},{12,26},{14,28},{16,30}... | collective-permute-start | bytes 393224 | tf_op jit(solution)/shard_map/ppermute | solution.py:28
  74.5 9.2 %collective-permute-start.33 = (bf16[256,256]{1,0:T(8,128)(2,1)S(1)}, bf16[256,256]{1,0:T(8,128)(2,1)S(1)}, u32[]{:S(2)}, u32[]{:S(2)}) collective-permute-start(bf16[256,256]{1,0:T(8,128)(2,1)S(1)} %kernel.28.have), channel_id=1, source_target_pairs={{0,1},{1,0},{2,3},{3,2},{4,5},{5,4},{6,7},{7,6},{8,9},{9,8},{10,11... | collective-permute-start | bytes 393224 | tf_op jit(solution)/shard_map/ppermute | solution.py:37
  74.6 9.1 %collective-permute-start.32 = (bf16[256,256]{1,0:T(8,128)(2,1)S(1)}, bf16[256,256]{1,0:T(8,128)(2,1)S(1)}, u32[]{:S(2)}, u32[]{:S(2)}) collective-permute-start(bf16[256,256]{1,0:T(8,128)(2,1)S(1)} %kernel.28.have), channel_id=1, source_target_pairs={{0,6},{2,4},{4,2},{6,0},{8,14},{10,12},{12,10},{14,8},{16,22},{18,... | collective-permute-start | bytes 393224 | tf_op jit(solution)/shard_map/ppermute | solution.py:33
  77.6 6.9 %collective-permute-start.31 = (bf16[256,256]{1,0:T(8,128)(2,1)S(1)}, bf16[256,256]{1,0:T(8,128)(2,1)S(1)}, u32[]{:S(2)}, u32[]{:S(2)}) collective-permute-start(bf16[256,256]{1,0:T(8,128)(2,1)S(1)} %kernel.28.have), channel_id=1, source_target_pairs={{0,4},{2,6},{4,0},{6,2},{8,12},{10,14},{12,8},{14,10},{16,20},{18,... | collective-permute-start | bytes 393224 | tf_op jit(solution)/shard_map/ppermute | solution.py:33
  77.6 11.1 %collective-permute-start.30 = (bf16[256,256]{1,0:T(8,128)(2,1)S(1)}, bf16[256,256]{1,0:T(8,128)(2,1)S(1)}, u32[]{:S(2)}, u32[]{:S(2)}) collective-permute-start(bf16[256,256]{1,0:T(8,128)(2,1)S(1)} %kernel.28.have), channel_id=1, source_target_pairs={{0,2},{2,0},{4,6},{6,4},{8,10},{10,8},{12,14},{14,12},{16,18},{18,... | collective-permute-start | bytes 393224 | tf_op jit(solution)/shard_map/ppermute | solution.py:33
  78.2 10.5 %collective-permute-start.13 = (bf16[768,128]{1,0:T(8,128)(2,1)S(1)}, bf16[768,128]{1,0:T(8,128)(2,1)S(1)}, u32[]{:S(2)}, u32[]{:S(2)}) collective-permute-start(bf16[768,128]{1,0:T(8,128)(2,1)S(1)} %get-tuple-element.60), channel_id=1, source_target_pairs={{0,30},{2,0},{4,2},{6,4},{8,6},{10,8},{12,10},{14,12},{16,14},{18,... | collective-permute-start | bytes 589832 | tf_op jit(solution)/shard_map/ppermute | solution.py:28
  83.7 11.1 %collective-permute-start.14 = (bf16[768,128]{1,0:T(8,128)(2,1)S(1)}, bf16[768,128]{1,0:T(8,128)(2,1)S(1)}, u32[]{:S(2)}, u32[]{:S(2)}) collective-permute-start(bf16[768,128]{1,0:T(8,128)(2,1)S(1)} %get-tuple-element.61), channel_id=1, source_target_pairs={{0,16},{2,18},{4,20},{6,22},{8,24},{10,26},{12,28},{14,30},{16,0},... | collective-permute-start | bytes 589832 | tf_op jit(solution)/shard_map/ppermute | solution.py:28
  83.7 13.0 %collective-permute-start.16 = (bf16[384,384]{1,0:T(8,128)(2,1)S(1)}, bf16[384,384]{1,0:T(8,128)(2,1)S(1)}, u32[]{:S(2)}, u32[]{:S(2)}) collective-permute-start(bf16[384,384]{1,0:T(8,128)(2,1)S(1)} %get-tuple-element.59.tm), channel_id=1, source_target_pairs={{0,1},{1,0},{2,3},{3,2},{4,5},{5,4},{6,7},{7,6},{8,9},{9,8},{10,11... | collective-permute-start | bytes 884744 | tf_op jit(solution)/shard_map/ppermute | solution.py:37
  84.5 10.4 %collective-permute-start.36 = (bf16[256,256]{1,0:T(8,128)(2,1)S(1)}, bf16[256,256]{1,0:T(8,128)(2,1)S(1)}, u32[]{:S(2)}, u32[]{:S(2)}) collective-permute-start(bf16[256,256]{1,0:T(8,128)(2,1)S(1)} %collective-permute-done.32.refs_2_), channel_id=1, source_target_pairs={{0,1},{1,0},{2,3},{3,2},{4,5},{5,4},{6,7},{7,6},{8,9},{9,8},{10,11... | collective-permute-start | bytes 393224 | tf_op jit(solution)/shard_map/ppermute | solution.py:37
  88.7 6.7 %collective-permute-start.35 = (bf16[256,256]{1,0:T(8,128)(2,1)S(1)}, bf16[256,256]{1,0:T(8,128)(2,1)S(1)}, u32[]{:S(2)}, u32[]{:S(2)}) collective-permute-start(bf16[256,256]{1,0:T(8,128)(2,1)S(1)} %collective-permute-done.31.refs_1_), channel_id=1, source_target_pairs={{0,1},{1,0},{2,3},{3,2},{4,5},{5,4},{6,7},{7,6},{8,9},{9,8},{10,11... | collective-permute-start | bytes 393224 | tf_op jit(solution)/shard_map/ppermute | solution.py:37
  88.7 8.0 %collective-permute-start.17 = (bf16[768,128]{1,0:T(8,128)(2,1)S(1)}, bf16[768,128]{1,0:T(8,128)(2,1)S(1)}, u32[]{:S(2)}, u32[]{:S(2)}) collective-permute-start(bf16[768,128]{1,0:T(8,128)(2,1)S(1)} %collective-permute-done.13.rm), channel_id=1, source_target_pairs={{0,1},{1,0},{2,3},{3,2},{4,5},{5,4},{6,7},{7,6},{8,9},{9,8},{10,11... | collective-permute-start | bytes 589832 | tf_op jit(solution)/shard_map/ppermute | solution.py:37
  104.1 16.2 %collective-permute-start.43 = (bf16[2,2,256,256]{3,2,1,0:T(8,128)(2,1)S(1)}, bf16[2,2,256,256]{3,2,1,0:T(8,128)(2,1)S(1)}, u32[]{:S(2)}, u32[]{:S(2)}) collective-permute-start(bf16[2,2,256,256]{3,2,1,0:T(8,128)(2,1)S(1)} %get-tuple-element.81), channel_id=1, source_target_pairs={{0,1},{1,0},{2,3},{3,2},{4,5},{5,4},{6,7},{7,6},{8,9},{9,8},{10,11... | collective-permute-start | bytes 1572872 | tf_op jit(solution)/shard_map/ppermute | solution.py:37
  105.5 13.6 %collective-permute-start.39 = (bf16[768,128]{1,0:T(8,128)(2,1)S(1)}, bf16[768,128]{1,0:T(8,128)(2,1)S(1)}, u32[]{:S(2)}, u32[]{:S(2)}) collective-permute-start(bf16[768,128]{1,0:T(8,128)(2,1)S(1)} %get-tuple-element.76), channel_id=1, source_target_pairs={{0,2},{2,4},{4,6},{6,8},{8,10},{10,12},{12,14},{14,16},{16,18},{18... | collective-permute-start | bytes 589832 | tf_op jit(solution)/shard_map/ppermute | solution.py:28
  105.6 13.5 %collective-permute-start.40 = (bf16[768,128]{1,0:T(8,128)(2,1)S(1)}, bf16[768,128]{1,0:T(8,128)(2,1)S(1)}, u32[]{:S(2)}, u32[]{:S(2)}) collective-permute-start(bf16[768,128]{1,0:T(8,128)(2,1)S(1)} %get-tuple-element.77), channel_id=1, source_target_pairs={{0,16},{2,18},{4,20},{6,22},{8,24},{10,26},{12,28},{14,30},{16,0},... | collective-permute-start | bytes 589832 | tf_op jit(solution)/shard_map/ppermute | solution.py:28
  105.7 13.4 %collective-permute-start.41 = (bf16[512,128]{1,0:T(8,128)(2,1)S(1)}, bf16[512,128]{1,0:T(8,128)(2,1)S(1)}, u32[]{:S(2)}, u32[]{:S(2)}) collective-permute-start(bf16[512,128]{1,0:T(8,128)(2,1)S(1)} %get-tuple-element.78), channel_id=1, source_target_pairs={{0,18},{2,20},{4,22},{6,24},{8,26},{10,28},{12,30},{14,0},{16,2},{... | collective-permute-start | bytes 393224 | tf_op jit(solution)/shard_map/ppermute | solution.py:28
  120.2 38.2 %collective-permute-start.42 = (f32[384,384]{1,0:T(8,128)S(1)}, f32[384,384]{1,0:T(8,128)S(1)}, u32[]{:S(2)}, u32[]{:S(2)}) collective-permute-start(f32[384,384]{1,0:T(8,128)S(1)} %get-tuple-element.79.state), channel_id=1, source_target_pairs={{0,1},{1,0},{2,3},{3,2},{4,5},{5,4},{6,7},{7,6},{8,9},{9,8},{10,11... | collective-permute-start | bytes 1769480 | tf_op jit(solution)/shard_map/ppermute | solution.py:37
  120.3 8.5 %collective-permute-start.44 = (bf16[256,256]{1,0:T(8,128)(2,1)S(1)}, bf16[256,256]{1,0:T(8,128)(2,1)S(1)}, u32[]{:S(2)}, u32[]{:S(2)}) collective-permute-start(bf16[256,256]{1,0:T(8,128)(2,1)S(1)} %get-tuple-element.83), channel_id=1, source_target_pairs={{0,2},{2,0},{4,6},{6,4},{8,10},{10,8},{12,14},{14,12},{16,18},{18,... | collective-permute-start | bytes 393224 | tf_op jit(solution)/shard_map/ppermute | solution.py:33
  124.6 8.4 %collective-permute-start.45 = (bf16[256,256]{1,0:T(8,128)(2,1)S(1)}, bf16[256,256]{1,0:T(8,128)(2,1)S(1)}, u32[]{:S(2)}, u32[]{:S(2)}) collective-permute-start(bf16[256,256]{1,0:T(8,128)(2,1)S(1)} %get-tuple-element.84), channel_id=1, source_target_pairs={{0,4},{2,6},{4,0},{6,2},{8,12},{10,14},{12,8},{14,10},{16,20},{18,... | collective-permute-start | bytes 393224 | tf_op jit(solution)/shard_map/ppermute | solution.py:33
  125.6 7.3 %collective-permute-start.46 = (bf16[256,256]{1,0:T(8,128)(2,1)S(1)}, bf16[256,256]{1,0:T(8,128)(2,1)S(1)}, u32[]{:S(2)}, u32[]{:S(2)}) collective-permute-start(bf16[256,256]{1,0:T(8,128)(2,1)S(1)} %get-tuple-element.85), channel_id=1, source_target_pairs={{0,6},{2,4},{4,2},{6,0},{8,14},{10,12},{12,10},{14,8},{16,22},{18,... | collective-permute-start | bytes 393224 | tf_op jit(solution)/shard_map/ppermute | solution.py:33
  133.1 5.4 %collective-permute-start.47 = (bf16[64,256]{1,0:T(8,128)(2,1)S(1)}, bf16[64,256]{1,0:T(8,128)(2,1)S(1)}, u32[]{:S(2)}, u32[]{:S(2)}) collective-permute-start(bf16[64,256]{1,0:T(8,128)(2,1)S(1)} %get-tuple-element.87), channel_id=1, source_target_pairs={{0,8},{2,10},{4,12},{6,14},{8,0},{10,2},{12,4},{14,6},{16,24},{18,... | collective-permute-start | bytes 98312 | tf_op jit(solution)/shard_map/ppermute | solution.py:33
  136.0 4.8 %collective-permute-start.48 = (bf16[64,256]{1,0:T(8,128)(2,1)S(1)}, bf16[64,256]{1,0:T(8,128)(2,1)S(1)}, u32[]{:S(2)}, u32[]{:S(2)}) collective-permute-start(bf16[64,256]{1,0:T(8,128)(2,1)S(1)} %get-tuple-element.88), channel_id=1, source_target_pairs={{0,16},{2,18},{4,20},{6,22},{8,24},{10,26},{12,28},{14,30},{16,0},... | collective-permute-start | bytes 98312 | tf_op jit(solution)/shard_map/ppermute | solution.py:33
  136.3 5.7 %collective-permute-start.49 = (bf16[64,256]{1,0:T(8,128)(2,1)S(1)}, bf16[64,256]{1,0:T(8,128)(2,1)S(1)}, u32[]{:S(2)}, u32[]{:S(2)}) collective-permute-start(bf16[64,256]{1,0:T(8,128)(2,1)S(1)} %get-tuple-element.89), channel_id=1, source_target_pairs={{0,24},{2,26},{4,28},{6,30},{8,16},{10,18},{12,20},{14,22},{16,8},... | collective-permute-start | bytes 98312 | tf_op jit(solution)/shard_map/ppermute | solution.py:33
  142.1 5.8 %collective-permute-start.52 = (bf16[64,256]{1,0:T(8,128)(2,1)S(1)}, bf16[64,256]{1,0:T(8,128)(2,1)S(1)}, u32[]{:S(2)}, u32[]{:S(2)}) collective-permute-start(bf16[64,256]{1,0:T(8,128)(2,1)S(1)} %kernel.37.have), channel_id=1, source_target_pairs={{0,24},{2,26},{4,28},{6,30},{8,16},{10,18},{12,20},{14,22},{16,8},... | collective-permute-start | bytes 98312 | tf_op jit(solution)/shard_map/ppermute | solution.py:33
  144.3 4.8 %collective-permute-start.51 = (bf16[64,256]{1,0:T(8,128)(2,1)S(1)}, bf16[64,256]{1,0:T(8,128)(2,1)S(1)}, u32[]{:S(2)}, u32[]{:S(2)}) collective-permute-start(bf16[64,256]{1,0:T(8,128)(2,1)S(1)} %kernel.37.have), channel_id=1, source_target_pairs={{0,16},{2,18},{4,20},{6,22},{8,24},{10,26},{12,28},{14,30},{16,0},... | collective-permute-start | bytes 98312 | tf_op jit(solution)/shard_map/ppermute | solution.py:33
  149.1 6.0 %collective-permute-start.55 = (bf16[256,256]{1,0:T(8,128)(2,1)S(1)}, bf16[256,256]{1,0:T(8,128)(2,1)S(1)}, u32[]{:S(2)}, u32[]{:S(2)}) collective-permute-start(bf16[256,256]{1,0:T(8,128)(2,1)S(1)} %kernel.38.have), channel_id=1, source_target_pairs={{0,6},{2,4},{4,2},{6,0},{8,14},{10,12},{12,10},{14,8},{16,22},{18,... | collective-permute-start | bytes 393224 | tf_op jit(solution)/shard_map/ppermute | solution.py:33
  150.7 5.8 %collective-permute-start.54 = (bf16[256,256]{1,0:T(8,128)(2,1)S(1)}, bf16[256,256]{1,0:T(8,128)(2,1)S(1)}, u32[]{:S(2)}, u32[]{:S(2)}) collective-permute-start(bf16[256,256]{1,0:T(8,128)(2,1)S(1)} %kernel.38.have), channel_id=1, source_target_pairs={{0,4},{2,6},{4,0},{6,2},{8,12},{10,14},{12,8},{14,10},{16,20},{18,... | collective-permute-start | bytes 393224 | tf_op jit(solution)/shard_map/ppermute | solution.py:33
  152.3 5.0 %collective-permute-start.53 = (bf16[256,256]{1,0:T(8,128)(2,1)S(1)}, bf16[256,256]{1,0:T(8,128)(2,1)S(1)}, u32[]{:S(2)}, u32[]{:S(2)}) collective-permute-start(bf16[256,256]{1,0:T(8,128)(2,1)S(1)} %kernel.38.have), channel_id=1, source_target_pairs={{0,2},{2,0},{4,6},{6,4},{8,10},{10,8},{12,14},{14,12},{16,18},{18,... | collective-permute-start | bytes 393224 | tf_op jit(solution)/shard_map/ppermute | solution.py:33
  (14 other events, 102.2 us)

commit v5 on v4

--- a/solution.py
+++ b/solution.py
@@ -345,7 +345,7 @@
     return call(kernel, edge_shapes(t, n), grad, got)
 
 
-def update_kernel(state, grad, got, right, low, diag, new, half, hr, hl, hd):
+def update_kernel(state, grad, got, right, low, diag, new, *smalls):
     t = state.shape[0]
     n = low.shape[0] * LANES // t
     own = grad[lax.axis_index("mode"), pl.ds(0, t), pl.ds(0, t)]
@@ -356,15 +356,18 @@
             new[pl.ds(0, high), lanes] += ref[pl.ds(k * high, high), :].astype(f32)
     value = state[...] - step_object * new[...]
     new[...] = value
-    small = value.astype(bf16)
-    half[...] = small
-    pack_edges(small, t, n, (hr, hl, hd))
-
-
-def update(state, keep, got, right, low, diag):
+    if smalls:
+        small = value.astype(bf16)
+        smalls[0][...] = small
+        pack_edges(small, t, n, smalls[1:])
+
+
+def update(state, keep, got, right, low, diag, last):
     t = state.shape[0]
     n = low.shape[0] * LANES // t
     outs = (((t, t), f32), ((t, t), bf16)) + edge_shapes(t, n)
+    if last:
+        outs = outs[:1]
     return call(update_kernel, outs, state, keep, got, right, low, diag)
 
 
@@ -514,9 +517,11 @@
         right = shifted(right, 1)
         pieces = probe_sum(acc, swapped(pgo))
         own_got = swapped(own_send)
-        state, half, *edges = update(state, grad, own_got, right, low, diag)
+        last = sweep == ITERS - 1
+        state, *after = update(state, grad, own_got, right, low, diag, last)
         pm = probe_step(rate, pm, pieces)
-        if sweep < ITERS - 1:
+        if not last:
+            half, *edges = after
             rest = swapped(half)
             others = [swapped(piece) for piece in pieces]
             po = probe_step(rate, po, others)

time: 160 us -> 159 us (level)
  transfers between devices with their start and end apart: 56 -> 56, of which waited for: 25 -> 25; matrix products, arithmetic and copies ran while one was open for 1% -> 1% of each run, Pallas kernels for 3% -> 2%
where the time goes in v5:
time: 159 us
  waiting for transfers between devices  71.8 us (45%)
  starting transfers between devices  64.7 us (41%)
  Pallas kernels  18 us (11%)
  between operations  1.64 us (1%)
    ppermute x24, starting transfers between devices, flipped(): return lax.ppermute(array, 'tile', [(i, i ^ mask) for i in range(peers)])  38.5 us
    ppermute x24, waiting for transfers between devices, flipped(): return lax.ppermute(array, 'tile', [(i, i ^ mask) for i in range(peers)])  36.5 us
    ppermute x12, waiting for transfers between devices, shifted(): lax.ppermute(array, 'tile', [(i, (i + by) % peers) for i in range(peers)])  31.4 us
    ppermute x12, starting transfers between devices, shifted(): lax.ppermute(array, 'tile', [(i, (i + by) % peers) for i in range(peers)])  21.8 us
    pallas_call x20, Pallas kernels, call(): pl.pallas_call(kernel, out_shape=tuple((jax.ShapeDtypeStruct(shape, dtype...  18 us
    ppermute x20, starting transfers between devices, swapped(): return lax.ppermute(array, 'mode', [(0, 1), (1, 0)])  4.36 us
    ppermute x20, waiting for transfers between devices, swapped(): return lax.ppermute(array, 'mode', [(0, 1), (1, 0)])  3.88 us
  transfers between devices with their start and end apart: 56, of which 25 were waited for; matrix products, arithmetic and copies ran while one was open for 1% of the time, Pallas kernels for 2%

profile of v5, /device:TPU:0, one launch (start us, length us, event | category | flops | bytes accessed | tf_op | source)
XLA Modules:
  0.0 158.7 jit_solution(16136224217167618633)
XLA Ops:
  1.3 1.3 copy-done.1
  2.7 4.9 %collective-permute-start.3 = (bf16[512,128]{1,0:T(8,128)(2,1)S(1)}, bf16[512,128]{1,0:T(8,128)(2,1)S(1)}, u32[]{:S(2)}, u32[]{:S(2)}) collective-permute-start(bf16[512,128]{1,0:T(8,128)(2,1)S(1)} %get-tuple-element.49), channel_id=1, source_target_pairs={{0,14},{2,16},{4,18},{6,20},{8,22},{10,24},{12,26},{14,28},{16,30}... | collective-permute-start | bytes 393224 | tf_op jit(solution)/shard_map/ppermute | solution.py:28
  7.6 2.3 %collective-permute-start.1 = (bf16[768,128]{1,0:T(8,128)(2,1)S(1)}, bf16[768,128]{1,0:T(8,128)(2,1)S(1)}, u32[]{:S(2)}, u32[]{:S(2)}) collective-permute-start(bf16[768,128]{1,0:T(8,128)(2,1)S(1)} %get-tuple-element.47), channel_id=1, source_target_pairs={{0,30},{2,0},{4,2},{6,4},{8,6},{10,8},{12,10},{14,12},{16,14},{18,... | collective-permute-start | bytes 589832 | tf_op jit(solution)/shard_map/ppermute | solution.py:28
  9.9 1.7 %collective-permute-start.2 = (bf16[768,128]{1,0:T(8,128)(2,1)S(1)}, bf16[768,128]{1,0:T(8,128)(2,1)S(1)}, u32[]{:S(2)}, u32[]{:S(2)}) collective-permute-start(bf16[768,128]{1,0:T(8,128)(2,1)S(1)} %get-tuple-element.48), channel_id=1, source_target_pairs={{0,16},{2,18},{4,20},{6,22},{8,24},{10,26},{12,28},{14,30},{16,0},... | collective-permute-start | bytes 589832 | tf_op jit(solution)/shard_map/ppermute | solution.py:28
  12.9 6.1 %collective-permute-done.3.dm = bf16[512,128]{1,0:T(8,128)(2,1)S(1)} collective-permute-done((bf16[512,128]{1,0:T(8,128)(2,1)S(1)}, bf16[512,128]{1,0:T(8,128)(2,1)S(1)}, u32[]{:S(2)}, u32[]{:S(2)}) %collective-permute-start.3) | collective-permute-done | bytes 131104 | tf_op jit(solution)/shard_map/ppermute | solution.py:28
  19.5 6.4 %collective-permute-done.2.bm = bf16[768,128]{1,0:T(8,128)(2,1)S(1)} collective-permute-done((bf16[768,128]{1,0:T(8,128)(2,1)S(1)}, bf16[768,128]{1,0:T(8,128)(2,1)S(1)}, u32[]{:S(2)}, u32[]{:S(2)}) %collective-permute-start.2) | collective-permute-done | bytes 196640 | tf_op jit(solution)/shard_map/ppermute | solution.py:28
  26.7 0.9 kernel.21.meas
  27.7 6.7 %kernel.22 = (f32[2,640,640]{2,1,0:T(8,128)S(1)}, bf16[384,384]{1,0:T(8,128)(2,1)S(1)}, bf16[2048,128]{1,0:T(8,128)(2,1)S(1)}, f32[4,2,256,256]{3,2,1,0:T(8,128)S(1)}, bf16[2,2,256,256]{3,2,1,0:T(8,128)(2,1)S(1)}) custom-call(s32[1]{0:T(128)S(6)} %copy.9.live, s32[2,4]{1,0:T(2,128)S(1)} %bitcast.30, s32[4]{0:T(128)S(1)} %copy-done.5, f32[2,8]{1,0:T(2,128)S(1)} %bitcast.33, ...), custom_call_target="tpu_custom_call" | custom-call | tf_op jit(solution)/shard_map/kernel/pallas_call | solution.py:233
  35.1 1.5 collective-permute-done.20
  37.1 3.1 %collective-permute-start.23 = (bf16[256,256]{1,0:T(8,128)(2,1)S(1)}, bf16[256,256]{1,0:T(8,128)(2,1)S(1)}, u32[]{:S(2)}, u32[]{:S(2)}) collective-permute-start(bf16[256,256]{1,0:T(8,128)(2,1)S(1)} %get-tuple-element.67), channel_id=1, source_target_pairs={{0,6},{2,4},{4,2},{6,0},{8,14},{10,12},{12,10},{14,8},{16,22},{18,... | collective-permute-start | bytes 393224 | tf_op jit(solution)/shard_map/ppermute | solution.py:33
  40.8 2.3 %collective-permute-done.21.refs_0_ = bf16[256,256]{1,0:T(8,128)(2,1)S(1)} collective-permute-done((bf16[256,256]{1,0:T(8,128)(2,1)S(1)}, bf16[256,256]{1,0:T(8,128)(2,1)S(1)}, u32[]{:S(2)}, u32[]{:S(2)}) %collective-permute-start.21) | collective-permute-done | bytes 131104 | tf_op jit(solution)/shard_map/ppermute | solution.py:33
  43.1 2.4 %collective-permute-done.22.refs_1_ = bf16[256,256]{1,0:T(8,128)(2,1)S(1)} collective-permute-done((bf16[256,256]{1,0:T(8,128)(2,1)S(1)}, bf16[256,256]{1,0:T(8,128)(2,1)S(1)}, u32[]{:S(2)}, u32[]{:S(2)}) %collective-permute-start.22) | collective-permute-done | bytes 131104 | tf_op jit(solution)/shard_map/ppermute | solution.py:33
  45.6 2.5 %collective-permute-start.24 = (bf16[64,256]{1,0:T(8,128)(2,1)S(1)}, bf16[64,256]{1,0:T(8,128)(2,1)S(1)}, u32[]{:S(2)}, u32[]{:S(2)}) collective-permute-start(bf16[64,256]{1,0:T(8,128)(2,1)S(1)} %get-tuple-element.69), channel_id=1, source_target_pairs={{0,8},{2,10},{4,12},{6,14},{8,0},{10,2},{12,4},{14,6},{16,24},{18,... | collective-permute-start | bytes 98312 | tf_op jit(solution)/shard_map/ppermute | solution.py:33
  48.1 3.0 %collective-permute-done.24.refs_0_ = bf16[64,256]{1,0:T(8,128)(2,1)S(1)} collective-permute-done((bf16[64,256]{1,0:T(8,128)(2,1)S(1)}, bf16[64,256]{1,0:T(8,128)(2,1)S(1)}, u32[]{:S(2)}, u32[]{:S(2)}) %collective-permute-start.24) | collective-permute-done | bytes 32800 | tf_op jit(solution)/shard_map/ppermute | solution.py:33
  51.0 2.9 %collective-permute-start.25 = (bf16[64,256]{1,0:T(8,128)(2,1)S(1)}, bf16[64,256]{1,0:T(8,128)(2,1)S(1)}, u32[]{:S(2)}, u32[]{:S(2)}) collective-permute-start(bf16[64,256]{1,0:T(8,128)(2,1)S(1)} %get-tuple-element.70), channel_id=1, source_target_pairs={{0,16},{2,18},{4,20},{6,22},{8,24},{10,26},{12,28},{14,30},{16,0},... | collective-permute-start | bytes 98312 | tf_op jit(solution)/shard_map/ppermute | solution.py:33
  53.9 3.4 %collective-permute-done.25.refs_1_ = bf16[64,256]{1,0:T(8,128)(2,1)S(1)} collective-permute-done((bf16[64,256]{1,0:T(8,128)(2,1)S(1)}, bf16[64,256]{1,0:T(8,128)(2,1)S(1)}, u32[]{:S(2)}, u32[]{:S(2)}) %collective-permute-start.25) | collective-permute-done | bytes 32800 | tf_op jit(solution)/shard_map/ppermute | solution.py:33
  57.2 2.6 %collective-permute-start.26 = (bf16[64,256]{1,0:T(8,128)(2,1)S(1)}, bf16[64,256]{1,0:T(8,128)(2,1)S(1)}, u32[]{:S(2)}, u32[]{:S(2)}) collective-permute-start(bf16[64,256]{1,0:T(8,128)(2,1)S(1)} %get-tuple-element.71), channel_id=1, source_target_pairs={{0,24},{2,26},{4,28},{6,30},{8,16},{10,18},{12,20},{14,22},{16,8},... | collective-permute-start | bytes 98312 | tf_op jit(solution)/shard_map/ppermute | solution.py:33
  59.9 3.1 %collective-permute-done.26.refs_2_ = bf16[64,256]{1,0:T(8,128)(2,1)S(1)} collective-permute-done((bf16[64,256]{1,0:T(8,128)(2,1)S(1)}, bf16[64,256]{1,0:T(8,128)(2,1)S(1)}, u32[]{:S(2)}, u32[]{:S(2)}) %collective-permute-start.26) | collective-permute-done | bytes 32800 | tf_op jit(solution)/shard_map/ppermute | solution.py:33
  63.0 2.7 %collective-permute-start.29 = (bf16[64,256]{1,0:T(8,128)(2,1)S(1)}, bf16[64,256]{1,0:T(8,128)(2,1)S(1)}, u32[]{:S(2)}, u32[]{:S(2)}) collective-permute-start(bf16[64,256]{1,0:T(8,128)(2,1)S(1)} %kernel.27.have), channel_id=1, source_target_pairs={{0,24},{2,26},{4,28},{6,30},{8,16},{10,18},{12,20},{14,22},{16,8},... | collective-permute-start | bytes 98312 | tf_op jit(solution)/shard_map/ppermute | solution.py:33
  65.7 1.7 %collective-permute-start.27 = (bf16[64,256]{1,0:T(8,128)(2,1)S(1)}, bf16[64,256]{1,0:T(8,128)(2,1)S(1)}, u32[]{:S(2)}, u32[]{:S(2)}) collective-permute-start(bf16[64,256]{1,0:T(8,128)(2,1)S(1)} %kernel.27.have), channel_id=1, source_target_pairs={{0,8},{2,10},{4,12},{6,14},{8,0},{10,2},{12,4},{14,6},{16,24},{18,... | collective-permute-start | bytes 98312 | tf_op jit(solution)/shard_map/ppermute | solution.py:33
  67.7 6.7 %collective-permute-start.15 = (bf16[512,128]{1,0:T(8,128)(2,1)S(1)}, bf16[512,128]{1,0:T(8,128)(2,1)S(1)}, u32[]{:S(2)}, u32[]{:S(2)}) collective-permute-start(bf16[512,128]{1,0:T(8,128)(2,1)S(1)} %get-tuple-element.61), channel_id=1, source_target_pairs={{0,14},{2,16},{4,18},{6,20},{8,22},{10,24},{12,26},{14,28},{16,30}... | collective-permute-start | bytes 393224 | tf_op jit(solution)/shard_map/ppermute | solution.py:28
  74.6 3.0 %collective-permute-start.32 = (bf16[256,256]{1,0:T(8,128)(2,1)S(1)}, bf16[256,256]{1,0:T(8,128)(2,1)S(1)}, u32[]{:S(2)}, u32[]{:S(2)}) collective-permute-start(bf16[256,256]{1,0:T(8,128)(2,1)S(1)} %kernel.28.have), channel_id=1, source_target_pairs={{0,6},{2,4},{4,2},{6,0},{8,14},{10,12},{12,10},{14,8},{16,22},{18,... | collective-permute-start | bytes 393224 | tf_op jit(solution)/shard_map/ppermute | solution.py:33
  78.2 5.5 %collective-permute-start.13 = (bf16[768,128]{1,0:T(8,128)(2,1)S(1)}, bf16[768,128]{1,0:T(8,128)(2,1)S(1)}, u32[]{:S(2)}, u32[]{:S(2)}) collective-permute-start(bf16[768,128]{1,0:T(8,128)(2,1)S(1)} %get-tuple-element.59), channel_id=1, source_target_pairs={{0,30},{2,0},{4,2},{6,4},{8,6},{10,8},{12,10},{14,12},{16,14},{18,... | collective-permute-start | bytes 589832 | tf_op jit(solution)/shard_map/ppermute | solution.py:28
  84.5 4.2 %collective-permute-done.30.refs_0_ = bf16[256,256]{1,0:T(8,128)(2,1)S(1)} collective-permute-done((bf16[256,256]{1,0:T(8,128)(2,1)S(1)}, bf16[256,256]{1,0:T(8,128)(2,1)S(1)}, u32[]{:S(2)}, u32[]{:S(2)}) %collective-permute-start.30) | collective-permute-done | bytes 131104 | tf_op jit(solution)/shard_map/ppermute | solution.py:33
  89.2 5.7 %collective-permute-done.14.bm = bf16[768,128]{1,0:T(8,128)(2,1)S(1)} collective-permute-done((bf16[768,128]{1,0:T(8,128)(2,1)S(1)}, bf16[768,128]{1,0:T(8,128)(2,1)S(1)}, u32[]{:S(2)}, u32[]{:S(2)}) %collective-permute-start.14) | collective-permute-done | bytes 196640 | tf_op jit(solution)/shard_map/ppermute | solution.py:28
  95.5 0.9 collective-permute-done.34.refs_0_
  96.7 6.7 %kernel.31 = (f32[2,640,640]{2,1,0:T(8,128)S(1)}, bf16[384,384]{1,0:T(8,128)(2,1)S(1)}, bf16[2048,128]{1,0:T(8,128)(2,1)S(1)}, f32[4,2,256,256]{3,2,1,0:T(8,128)S(1)}, bf16[2,2,256,256]{3,2,1,0:T(8,128)(2,1)S(1)}) custom-call(s32[1]{0:T(128)S(6)} %copy.9.live, s32[2,4]{1,0:T(2,128)S(1)} %bitcast.31, s32[4]{0:T(128)S(1)} %copy-done.5, f32[2,8]{1,0:T(2,128)S(1)} %bitcast.34, ...), custom_call_target="tpu_custom_call" | custom-call | tf_op jit(solution)/shard_map/kernel/pallas_call | solution.py:233
  104.2 1.2 collective-permute-done.38.got
  105.9 13.2 %collective-permute-done.41.diag = bf16[512,128]{1,0:T(8,128)(2,1)S(1)} collective-permute-done((bf16[512,128]{1,0:T(8,128)(2,1)S(1)}, bf16[512,128]{1,0:T(8,128)(2,1)S(1)}, u32[]{:S(2)}, u32[]{:S(2)}) %collective-permute-start.41) | collective-permute-done | bytes 131104 | tf_op jit(solution)/shard_map/ppermute | solution.py:28
  119.5 4.2 %collective-permute-start.44 = (bf16[256,256]{1,0:T(8,128)(2,1)S(1)}, bf16[256,256]{1,0:T(8,128)(2,1)S(1)}, u32[]{:S(2)}, u32[]{:S(2)}) collective-permute-start(bf16[256,256]{1,0:T(8,128)(2,1)S(1)} %get-tuple-element.81), channel_id=1, source_target_pairs={{0,2},{2,0},{4,6},{6,4},{8,10},{10,8},{12,14},{14,12},{16,18},{18,... | collective-permute-start | bytes 393224 | tf_op jit(solution)/shard_map/ppermute | solution.py:33
  123.7 1.1 collective-permute-start.45
  125.3 2.8 %collective-permute-done.44.refs_0_ = bf16[256,256]{1,0:T(8,128)(2,1)S(1)} collective-permute-done((bf16[256,256]{1,0:T(8,128)(2,1)S(1)}, bf16[256,256]{1,0:T(8,128)(2,1)S(1)}, u32[]{:S(2)}, u32[]{:S(2)}) %collective-permute-start.44) | collective-permute-done | bytes 131104 | tf_op jit(solution)/shard_map/ppermute | solution.py:33
  128.0 4.1 %collective-permute-done.45.refs_1_ = bf16[256,256]{1,0:T(8,128)(2,1)S(1)} collective-permute-done((bf16[256,256]{1,0:T(8,128)(2,1)S(1)}, bf16[256,256]{1,0:T(8,128)(2,1)S(1)}, u32[]{:S(2)}, u32[]{:S(2)}) %collective-permute-start.45) | collective-permute-done | bytes 131104 | tf_op jit(solution)/shard_map/ppermute | solution.py:33
  132.2 3.1 %collective-permute-start.47 = (bf16[64,256]{1,0:T(8,128)(2,1)S(1)}, bf16[64,256]{1,0:T(8,128)(2,1)S(1)}, u32[]{:S(2)}, u32[]{:S(2)}) collective-permute-start(bf16[64,256]{1,0:T(8,128)(2,1)S(1)} %get-tuple-element.85), channel_id=1, source_target_pairs={{0,8},{2,10},{4,12},{6,14},{8,0},{10,2},{12,4},{14,6},{16,24},{18,... | collective-permute-start | bytes 98312 | tf_op jit(solution)/shard_map/ppermute | solution.py:33
  135.5 2.2 %collective-permute-start.49 = (bf16[64,256]{1,0:T(8,128)(2,1)S(1)}, bf16[64,256]{1,0:T(8,128)(2,1)S(1)}, u32[]{:S(2)}, u32[]{:S(2)}) collective-permute-start(bf16[64,256]{1,0:T(8,128)(2,1)S(1)} %get-tuple-element.87), channel_id=1, source_target_pairs={{0,24},{2,26},{4,28},{6,30},{8,16},{10,18},{12,20},{14,22},{16,8},... | collective-permute-start | bytes 98312 | tf_op jit(solution)/shard_map/ppermute | solution.py:33
  137.8 2.4 %collective-permute-done.48.refs_1_ = bf16[64,256]{1,0:T(8,128)(2,1)S(1)} collective-permute-done((bf16[64,256]{1,0:T(8,128)(2,1)S(1)}, bf16[64,256]{1,0:T(8,128)(2,1)S(1)}, u32[]{:S(2)}, u32[]{:S(2)}) %collective-permute-start.48) | collective-permute-done | bytes 32800 | tf_op jit(solution)/shard_map/ppermute | solution.py:33
  140.1 1.1 collective-permute-done.49.refs_2_
  141.3 2.3 %collective-permute-start.52 = (bf16[64,256]{1,0:T(8,128)(2,1)S(1)}, bf16[64,256]{1,0:T(8,128)(2,1)S(1)}, u32[]{:S(2)}, u32[]{:S(2)}) collective-permute-start(bf16[64,256]{1,0:T(8,128)(2,1)S(1)} %kernel.37.have), channel_id=1, source_target_pairs={{0,24},{2,26},{4,28},{6,30},{8,16},{10,18},{12,20},{14,22},{16,8},... | collective-permute-start | bytes 98312 | tf_op jit(solution)/shard_map/ppermute | solution.py:33
  143.6 2.1 %collective-permute-start.50 = (bf16[64,256]{1,0:T(8,128)(2,1)S(1)}, bf16[64,256]{1,0:T(8,128)(2,1)S(1)}, u32[]{:S(2)}, u32[]{:S(2)}) collective-permute-start(bf16[64,256]{1,0:T(8,128)(2,1)S(1)} %kernel.37.have), channel_id=1, source_target_pairs={{0,8},{2,10},{4,12},{6,14},{8,0},{10,2},{12,4},{14,6},{16,24},{18,... | collective-permute-start | bytes 98312 | tf_op jit(solution)/shard_map/ppermute | solution.py:33
  145.7 1.3 collective-permute-done.52.refs_2_
  147.0 1.3 collective-permute-done.51.refs_1_
  148.4 1.6 collective-permute-start.55
  149.9 1.6 %collective-permute-start.54 = (bf16[256,256]{1,0:T(8,128)(2,1)S(1)}, bf16[256,256]{1,0:T(8,128)(2,1)S(1)}, u32[]{:S(2)}, u32[]{:S(2)}) collective-permute-start(bf16[256,256]{1,0:T(8,128)(2,1)S(1)} %kernel.38.have), channel_id=1, source_target_pairs={{0,4},{2,6},{4,0},{6,2},{8,12},{10,14},{12,8},{14,10},{16,20},{18,... | collective-permute-start | bytes 393224 | tf_op jit(solution)/shard_map/ppermute | solution.py:33
  151.9 2.5 %collective-permute-done.55.refs_2_ = bf16[256,256]{1,0:T(8,128)(2,1)S(1)} collective-permute-done((bf16[256,256]{1,0:T(8,128)(2,1)S(1)}, bf16[256,256]{1,0:T(8,128)(2,1)S(1)}, u32[]{:S(2)}, u32[]{:S(2)}) %collective-permute-start.55) | collective-permute-done | bytes 131104 | tf_op jit(solution)/shard_map/ppermute | solution.py:33
  154.4 1.3 collective-permute-done.54.refs_1_
  155.7 0.8 collective-permute-done.53.refs_0_
  156.6 1.1 kernel.39
  157.6 1.1 kernel.34
  (104 shorter events, 10.4 us)
Async XLA Ops:
  0.6 26.9 %collective-permute-start = (f32[2,8]{1,0:T(2,128)}, f32[2,8]{1,0:T(2,128)S(1)}, u32[]{:S(2)}, u32[]{:S(2)}) collective-permute-start(f32[2,8]{1,0:T(2,128)} %bitcast.32), channel_id=1, source_target_pairs={{0,1},{1,0},{2,3},{3,2},{4,5},{5,4},{6,7},{7,6},{8,9},{9,8},{10,11... | collective-permute-start | bytes 200 | tf_op jit(solution)/shard_map/ppermute | solution.py:37
  1.2 26.4 %collective-permute-start.7 = (f32[2,2,256,256]{3,2,1,0:T(8,128)}, f32[2,2,256,256]{3,2,1,0:T(8,128)S(1)}, u32[]{:S(2)}, u32[]{:S(2)}) collective-permute-start(f32[2,2,256,256]{3,2,1,0:T(8,128)} %pm.1), channel_id=1, source_target_pairs={{0,1},{1,0},{2,3},{3,2},{4,5},{5,4},{6,7},{7,6},{8,9},{9,8},{10,11... | collective-permute-start | bytes 3145736 | tf_op jit(solution)/shard_map/ppermute | solution.py:37
  2.7 16.4 %collective-permute-start.3 = (bf16[512,128]{1,0:T(8,128)(2,1)S(1)}, bf16[512,128]{1,0:T(8,128)(2,1)S(1)}, u32[]{:S(2)}, u32[]{:S(2)}) collective-permute-start(bf16[512,128]{1,0:T(8,128)(2,1)S(1)} %get-tuple-element.49), channel_id=1, source_target_pairs={{0,14},{2,16},{4,18},{6,20},{8,22},{10,24},{12,26},{14,28},{16,30}... | collective-permute-start | bytes 393224 | tf_op jit(solution)/shard_map/ppermute | solution.py:28
  7.6 11.4 %collective-permute-start.1 = (bf16[768,128]{1,0:T(8,128)(2,1)S(1)}, bf16[768,128]{1,0:T(8,128)(2,1)S(1)}, u32[]{:S(2)}, u32[]{:S(2)}) collective-permute-start(bf16[768,128]{1,0:T(8,128)(2,1)S(1)} %get-tuple-element.47), channel_id=1, source_target_pairs={{0,30},{2,0},{4,2},{6,4},{8,6},{10,8},{12,10},{14,12},{16,14},{18,... | collective-permute-start | bytes 589832 | tf_op jit(solution)/shard_map/ppermute | solution.py:28
  9.9 16.0 %collective-permute-start.2 = (bf16[768,128]{1,0:T(8,128)(2,1)S(1)}, bf16[768,128]{1,0:T(8,128)(2,1)S(1)}, u32[]{:S(2)}, u32[]{:S(2)}) collective-permute-start(bf16[768,128]{1,0:T(8,128)(2,1)S(1)} %get-tuple-element.48), channel_id=1, source_target_pairs={{0,16},{2,18},{4,20},{6,22},{8,24},{10,26},{12,28},{14,30},{16,0},... | collective-permute-start | bytes 589832 | tf_op jit(solution)/shard_map/ppermute | solution.py:28
  19.0 8.5 %collective-permute-start.6 = (bf16[512,128]{1,0:T(8,128)(2,1)S(1)}, bf16[512,128]{1,0:T(8,128)(2,1)S(1)}, u32[]{:S(2)}, u32[]{:S(2)}) collective-permute-start(bf16[512,128]{1,0:T(8,128)(2,1)S(1)} %collective-permute-done.3.dm), channel_id=1, source_target_pairs={{0,1},{1,0},{2,3},{3,2},{4,5},{5,4},{6,7},{7,6},{8,9},{9,8},{10,11... | collective-permute-start | bytes 393224 | tf_op jit(solution)/shard_map/ppermute | solution.py:37
  19.0 8.5 %collective-permute-start.4 = (bf16[768,128]{1,0:T(8,128)(2,1)S(1)}, bf16[768,128]{1,0:T(8,128)(2,1)S(1)}, u32[]{:S(2)}, u32[]{:S(2)}) collective-permute-start(bf16[768,128]{1,0:T(8,128)(2,1)S(1)} %collective-permute-done.1.rm), channel_id=1, source_target_pairs={{0,1},{1,0},{2,3},{3,2},{4,5},{5,4},{6,7},{7,6},{8,9},{9,8},{10,11... | collective-permute-start | bytes 589832 | tf_op jit(solution)/shard_map/ppermute | solution.py:37
  35.0 5.3 %collective-permute-start.9 = (bf16[2048,128]{1,0:T(8,128)(2,1)S(1)}, bf16[2048,128]{1,0:T(8,128)(2,1)S(1)}, u32[]{:S(2)}, u32[]{:S(2)}) collective-permute-start(bf16[2048,128]{1,0:T(8,128)(2,1)S(1)} %get-tuple-element.53), channel_id=1, source_target_pairs={{0,1},{1,0},{2,3},{3,2},{4,5},{5,4},{6,7},{7,6},{8,9},{9,8},{10,11... | collective-permute-start | bytes 1572872 | tf_op jit(solution)/shard_map/ppermute | solution.py:37
  36.6 6.4 %collective-permute-start.21 = (bf16[256,256]{1,0:T(8,128)(2,1)S(1)}, bf16[256,256]{1,0:T(8,128)(2,1)S(1)}, u32[]{:S(2)}, u32[]{:S(2)}) collective-permute-start(bf16[256,256]{1,0:T(8,128)(2,1)S(1)} %get-tuple-element.65), channel_id=1, source_target_pairs={{0,2},{2,0},{4,6},{6,4},{8,10},{10,8},{12,14},{14,12},{16,18},{18,... | collective-permute-start | bytes 393224 | tf_op jit(solution)/shard_map/ppermute | solution.py:33
  36.7 29.0 %collective-permute-start.8 = (bf16[384,384]{1,0:T(8,128)(2,1)S(1)}, bf16[384,384]{1,0:T(8,128)(2,1)S(1)}, u32[]{:S(2)}, u32[]{:S(2)}) collective-permute-start(bf16[384,384]{1,0:T(8,128)(2,1)S(1)} %get-tuple-element.52), channel_id=1, source_target_pairs={{0,1},{1,0},{2,3},{3,2},{4,5},{5,4},{6,7},{7,6},{8,9},{9,8},{10,11... | collective-permute-start | bytes 884744 | tf_op jit(solution)/shard_map/ppermute | solution.py:37
  37.1 8.3 %collective-permute-start.22 = (bf16[256,256]{1,0:T(8,128)(2,1)S(1)}, bf16[256,256]{1,0:T(8,128)(2,1)S(1)}, u32[]{:S(2)}, u32[]{:S(2)}) collective-permute-start(bf16[256,256]{1,0:T(8,128)(2,1)S(1)} %get-tuple-element.66), channel_id=1, source_target_pairs={{0,4},{2,6},{4,0},{6,2},{8,12},{10,14},{12,8},{14,10},{16,20},{18,... | collective-permute-start | bytes 393224 | tf_op jit(solution)/shard_map/ppermute | solution.py:33
  37.1 8.4 %collective-permute-start.23 = (bf16[256,256]{1,0:T(8,128)(2,1)S(1)}, bf16[256,256]{1,0:T(8,128)(2,1)S(1)}, u32[]{:S(2)}, u32[]{:S(2)}) collective-permute-start(bf16[256,256]{1,0:T(8,128)(2,1)S(1)} %get-tuple-element.67), channel_id=1, source_target_pairs={{0,6},{2,4},{4,2},{6,0},{8,14},{10,12},{12,10},{14,8},{16,22},{18,... | collective-permute-start | bytes 393224 | tf_op jit(solution)/shard_map/ppermute | solution.py:33
  40.4 27.1 %collective-permute-start.10 = (bf16[768,128]{1,0:T(8,128)(2,1)S(1)}, bf16[768,128]{1,0:T(8,128)(2,1)S(1)}, u32[]{:S(2)}, u32[]{:S(2)}) collective-permute-start(bf16[768,128]{1,0:T(8,128)(2,1)S(1)} %get-tuple-element.54), channel_id=1, source_target_pairs={{0,2},{2,4},{4,6},{6,8},{8,10},{10,12},{12,14},{14,16},{16,18},{18... | collective-permute-start | bytes 589832 | tf_op jit(solution)/shard_map/ppermute | solution.py:28
  43.0 24.4 %collective-permute-start.11 = (bf16[768,128]{1,0:T(8,128)(2,1)S(1)}, bf16[768,128]{1,0:T(8,128)(2,1)S(1)}, u32[]{:S(2)}, u32[]{:S(2)}) collective-permute-start(bf16[768,128]{1,0:T(8,128)(2,1)S(1)} %get-tuple-element.55), channel_id=1, source_target_pairs={{0,16},{2,18},{4,20},{6,22},{8,24},{10,26},{12,28},{14,30},{16,0},... | collective-permute-start | bytes 589832 | tf_op jit(solution)/shard_map/ppermute | solution.py:28
  45.5 20.2 %collective-permute-start.12 = (bf16[512,128]{1,0:T(8,128)(2,1)S(1)}, bf16[512,128]{1,0:T(8,128)(2,1)S(1)}, u32[]{:S(2)}, u32[]{:S(2)}) collective-permute-start(bf16[512,128]{1,0:T(8,128)(2,1)S(1)} %get-tuple-element.56), channel_id=1, source_target_pairs={{0,18},{2,20},{4,22},{6,24},{8,26},{10,28},{12,30},{14,0},{16,2},{... | collective-permute-start | bytes 393224 | tf_op jit(solution)/shard_map/ppermute | solution.py:28
  45.6 5.4 %collective-permute-start.24 = (bf16[64,256]{1,0:T(8,128)(2,1)S(1)}, bf16[64,256]{1,0:T(8,128)(2,1)S(1)}, u32[]{:S(2)}, u32[]{:S(2)}) collective-permute-start(bf16[64,256]{1,0:T(8,128)(2,1)S(1)} %get-tuple-element.69), channel_id=1, source_target_pairs={{0,8},{2,10},{4,12},{6,14},{8,0},{10,2},{12,4},{14,6},{16,24},{18,... | collective-permute-start | bytes 98312 | tf_op jit(solution)/shard_map/ppermute | solution.py:33
  51.0 6.2 %collective-permute-start.25 = (bf16[64,256]{1,0:T(8,128)(2,1)S(1)}, bf16[64,256]{1,0:T(8,128)(2,1)S(1)}, u32[]{:S(2)}, u32[]{:S(2)}) collective-permute-start(bf16[64,256]{1,0:T(8,128)(2,1)S(1)} %get-tuple-element.70), channel_id=1, source_target_pairs={{0,16},{2,18},{4,20},{6,22},{8,24},{10,26},{12,28},{14,30},{16,0},... | collective-permute-start | bytes 98312 | tf_op jit(solution)/shard_map/ppermute | solution.py:33
  57.2 5.7 %collective-permute-start.26 = (bf16[64,256]{1,0:T(8,128)(2,1)S(1)}, bf16[64,256]{1,0:T(8,128)(2,1)S(1)}, u32[]{:S(2)}, u32[]{:S(2)}) collective-permute-start(bf16[64,256]{1,0:T(8,128)(2,1)S(1)} %get-tuple-element.71), channel_id=1, source_target_pairs={{0,24},{2,26},{4,28},{6,30},{8,16},{10,18},{12,20},{14,22},{16,8},... | collective-permute-start | bytes 98312 | tf_op jit(solution)/shard_map/ppermute | solution.py:33
  63.0 11.5 %collective-permute-start.29 = (bf16[64,256]{1,0:T(8,128)(2,1)S(1)}, bf16[64,256]{1,0:T(8,128)(2,1)S(1)}, u32[]{:S(2)}, u32[]{:S(2)}) collective-permute-start(bf16[64,256]{1,0:T(8,128)(2,1)S(1)} %kernel.27.have), channel_id=1, source_target_pairs={{0,24},{2,26},{4,28},{6,30},{8,16},{10,18},{12,20},{14,22},{16,8},... | collective-permute-start | bytes 98312 | tf_op jit(solution)/shard_map/ppermute | solution.py:33
  65.7 8.8 %collective-permute-start.28 = (bf16[64,256]{1,0:T(8,128)(2,1)S(1)}, bf16[64,256]{1,0:T(8,128)(2,1)S(1)}, u32[]{:S(2)}, u32[]{:S(2)}) collective-permute-start(bf16[64,256]{1,0:T(8,128)(2,1)S(1)} %kernel.27.have), channel_id=1, source_target_pairs={{0,16},{2,18},{4,20},{6,22},{8,24},{10,26},{12,28},{14,30},{16,0},... | collective-permute-start | bytes 98312 | tf_op jit(solution)/shard_map/ppermute | solution.py:33
  65.7 8.8 %collective-permute-start.27 = (bf16[64,256]{1,0:T(8,128)(2,1)S(1)}, bf16[64,256]{1,0:T(8,128)(2,1)S(1)}, u32[]{:S(2)}, u32[]{:S(2)}) collective-permute-start(bf16[64,256]{1,0:T(8,128)(2,1)S(1)} %kernel.27.have), channel_id=1, source_target_pairs={{0,8},{2,10},{4,12},{6,14},{8,0},{10,2},{12,4},{14,6},{16,24},{18,... | collective-permute-start | bytes 98312 | tf_op jit(solution)/shard_map/ppermute | solution.py:33
  67.7 10.5 %collective-permute-start.15 = (bf16[512,128]{1,0:T(8,128)(2,1)S(1)}, bf16[512,128]{1,0:T(8,128)(2,1)S(1)}, u32[]{:S(2)}, u32[]{:S(2)}) collective-permute-start(bf16[512,128]{1,0:T(8,128)(2,1)S(1)} %get-tuple-element.61), channel_id=1, source_target_pairs={{0,14},{2,16},{4,18},{6,20},{8,22},{10,24},{12,26},{14,28},{16,30}... | collective-permute-start | bytes 393224 | tf_op jit(solution)/shard_map/ppermute | solution.py:28
  74.5 9.2 %collective-permute-start.33 = (bf16[256,256]{1,0:T(8,128)(2,1)S(1)}, bf16[256,256]{1,0:T(8,128)(2,1)S(1)}, u32[]{:S(2)}, u32[]{:S(2)}) collective-permute-start(bf16[256,256]{1,0:T(8,128)(2,1)S(1)} %kernel.28.have), channel_id=1, source_target_pairs={{0,1},{1,0},{2,3},{3,2},{4,5},{5,4},{6,7},{7,6},{8,9},{9,8},{10,11... | collective-permute-start | bytes 393224 | tf_op jit(solution)/shard_map/ppermute | solution.py:37
  74.6 9.1 %collective-permute-start.32 = (bf16[256,256]{1,0:T(8,128)(2,1)S(1)}, bf16[256,256]{1,0:T(8,128)(2,1)S(1)}, u32[]{:S(2)}, u32[]{:S(2)}) collective-permute-start(bf16[256,256]{1,0:T(8,128)(2,1)S(1)} %kernel.28.have), channel_id=1, source_target_pairs={{0,6},{2,4},{4,2},{6,0},{8,14},{10,12},{12,10},{14,8},{16,22},{18,... | collective-permute-start | bytes 393224 | tf_op jit(solution)/shard_map/ppermute | solution.py:33
  77.6 6.9 %collective-permute-start.31 = (bf16[256,256]{1,0:T(8,128)(2,1)S(1)}, bf16[256,256]{1,0:T(8,128)(2,1)S(1)}, u32[]{:S(2)}, u32[]{:S(2)}) collective-permute-start(bf16[256,256]{1,0:T(8,128)(2,1)S(1)} %kernel.28.have), channel_id=1, source_target_pairs={{0,4},{2,6},{4,0},{6,2},{8,12},{10,14},{12,8},{14,10},{16,20},{18,... | collective-permute-start | bytes 393224 | tf_op jit(solution)/shard_map/ppermute | solution.py:33
  77.6 11.1 %collective-permute-start.30 = (bf16[256,256]{1,0:T(8,128)(2,1)S(1)}, bf16[256,256]{1,0:T(8,128)(2,1)S(1)}, u32[]{:S(2)}, u32[]{:S(2)}) collective-permute-start(bf16[256,256]{1,0:T(8,128)(2,1)S(1)} %kernel.28.have), channel_id=1, source_target_pairs={{0,2},{2,0},{4,6},{6,4},{8,10},{10,8},{12,14},{14,12},{16,18},{18,... | collective-permute-start | bytes 393224 | tf_op jit(solution)/shard_map/ppermute | solution.py:33
  78.2 10.5 %collective-permute-start.13 = (bf16[768,128]{1,0:T(8,128)(2,1)S(1)}, bf16[768,128]{1,0:T(8,128)(2,1)S(1)}, u32[]{:S(2)}, u32[]{:S(2)}) collective-permute-start(bf16[768,128]{1,0:T(8,128)(2,1)S(1)} %get-tuple-element.59), channel_id=1, source_target_pairs={{0,30},{2,0},{4,2},{6,4},{8,6},{10,8},{12,10},{14,12},{16,14},{18,... | collective-permute-start | bytes 589832 | tf_op jit(solution)/shard_map/ppermute | solution.py:28
  83.7 11.1 %collective-permute-start.14 = (bf16[768,128]{1,0:T(8,128)(2,1)S(1)}, bf16[768,128]{1,0:T(8,128)(2,1)S(1)}, u32[]{:S(2)}, u32[]{:S(2)}) collective-permute-start(bf16[768,128]{1,0:T(8,128)(2,1)S(1)} %get-tuple-element.60), channel_id=1, source_target_pairs={{0,16},{2,18},{4,20},{6,22},{8,24},{10,26},{12,28},{14,30},{16,0},... | collective-permute-start | bytes 589832 | tf_op jit(solution)/shard_map/ppermute | solution.py:28
  83.7 13.0 %collective-permute-start.16 = (bf16[384,384]{1,0:T(8,128)(2,1)S(1)}, bf16[384,384]{1,0:T(8,128)(2,1)S(1)}, u32[]{:S(2)}, u32[]{:S(2)}) collective-permute-start(bf16[384,384]{1,0:T(8,128)(2,1)S(1)} %get-tuple-element.58.tm), channel_id=1, source_target_pairs={{0,1},{1,0},{2,3},{3,2},{4,5},{5,4},{6,7},{7,6},{8,9},{9,8},{10,11... | collective-permute-start | bytes 884744 | tf_op jit(solution)/shard_map/ppermute | solution.py:37
  84.5 10.4 %collective-permute-start.36 = (bf16[256,256]{1,0:T(8,128)(2,1)S(1)}, bf16[256,256]{1,0:T(8,128)(2,1)S(1)}, u32[]{:S(2)}, u32[]{:S(2)}) collective-permute-start(bf16[256,256]{1,0:T(8,128)(2,1)S(1)} %collective-permute-done.32.refs_2_), channel_id=1, source_target_pairs={{0,1},{1,0},{2,3},{3,2},{4,5},{5,4},{6,7},{7,6},{8,9},{9,8},{10,11... | collective-permute-start | bytes 393224 | tf_op jit(solution)/shard_map/ppermute | solution.py:37
  88.7 6.7 %collective-permute-start.35 = (bf16[256,256]{1,0:T(8,128)(2,1)S(1)}, bf16[256,256]{1,0:T(8,128)(2,1)S(1)}, u32[]{:S(2)}, u32[]{:S(2)}) collective-permute-start(bf16[256,256]{1,0:T(8,128)(2,1)S(1)} %collective-permute-done.31.refs_1_), channel_id=1, source_target_pairs={{0,1},{1,0},{2,3},{3,2},{4,5},{5,4},{6,7},{7,6},{8,9},{9,8},{10,11... | collective-permute-start | bytes 393224 | tf_op jit(solution)/shard_map/ppermute | solution.py:37
  88.7 8.0 %collective-permute-start.17 = (bf16[768,128]{1,0:T(8,128)(2,1)S(1)}, bf16[768,128]{1,0:T(8,128)(2,1)S(1)}, u32[]{:S(2)}, u32[]{:S(2)}) collective-permute-start(bf16[768,128]{1,0:T(8,128)(2,1)S(1)} %collective-permute-done.13.rm), channel_id=1, source_target_pairs={{0,1},{1,0},{2,3},{3,2},{4,5},{5,4},{6,7},{7,6},{8,9},{9,8},{10,11... | collective-permute-start | bytes 589832 | tf_op jit(solution)/shard_map/ppermute | solution.py:37
  104.1 15.4 %collective-permute-start.43 = (bf16[2,2,256,256]{3,2,1,0:T(8,128)(2,1)S(1)}, bf16[2,2,256,256]{3,2,1,0:T(8,128)(2,1)S(1)}, u32[]{:S(2)}, u32[]{:S(2)}) collective-permute-start(bf16[2,2,256,256]{3,2,1,0:T(8,128)(2,1)S(1)} %get-tuple-element.79), channel_id=1, source_target_pairs={{0,1},{1,0},{2,3},{3,2},{4,5},{5,4},{6,7},{7,6},{8,9},{9,8},{10,11... | collective-permute-start | bytes 1572872 | tf_op jit(solution)/shard_map/ppermute | solution.py:37
  105.5 13.6 %collective-permute-start.39 = (bf16[768,128]{1,0:T(8,128)(2,1)S(1)}, bf16[768,128]{1,0:T(8,128)(2,1)S(1)}, u32[]{:S(2)}, u32[]{:S(2)}) collective-permute-start(bf16[768,128]{1,0:T(8,128)(2,1)S(1)} %get-tuple-element.75), channel_id=1, source_target_pairs={{0,2},{2,4},{4,6},{6,8},{8,10},{10,12},{12,14},{14,16},{16,18},{18... | collective-permute-start | bytes 589832 | tf_op jit(solution)/shard_map/ppermute | solution.py:28
  105.6 13.5 %collective-permute-start.40 = (bf16[768,128]{1,0:T(8,128)(2,1)S(1)}, bf16[768,128]{1,0:T(8,128)(2,1)S(1)}, u32[]{:S(2)}, u32[]{:S(2)}) collective-permute-start(bf16[768,128]{1,0:T(8,128)(2,1)S(1)} %get-tuple-element.76), channel_id=1, source_target_pairs={{0,16},{2,18},{4,20},{6,22},{8,24},{10,26},{12,28},{14,30},{16,0},... | collective-permute-start | bytes 589832 | tf_op jit(solution)/shard_map/ppermute | solution.py:28
  105.7 13.4 %collective-permute-start.41 = (bf16[512,128]{1,0:T(8,128)(2,1)S(1)}, bf16[512,128]{1,0:T(8,128)(2,1)S(1)}, u32[]{:S(2)}, u32[]{:S(2)}) collective-permute-start(bf16[512,128]{1,0:T(8,128)(2,1)S(1)} %get-tuple-element.77), channel_id=1, source_target_pairs={{0,18},{2,20},{4,22},{6,24},{8,26},{10,28},{12,30},{14,0},{16,2},{... | collective-permute-start | bytes 393224 | tf_op jit(solution)/shard_map/ppermute | solution.py:28
  119.3 38.3 %collective-permute-start.42 = (f32[384,384]{1,0:T(8,128)S(1)}, f32[384,384]{1,0:T(8,128)S(1)}, u32[]{:S(2)}, u32[]{:S(2)}) collective-permute-start(f32[384,384]{1,0:T(8,128)S(1)} %kernel.33.state), channel_id=1, source_target_pairs={{0,1},{1,0},{2,3},{3,2},{4,5},{5,4},{6,7},{7,6},{8,9},{9,8},{10,11... | collective-permute-start | bytes 1769480 | tf_op jit(solution)/shard_map/ppermute | solution.py:37
  119.5 8.5 %collective-permute-start.44 = (bf16[256,256]{1,0:T(8,128)(2,1)S(1)}, bf16[256,256]{1,0:T(8,128)(2,1)S(1)}, u32[]{:S(2)}, u32[]{:S(2)}) collective-permute-start(bf16[256,256]{1,0:T(8,128)(2,1)S(1)} %get-tuple-element.81), channel_id=1, source_target_pairs={{0,2},{2,0},{4,6},{6,4},{8,10},{10,8},{12,14},{14,12},{16,18},{18,... | collective-permute-start | bytes 393224 | tf_op jit(solution)/shard_map/ppermute | solution.py:33
  123.7 8.4 %collective-permute-start.45 = (bf16[256,256]{1,0:T(8,128)(2,1)S(1)}, bf16[256,256]{1,0:T(8,128)(2,1)S(1)}, u32[]{:S(2)}, u32[]{:S(2)}) collective-permute-start(bf16[256,256]{1,0:T(8,128)(2,1)S(1)} %get-tuple-element.82), channel_id=1, source_target_pairs={{0,4},{2,6},{4,0},{6,2},{8,12},{10,14},{12,8},{14,10},{16,20},{18,... | collective-permute-start | bytes 393224 | tf_op jit(solution)/shard_map/ppermute | solution.py:33
  124.8 7.3 %collective-permute-start.46 = (bf16[256,256]{1,0:T(8,128)(2,1)S(1)}, bf16[256,256]{1,0:T(8,128)(2,1)S(1)}, u32[]{:S(2)}, u32[]{:S(2)}) collective-permute-start(bf16[256,256]{1,0:T(8,128)(2,1)S(1)} %get-tuple-element.83), channel_id=1, source_target_pairs={{0,6},{2,4},{4,2},{6,0},{8,14},{10,12},{12,10},{14,8},{16,22},{18,... | collective-permute-start | bytes 393224 | tf_op jit(solution)/shard_map/ppermute | solution.py:33
  132.2 5.5 %collective-permute-start.47 = (bf16[64,256]{1,0:T(8,128)(2,1)S(1)}, bf16[64,256]{1,0:T(8,128)(2,1)S(1)}, u32[]{:S(2)}, u32[]{:S(2)}) collective-permute-start(bf16[64,256]{1,0:T(8,128)(2,1)S(1)} %get-tuple-element.85), channel_id=1, source_target_pairs={{0,8},{2,10},{4,12},{6,14},{8,0},{10,2},{12,4},{14,6},{16,24},{18,... | collective-permute-start | bytes 98312 | tf_op jit(solution)/shard_map/ppermute | solution.py:33
  135.3 4.8 %collective-permute-start.48 = (bf16[64,256]{1,0:T(8,128)(2,1)S(1)}, bf16[64,256]{1,0:T(8,128)(2,1)S(1)}, u32[]{:S(2)}, u32[]{:S(2)}) collective-permute-start(bf16[64,256]{1,0:T(8,128)(2,1)S(1)} %get-tuple-element.86), channel_id=1, source_target_pairs={{0,16},{2,18},{4,20},{6,22},{8,24},{10,26},{12,28},{14,30},{16,0},... | collective-permute-start | bytes 98312 | tf_op jit(solution)/shard_map/ppermute | solution.py:33
  135.5 5.7 %collective-permute-start.49 = (bf16[64,256]{1,0:T(8,128)(2,1)S(1)}, bf16[64,256]{1,0:T(8,128)(2,1)S(1)}, u32[]{:S(2)}, u32[]{:S(2)}) collective-permute-start(bf16[64,256]{1,0:T(8,128)(2,1)S(1)} %get-tuple-element.87), channel_id=1, source_target_pairs={{0,24},{2,26},{4,28},{6,30},{8,16},{10,18},{12,20},{14,22},{16,8},... | collective-permute-start | bytes 98312 | tf_op jit(solution)/shard_map/ppermute | solution.py:33
  141.3 5.8 %collective-permute-start.52 = (bf16[64,256]{1,0:T(8,128)(2,1)S(1)}, bf16[64,256]{1,0:T(8,128)(2,1)S(1)}, u32[]{:S(2)}, u32[]{:S(2)}) collective-permute-start(bf16[64,256]{1,0:T(8,128)(2,1)S(1)} %kernel.37.have), channel_id=1, source_target_pairs={{0,24},{2,26},{4,28},{6,30},{8,16},{10,18},{12,20},{14,22},{16,8},... | collective-permute-start | bytes 98312 | tf_op jit(solution)/shard_map/ppermute | solution.py:33
  143.6 4.8 %collective-permute-start.51 = (bf16[64,256]{1,0:T(8,128)(2,1)S(1)}, bf16[64,256]{1,0:T(8,128)(2,1)S(1)}, u32[]{:S(2)}, u32[]{:S(2)}) collective-permute-start(bf16[64,256]{1,0:T(8,128)(2,1)S(1)} %kernel.37.have), channel_id=1, source_target_pairs={{0,16},{2,18},{4,20},{6,22},{8,24},{10,26},{12,28},{14,30},{16,0},... | collective-permute-start | bytes 98312 | tf_op jit(solution)/shard_map/ppermute | solution.py:33
  148.4 6.0 %collective-permute-start.55 = (bf16[256,256]{1,0:T(8,128)(2,1)S(1)}, bf16[256,256]{1,0:T(8,128)(2,1)S(1)}, u32[]{:S(2)}, u32[]{:S(2)}) collective-permute-start(bf16[256,256]{1,0:T(8,128)(2,1)S(1)} %kernel.38.have), channel_id=1, source_target_pairs={{0,6},{2,4},{4,2},{6,0},{8,14},{10,12},{12,10},{14,8},{16,22},{18,... | collective-permute-start | bytes 393224 | tf_op jit(solution)/shard_map/ppermute | solution.py:33
  149.9 5.8 %collective-permute-start.54 = (bf16[256,256]{1,0:T(8,128)(2,1)S(1)}, bf16[256,256]{1,0:T(8,128)(2,1)S(1)}, u32[]{:S(2)}, u32[]{:S(2)}) collective-permute-start(bf16[256,256]{1,0:T(8,128)(2,1)S(1)} %kernel.38.have), channel_id=1, source_target_pairs={{0,4},{2,6},{4,0},{6,2},{8,12},{10,14},{12,8},{14,10},{16,20},{18,... | collective-permute-start | bytes 393224 | tf_op jit(solution)/shard_map/ppermute | solution.py:33
  151.6 5.0 %collective-permute-start.53 = (bf16[256,256]{1,0:T(8,128)(2,1)S(1)}, bf16[256,256]{1,0:T(8,128)(2,1)S(1)}, u32[]{:S(2)}, u32[]{:S(2)}) collective-permute-start(bf16[256,256]{1,0:T(8,128)(2,1)S(1)} %kernel.38.have), channel_id=1, source_target_pairs={{0,2},{2,0},{4,6},{6,4},{8,10},{10,8},{12,14},{14,12},{16,18},{18,... | collective-permute-start | bytes 393224 | tf_op jit(solution)/shard_map/ppermute | solution.py:33
  (14 other events, 102.2 us)
